TPU v7x, 32 devices: a whole 2x2x4 slice. The times are simulated.
32 devices in a mesh: line: 8 (over y, x, core), surf: 4 (over z).
Axes of the slice: x: 2, y: 2, z: 4, core: 2. Of those that a mesh axis runs over, the one named last changes fastest.
Arguments:
- right_side: float32 [8, 64, 135], P('surf', 'line'), may hold values from -6 to 6
- previous: float32 [8, 64, 135], P('surf', 'line'), may hold values from -6 to 6
- coupling: float32 [8, 64, 4, 135], P('surf', 'line'), may hold values from 0.1 to 0.4
- neighbours: int32 [8, 4], P('surf'), may hold values from 0 to 7, as said below
- pivots: bfloat16 [8, 64, 135, 135], P('surf', 'line'), may hold values from -0.0625 to 0.0625
- lower_factor: bfloat16 [8, 64, 135, 135], P('surf', 'line')
- upper_factor: bfloat16 [8, 64, 135, 135], P('surf', 'line')
Outputs:
- correction: float32 [8, 64, 135], P('surf', 'line')
Inputs may be any that keep to these rules, and one draw needn't show every extreme that they name: `neighbours`: lines of surface patch q are q * 2 to (q + 1) * 2 - 1. Face 0 of a line in patch q names a line of patch q - 1 and face 1 one of patch q + 1 (patches wrap around); faces 2 and 3 name lines of its own patch.
All inputs are finite; a program needn't handle non-finite values.
Results may differ from a plain program's by a relative error of at most 0.0003.
Values sent between devices are 32-bit elements; how exact they have to be, the bound alone decides.
No kernel may reach another device: no remote copies, remote signals or barrier semaphores. Data moves between devices by JAX's collectives and lax.ppermute only.
A program may use at most 64 MiB of HBM per device.

v0:
```python
import jax
import jax.numpy as jnp
from jax import lax
from jax.sharding import PartitionSpec as P


def padded(array, sides, width):
    for axis, dim in sides:
        size, length = (lax.axis_size(axis), array.shape[dim])
        up = [(i, (i + 1) % size) for i in range(size)]
        down = [(j, i) for i, j in up]
        last = lax.slice_in_dim(array, length - width, length, axis=dim)
        leading = lax.slice_in_dim(array, 0, width, axis=dim)
        before = lax.ppermute(last, axis, up)
        after = lax.ppermute(leading, axis, down)
        array = jnp.concatenate([before, array, after], axis=dim)
    return array


def entering(part, axis, combine, identity, reverse):
    count = lax.axis_size(axis)
    place = lax.axis_index(axis)
    ahead = count - 1 - place if reverse else place
    gathered = jax.tree.map(lambda a: lax.all_gather(a, axis), part)
    state = jax.tree.map(lambda a, e: jnp.zeros_like(a) + jnp.asarray(e, a.dtype), part, identity)

    def one(step, state):
        source = count - 1 - step if reverse else step
        return combine(
            state, jax.tree.map(lambda a: lax.dynamic_index_in_dim(a, source, 0, False), gathered)
        )

    return lax.fori_loop(0, ahead, one, state)


def pick_block(blocks, element):
    return lax.dynamic_index_in_dim(blocks, element, 1, keepdims=False).astype(jnp.float32)


def apply_block(matrix, vector):
    return jnp.einsum("lab,lb->la", matrix, vector, precision=lax.Precision.HIGHEST)


def times_block(matrix, other):
    return jnp.einsum("lab,lbc->lac", matrix, other, precision=lax.Precision.HIGHEST)


def pivot_terms(source, pivots):

    def pivot_visit(element):
        return apply_block(
            pick_block(pivots, element),
            lax.dynamic_index_in_dim(source, element, 1, keepdims=False),
        )

    return lax.map(pivot_visit, jnp.arange(source.shape[1], dtype=jnp.int32))


def forward_sweep(driven, lower_factor, inflow):

    def forward_visit(carried, element):
        result = driven[element] + apply_block(pick_block(lower_factor, element), carried)
        return (result, result)

    return lax.scan(forward_visit, inflow, jnp.arange(driven.shape[0], dtype=jnp.int32))


def backward_sweep(values, upper_factor, inflow):

    def backward_visit(carried, element):
        result = values[element] + apply_block(pick_block(upper_factor, element), carried)
        return (result, result)

    return lax.scan(
        backward_visit, inflow, jnp.arange(values.shape[0], dtype=jnp.int32), reverse=True
    )


def chain_product(blocks, identity, reverse_passes):

    def chain_visit(carried, element):
        return (times_block(pick_block(blocks, element), carried), None)

    result, _ = lax.scan(
        chain_visit, identity, jnp.arange(blocks.shape[1], dtype=jnp.int32), reverse=reverse_passes
    )
    return result


def compose(earlier, later):
    return (times_block(later[0], earlier[0]), apply_block(later[0], earlier[1]) + later[1])


def shards(right_side, previous, coupling, neighbours, pivots, lower_factor, upper_factor):
    rows, depth, width = right_side.shape
    patches = lax.axis_size("surf")
    here = lax.axis_index("surf")
    widened = padded(previous, (("surf", 0),), rows)
    relative = (neighbours // rows - here + 1 + patches) % patches
    located = relative * rows + neighbours % rows
    selector = (located[:, :, None] == jnp.arange(3 * rows, dtype=jnp.int32)[None, None, :]).astype(
        jnp.float32
    )
    picked = jnp.einsum("lfm,meb->lefb", selector, widened, precision=lax.Precision.HIGHEST)
    source = right_side - jnp.sum(coupling * picked, axis=2)
    driven = pivot_terms(source, pivots)
    empty = jnp.zeros((rows, width), jnp.float32)
    identity = jnp.broadcast_to(jnp.eye(width, dtype=jnp.float32), (rows, width, width))
    forward_map = chain_product(lower_factor, identity, False)
    backward_map = chain_product(upper_factor, identity, True)
    forward_end, _ = forward_sweep(driven, lower_factor, empty)
    forward_prefix = entering((forward_map, forward_end), "line", compose, (identity, empty), False)
    forward_in = forward_prefix[1]
    _, values = forward_sweep(driven, lower_factor, forward_in)
    backward_head, _ = backward_sweep(values, upper_factor, empty)
    backward_prefix = entering(
        (backward_map, backward_head), "line", compose, (identity, empty), True
    )
    backward_in = backward_prefix[1]
    _, solved = backward_sweep(values, upper_factor, backward_in)
    return jnp.transpose(solved, (1, 0, 2))


def solution(mesh):
    return jax.shard_map(
        shards,
        mesh=mesh,
        in_specs=(
            P("surf", "line", None),
            P("surf", "line", None),
            P("surf", "line", None, None),
            P("surf", None),
            P("surf", "line", None, None),
            P("surf", "line", None, None),
            P("surf", "line", None, None),
        ),
        out_specs=P("surf", "line", None),
        check_vma=False,
    )
```

profile of v0, /device:TPU:0, one launch (start us, length us, event | category | flops | bytes accessed | tf_op | source)
XLA Modules:
  0.0 220.2 jit_solution(1876632386415605589)
XLA Ops:
  6.6 1.5 copy.28
  8.1 23.0 %while.115 = (s32[]{:T(128)}, f32[2,135,135]{2,1,0:T(8,128)S(1)}, s32[8]{0:T(128)S(1)}, bf16[2,8,135,135]{3,2,0,1:T(8,128)(2,1)S(1)}, s32[]{:T(128)}, /*index=5*/s32[]{:T(128)}, s32[]{:T(128)}) while((s32[]{:T(128)}, f32[2,135,135]{2,1,0:T(8,128)S(1)}, s32[8]{0:T(128)S(1)}, bf16[2,8,135,135]{3,2,0,1:T(8,128)(2,1)S(1)}, s32[]{:T(128)}, ...), condition=%wide.region_3.4_spmd, body=%wide.region_2.3_spmd.sunk | while | flops 59049004 | bytes 855319 | solution.py:84
  8.1 0.7 dynamic_slice.209
  31.1 0.7 copy-done.1
  31.9 3.1 %collective-permute-start = (f32[2,8,135]{2,0,1:T(2,128)S(1)}, f32[2,8,135]{2,0,1:T(2,128)S(1)}, u32[]{:S(2)}, u32[]{:S(2)}) collective-permute-start(f32[2,8,135]{2,0,1:T(2,128)S(1)} %copy.29), channel_id=1, source_target_pairs={{0,1},{1,2},{2,3},{3,0},{4,5},{5,6},{6,7},{7,4},{8,9},{9,10},{10,1... | collective-permute-start | bytes 25928 | tf_op jit(solution)/shard_map/ppermute | solution.py:14
  35.0 2.1 collective-permute-start.1
  37.3 24.4 %while.114 = (s32[]{:T(128)}, f32[2,135,135]{2,1,0:T(8,128)S(1)}, s32[8]{0:T(128)S(1)}, bf16[2,8,135,135]{3,2,0,1:T(8,128)(2,1)S(1)}, s32[]{:T(128)}, /*index=5*/s32[]{:T(128)}, s32[]{:T(128)}, s32[]{:T(128)}) while((s32[]{:T(128)}, f32[2,135,135]{2,1,0:T(8,128)S(1)}, s32[8]{0:T(128)S(1)}, bf16[2,8,135,135]{3,2,0,1:T(8,128)(2,1)S(1)}, ...), condition=%wide.region_1.2_spmd, body=%wide.region_0.1_spmd.sunk | while | flops 59049004 | bytes 855339 | solution.py:84
  37.4 0.7 dynamic_slice.207
  40.4 0.7 dynamic_slice.207
  43.5 0.7 dynamic_slice.207
  46.5 0.7 dynamic_slice.207
  49.6 0.7 dynamic_slice.207
  52.6 0.7 dynamic_slice.207
  55.7 0.7 dynamic_slice.207
  58.7 0.7 dynamic_slice.207
  61.8 0.7 copy-done
  62.6 1.5 copy.34
  64.5 21.8 %while.116 = (s32[]{:T(128)}, f32[8,2,135]{2,1,0:T(2,128)S(1)}, s32[8]{0:T(128)S(1)}, bf16[2,8,135,135]{3,2,0,1:T(8,128)(2,1)S(1)}, f32[2,8,135]{2,0,1:T(2,128)S(1)}, /*index=5*/s32[]{:T(128)}, s32[]{:T(128)}, s32[]{:T(128)}) while((s32[]{:T(128)}, f32[8,2,135]{2,1,0:T(2,128)S(1)}, s32[8]{0:T(128)S(1)}, ...), condition=%wide.region_6.7_spmd, body=%wide.region_5.6_spmd.sunk | while | flops 437405 | bytes 148791 | solution.py:56
  86.3 23.5 %while.121 = (s32[]{:T(128)}, f32[2,135]{1,0:T(2,128)S(1)}, s32[8]{0:T(128)S(1)}, f32[8,2,135]{2,1,0:T(2,128)S(1)}, bf16[2,8,135,135]{3,2,0,1:T(8,128)(2,1)S(1)}, /*index=5*/s32[]{:T(128)}, s32[]{:T(128)}, s32[]{:T(128)}) while((s32[]{:T(128)}, f32[2,135]{1,0:T(2,128)S(1)}, s32[8]{0:T(128)S(1)}, f32[8,2,135]{2,1,0:T(2,128)S(1)}, ...), condition=%wide.region_8.9_spmd.clone, body=%wide.region_7.8_spmd.clone.sunk | while | flops 437946 | bytes 147941 | solution.py:65
  86.3 0.7 dynamic_slice.224
  89.3 0.7 dynamic_slice.224
  92.2 0.7 dynamic_slice.224
  95.2 0.7 dynamic_slice.224
  98.1 0.7 dynamic_slice.224
  101.0 0.7 dynamic_slice.224
  104.0 0.7 dynamic_slice.224
  106.9 0.7 dynamic_slice.224
  109.8 9.1 %all-gather.4 = f32[8,2,135]{2,1,0:T(2,128)S(1)} all-gather(f32[1,2,135]{2,1,0:T(2,128)S(1)} %bitcast.182), channel_id=4, replica_groups=mesh['line'=8,'surf'=4] {'line'}, dimensions={0}, use_global_device_ids=true | all-gather | bytes 9720 | tf_op jit(solution)/shard_map/all_gather | solution.py:24
  118.9 22.4 %while.118 = (s32[]{:T(128)}, f32[2,135]{1,0:T(2,128)S(1)}, f32[8,2,135]{2,1,0:T(2,128)S(1)}, s32[8]{0:T(128)S(1)}, f32[8,2,135]{2,1,0:T(2,128)S(1)}, /*index=5*...) while((s32[]{:T(128)}, f32[2,135]{1,0:T(2,128)S(1)}, f32[8,2,135]{2,1,0:T(2,128)S(1)}, ...), condition=%wide.region_12.13_spmd, body=%wide.region_11.12_spmd.sunk | while | flops 437675 | bytes 150735 | solution.py:65
  119.0 0.7 dynamic_slice.216
  121.7 0.7 dynamic_slice.216
  124.5 0.7 dynamic_slice.216
  127.4 0.7 dynamic_slice.216
  130.2 0.7 dynamic_slice.216
  133.0 0.7 dynamic_slice.216
  135.8 0.7 dynamic_slice.216
  138.6 0.7 dynamic_slice.216
  141.4 22.5 %while.122 = (s32[]{:T(128)}, f32[2,135]{1,0:T(2,128)S(1)}, s32[8]{0:T(128)S(1)}, f32[8,2,135]{2,1,0:T(2,128)S(1)}, bf16[2,8,135,135]{3,2,0,1:T(8,128)(2,1)S(1)}...) while((s32[]{:T(128)}, f32[2,135]{1,0:T(2,128)S(1)}, s32[8]{0:T(128)S(1)}, ...), condition=%wide.region_14.15_spmd.clone, body=%wide.region_13.14_spmd.clone.sunk | while | flops 437947 | bytes 147961 | solution.py:74
  141.4 0.7 dynamic_slice.227
  144.2 0.7 dynamic_slice.227
  147.0 0.7 dynamic_slice.227
  149.8 0.7 dynamic_slice.227
  152.6 0.7 dynamic_slice.227
  155.5 0.7 dynamic_slice.227
  158.3 0.7 dynamic_slice.227
  161.1 0.7 dynamic_slice.227
  163.9 17.0 %all-gather.5 = f32[8,2,135]{2,1,0:T(2,128)S(1)} all-gather(f32[1,2,135]{2,1,0:T(2,128)S(1)} %bitcast.181), channel_id=5, replica_groups=mesh['line'=8,'surf'=4] {'line'}, dimensions={0}, use_global_device_ids=true | all-gather | bytes 9720 | tf_op jit(solution)/shard_map/all_gather | solution.py:24
  180.9 9.2 %while.119 = (s32[]{:T(128)}, f32[2,135]{1,0:T(2,128)S(1)}, s32[]{:T(128)}, f32[8,2,135,135]{3,2,1,0:T(8,128)}, f32[8,2,135]{2,1,0:T(2,128)S(1)}, /*index=5*/s32[]{:T(128)}, s32[]{:T(128)}, s32[]{:T(128)}, s32[]{:T(128)}) while((s32[]{:T(128)}, f32[2,135]{1,0:T(2,128)S(1)}, s32[]{:T(128)}, f32[8,2,135,135]{3,2,1,0:T(8,128)}, ...), condition=%wide.region_16.17_spmd, body=%wide.region_15.16_spmd.sunk | while | flops 437676 | bytes 284075 | solution.py:33
  180.9 1.3 fusion.100
  182.2 1.3 fusion.100
  183.5 1.3 fusion.100
  184.8 1.3 fusion.100
  186.2 1.3 fusion.100
  187.5 1.3 fusion.100
  188.8 1.3 fusion.100
  190.1 22.6 %while.120 = (s32[]{:T(128)}, f32[2,135]{1,0:T(2,128)S(1)}, f32[8,2,135]{2,0,1:T(8,128)S(1)}, s32[8]{0:T(128)S(1)}, f32[8,2,135]{2,1,0:T(2,128)S(1)}, /*index=5*...) while((s32[]{:T(128)}, f32[2,135]{1,0:T(2,128)S(1)}, ...), condition=%wide.region_18.19_spmd, body=%wide.region_17.18_spmd.sunk | while | flops 437676 | bytes 150123 | solution.py:74
  190.1 0.7 dynamic_slice.221
  193.0 0.7 dynamic_slice.221
  195.8 0.7 dynamic_slice.221
  198.6 0.7 dynamic_slice.221
  201.5 0.7 dynamic_slice.221
  204.3 0.7 dynamic_slice.221
  207.1 0.7 dynamic_slice.221
  209.9 0.7 dynamic_slice.221
  (219 shorter events, 25.5 us)
Async XLA Ops:
  6.5 112.4 %all-gather.11.cloned.1.call-start = ((), (), s32[]{:S(2)}) async-start(), calls=%async_computation.1 | async-start | bytes 2506752 | tf_op jit(solution)/shard_map/all_gather | solution.py:24
  8.1 23.8 %copy-start.4 = (f32[2,8,135]{2,1,0:T(8,128)S(1)}, f32[2,8,135]{2,1,0:T(8,128)}, u32[]{:S(2)}) copy-start(f32[2,8,135]{2,1,0:T(8,128)} %param.26) | copy-start | bytes 25924
  8.1 29.0 %copy-start.2 = (bf16[2,8,135,135]{3,1,2,0:T(8,128)(2,1)S(1)}, bf16[2,8,135,135]{3,1,2,0:T(8,128)(2,1)}, u32[]{:S(2)}) copy-start(bf16[2,8,135,135]{3,1,2,0:T(8,128)(2,1)} %param.31) | copy-start | bytes 1749604
  31.1 0.7 copy-start.1
  31.8 149.1 %all-gather.9.cloned.1.call-start = ((), (), s32[]{:S(2)}) async-start(), calls=%async_computation | async-start | bytes 2506752 | tf_op jit(solution)/shard_map/all_gather | solution.py:24
  31.9 32.2 %collective-permute-start = (f32[2,8,135]{2,0,1:T(2,128)S(1)}, f32[2,8,135]{2,0,1:T(2,128)S(1)}, u32[]{:S(2)}, u32[]{:S(2)}) collective-permute-start(f32[2,8,135]{2,0,1:T(2,128)S(1)} %copy.29), channel_id=1, source_target_pairs={{0,1},{1,2},{2,3},{3,0},{4,5},{5,6},{6,7},{7,4},{8,9},{9,10},{10,1... | collective-permute-start | bytes 25928 | tf_op jit(solution)/shard_map/ppermute | solution.py:14
  35.0 29.2 %collective-permute-start.1 = (f32[2,8,135]{2,0,1:T(2,128)S(1)}, f32[2,8,135]{2,0,1:T(2,128)S(1)}, u32[]{:S(2)}, u32[]{:S(2)}) collective-permute-start(f32[2,8,135]{2,0,1:T(2,128)S(1)} %copy.29), channel_id=1, source_target_pairs={{1,0},{2,1},{3,2},{0,3},{5,4},{6,5},{7,6},{4,7},{9,8},{10,9},{11,1... | collective-permute-start | bytes 25928 | tf_op jit(solution)/shard_map/ppermute | solution.py:15
  37.3 25.2 %copy-start.6 = (s32[2,4]{1,0:T(2,128)S(1)}, s32[2,4]{1,0:T(2,128)}, u32[]{:S(2)}) copy-start(s32[2,4]{1,0:T(2,128)} %param.28) | copy-start | bytes 100
  61.8 0.7 copy-start
  62.6 1.6 copy-start.7
  62.6 1.9 copy-start.3
  212.8 0.6 copy-start.5
Sparse Core Ops, SparseCore 0:
  31.9 31.1 all-gather.10
  65.1 28.5 all-gather.8
where the time goes:
time: 222 us; the launch traced here: 220 us
  loops' own time  109 us (49%)
  local copies, waits for them, and re-layouts  42.7 us (19%)
  blocking collectives  26.1 us (12%)
  matrix products  22.8 us (10%)
  between operations  13.7 us (6%)
  starting transfers between devices  5.21 us (2%)
    dynamic_slice x56, local copies, waits for them, and re-layouts, pivot_terms(): return lax.map(pivot_visit, jnp.arange(source.shape[1], dtype=jnp.int32))  36.4 us
    another operation x2, loops' own time, chain_product(): lax.scan(chain_visit, identity, jnp.arange(blocks.shape[1], dtype=jnp.int...  31.9 us
    another operation x2, loops' own time, forward_sweep(): lax.scan(forward_visit, inflow, jnp.arange(driven.shape[0], dtype=jnp.int...  31.7 us
    another operation x2, loops' own time, backward_sweep(): lax.scan(backward_visit, inflow, jnp.arange(values.shape[0], dtype=jnp.in...  30.6 us
    all_gather x2, blocking collectives, entering(): gathered = jax.tree.map(lambda a: lax.all_gather(a, axis), part)  26.1 us
    dot_general x47, matrix products, apply_block(): jnp.einsum('lab,lb->la', matrix, vector, precision=lax.Precision.HIGHEST)  17.7 us
    another operation x1, loops' own time, pivot_terms(): return lax.map(pivot_visit, jnp.arange(source.shape[1], dtype=jnp.int32))  15.1 us
    dot_general x16, matrix products, times_block(): jnp.einsum('lab,lbc->lac', matrix, other, precision=lax.Precision.HIGHEST)  4.82 us
  transfers between devices with their start and end apart: 4, of which 0 were waited for; matrix products, arithmetic and copies ran while one was open for 17% of the time, Pallas kernels for 0%

commit v1 on v0

v1 whole, which is shorter than its diff:
```python
import functools

import jax
import jax.numpy as jnp
from jax import lax
from jax.experimental import pallas as pl
from jax.experimental.pallas import tpu as pltpu
from jax.sharding import PartitionSpec as P

F32 = jnp.float32
BF16 = jnp.bfloat16
VMEM = pl.BlockSpec(memory_space=pltpu.VMEM)
SMEM = pl.BlockSpec(memory_space=pltpu.SMEM)
LANES = 256
LIMIT = 40 * 1024 * 1024


def dot_nt(a, b):
    return lax.dot_general(a, b, (((1,), (1,)), ((), ())), preferred_element_type=F32)


def dot_nn(a, b):
    return lax.dot_general(a, b, (((1,), (0,)), ((), ())), preferred_element_type=F32)


def stacked(x):
    rest = x - x.astype(BF16).astype(F32)
    return jnp.concatenate([x, rest], axis=0).astype(BF16)


def times_block(x, block):
    n = x.shape[0]
    r = dot_nt(stacked(x), block)
    return r[:n] + r[n:]


def times_map(x, m):
    n = x.shape[0]
    hi = m.astype(BF16)
    lo = (m - hi.astype(F32)).astype(BF16)
    a = stacked(x)
    r = dot_nn(a, hi)
    return r[:n] + r[n:] + dot_nn(a[:n], lo)


def maps_kernel(lower, upper, tail, lead):
    rows, cells, width, _ = lower.shape
    high = lead.shape[1]
    eye = (
        lax.broadcasted_iota(jnp.int32, (high, width), 0)
        == lax.broadcasted_iota(jnp.int32, (high, width), 1)
    ).astype(BF16)
    lead[...] = jnp.zeros(lead.shape, F32)
    tail[...] = jnp.zeros(tail.shape, F32)
    for i in range(cells):
        for l in range(rows):
            if i == 0:
                now = dot_nt(eye, lower[l, 0])
            else:
                now = times_block(tail[l, i - 1, :high, :width], lower[l, i])
            tail[l, i, :high, :width] = now
    for l in range(rows):
        lead[l, :, :width] = tail[l, cells - 1, :high, :width]
    for i in reversed(range(cells)):
        for l in range(rows):
            if i == cells - 1:
                tail[l, i, high:, :width] = dot_nt(eye, upper[l, i])
                continue_g = dot_nt(eye, upper[l, i])
            else:
                both = times_block(tail[l, i + 1, :, :width], upper[l, i])
                tail[l, i, :high, :width] += both[:high]
                tail[l, i, high:, :width] = both[high:]


def segment_kernel(
    where, neighbours, right, own, first, second, coupling, pivots, lower, upper,
    lead, tail, inner, keep, send, near,
):
    rows, cells, width = right.shape
    high = lead.shape[1]
    core = where[0]
    here = where[1]
    patches = where[2]
    for l in range(rows):
        near[l] = own[l]
        near[rows + l] = first[l]
        near[2 * rows + l] = second[l]
    even = lax.rem(here, 2) == 0
    driven = []
    for l in range(rows):
        total = right[l]
        for f in range(coupling.shape[2]):
            line = neighbours[l, f]
            patch = line // rows
            ahead = lax.rem(patch - here + patches, patches)
            before = jnp.where(even, 2, 1)
            after = jnp.where(even, 1, 2)
            slot = jnp.where(ahead == 0, 0, jnp.where(ahead == 1, after, before))
            total = total - coupling[l, :, f, :] * near[slot * rows + lax.rem(line, rows)]
        driven.append(total)
    lhs = [stacked(d) for d in driven]
    value = [None] * rows
    values = [[None] * cells for _ in range(rows)]
    for i in range(cells):
        for l in range(rows):
            r = dot_nt(lhs[l], pivots[l, i])
            d = jnp.broadcast_to(r[i : i + 1] + r[cells + i : cells + i + 1], (8, width))
            if i:
                d = d + times_block(value[l], lower[l, i])
            value[l] = d
            values[l][i] = d
    corr = [None] * rows
    for i in reversed(range(cells)):
        for l in range(rows):
            d = values[l][i]
            if i < cells - 1:
                d = d + times_block(corr[l], upper[l, i])
            corr[l] = d
            inner[l, i : i + 1, :] = d[:1]
    unit = (lax.broadcasted_iota(jnp.int32, (high, LANES), 0) == high - 1) & (
        lax.broadcasted_iota(jnp.int32, (high, LANES), 1) == high - 1
    )
    for l in range(rows):
        def put(dst):
            dst[0] = jnp.where(unit, 1.0, lead[l])
            dst[1] = tail[l, 0, :high, :]
            dst[2] = tail[l, 0, high:, :]
            dst[0, width : width + 1, :width] = value[l][:1]
            dst[1, width : width + 1, :width] = corr[l][:1]

        @pl.when(core == l)
        def _():
            put(keep)

        @pl.when(core != l)
        def _():
            put(send)


def merge_kernel(side, mine, theirs, down, up):
    s = side[0]
    high = mine.shape[1]

    def pick(k):
        a, b = mine[k], theirs[k]
        return jnp.where(s == 0, a, b), jnp.where(s == 0, b, a)

    f_left, f_right = pick(0)
    g_left, g_right = pick(1)
    b_left, b_right = pick(2)
    down[0] = f_left
    down[1] = g_right
    down[2] = b_right
    lhs = f_left[:, :high]
    up[0] = times_map(lhs, f_right)
    inner = times_map(lhs, g_right)
    both = times_map(jnp.concatenate([inner, b_right], axis=0)[:, :high], b_left)
    up[1] = g_left + both[:high]
    up[2] = both[high:]


def top_kernel(sides, mine, theirs, *refs):
    downs, out = refs[:-1], refs[-1]
    levels = len(downs)
    s = sides[levels]
    high = mine.shape[1]
    f_left = jnp.where(s == 0, mine[0], theirs[0])
    g_right = jnp.where(s == 0, theirs[1], mine[1])
    unit = lax.broadcasted_iota(jnp.int32, (8, LANES), 1) == high - 1
    one = jnp.where(unit, 1.0, 0.0)
    middle = jnp.broadcast_to(f_left[high - 1 : high], (8, LANES))
    back = times_map(middle[:, :high], g_right)
    value = jnp.where(s == 0, one, middle)
    corr = jnp.where(s == 0, back, 0.0)
    for k in reversed(range(levels)):
        d = downs[k]
        middle = times_map(value[:, :high], d[0])
        back = times_map(middle[:, :high], d[1]) + times_map(corr[:, :high], d[2])
        if k:
            value = jnp.where(sides[k] == 0, value, middle)
            corr = jnp.where(sides[k] == 0, back, corr)
        else:
            out[0] = jnp.where(sides[0] == 0, value, middle)
            out[1] = jnp.where(sides[0] == 0, back, corr)
            out[2] = jnp.where(sides[0] == 0, middle, value)
            out[3] = jnp.where(sides[0] == 0, corr, back)


def final_kernel(where, mine, theirs, inner, tail, out):
    rows, cells, width = inner.shape
    high = tail.shape[2] // 2
    core = where[0]
    for l in range(rows):
        y = jnp.where(core == l, mine[0], theirs[0])
        c = jnp.where(core == l, mine[1], theirs[1])
        ycol = jnp.transpose(y)[:high, :1]
        ccol = jnp.transpose(c)[:high, :1]
        for i in range(cells):
            t = tail[l, i, :high, :] * ycol + tail[l, i, high:, :] * ccol
            out[l, i : i + 1, :] = inner[l, i : i + 1, :] + jnp.sum(t, axis=0, keepdims=True)[:, :width]


def call(body, outs, specs, scratch=()):
    return pl.pallas_call(
        body,
        out_shape=outs,
        in_specs=specs,
        out_specs=jax.tree.map(lambda _: VMEM, outs),
        scratch_shapes=scratch,
        compiler_params=pltpu.CompilerParams(vmem_limit_bytes=LIMIT),
    )


def f32(*shape):
    return jax.ShapeDtypeStruct(shape, F32)


def shards(right_side, previous, coupling, neighbours, pivots, lower_factor, upper_factor):
    rows, cells, width = right_side.shape
    high = width + 1
    patches = lax.axis_size("surf")
    here = lax.axis_index("surf")
    count = lax.axis_size("line")
    place = lax.axis_index("line")
    levels = count.bit_length() - 1
    core = place % 2
    pairs = [(i, i + 1 - 2 * (i % 2)) for i in range(patches)]
    odd = [(i, (i - 1 + 2 * (i % 2)) % patches) for i in range(patches)]
    second = lax.ppermute(previous, "surf", odd)
    first = lax.ppermute(previous, "surf", pairs)
    where = jnp.stack([core, here, jnp.int32(patches)]).astype(jnp.int32)
    sides = jnp.stack([(place >> k) & 1 for k in range(levels)]).astype(jnp.int32)
    tail, lead = call(
        maps_kernel,
        [f32(rows, cells, 2 * high, LANES), f32(rows, high, LANES)],
        [VMEM] * 2,
    )(lower_factor, upper_factor)
    inner, keep, send = call(
        segment_kernel,
        [f32(rows, cells, width), f32(3, high, LANES), f32(3, high, LANES)],
        [SMEM] * 2 + [VMEM] * 10,
        [pltpu.VMEM((3 * rows, cells, width), F32)],
    )(
        where, neighbours, right_side, previous, first, second, coupling, pivots,
        lower_factor, upper_factor, lead, tail,
    )
    swap = lambda a, k: lax.ppermute(a, "line", [(i, i ^ (1 << k)) for i in range(count)])
    downs = []
    theirs = swap(send, 0)
    mine = keep
    for k in range(levels - 1):
        down, mine = call(
            merge_kernel, [f32(3, high, LANES), f32(3, high, LANES)], [SMEM, VMEM, VMEM]
        )(sides[k : k + 1], mine, theirs)
        downs.append(down)
        if k + 1 == levels - 1:
            mine = mine[:2]
        theirs = swap(mine, k + 1)
    ends = call(top_kernel, [f32(4, 8, LANES)], [SMEM] + [VMEM] * (2 + len(downs)))(
        sides, mine, theirs, *downs
    )[0]
    other = swap(ends[2:], 0)
    return call(final_kernel, [f32(rows, cells, width)], [SMEM] + [VMEM] * 4)(
        where, ends[:2], other, inner, tail
    )[0]


def solution(mesh):
    return jax.shard_map(
        shards,
        mesh=mesh,
        in_specs=(
            P("surf", "line", None),
            P("surf", "line", None),
            P("surf", "line", None, None),
            P("surf", None),
            P("surf", "line", None, None),
            P("surf", "line", None, None),
            P("surf", "line", None, None),
        ),
        out_specs=P("surf", "line", None),
        check_vma=False,
    )
```

time: 222 us -> 43.5 us (0.20)
  loops' own time: 109 us -> 0 us
  local copies, waits for them, and re-layouts: 42.7 us -> 5.32 us
  blocking collectives: 26.1 us -> 0 us
  matrix products: 22.8 us -> 0 us
  waiting for transfers between devices: 0.04 us -> 19.4 us
  between operations: 13.7 us -> 0.19 us
  Pallas kernels: 0 us -> 9.47 us
  starting transfers between devices: 5.21 us -> 8.78 us
    another operation x9 -> x0, loops' own time: 109 us -> none  [the longest x2 31.9 us: chain_product(): lax.scan(chain_visit, identity, jnp.arange(blocks.shape[1], dtype=jnp.int...]
    dynamic_slice x64 -> x0, local copies, waits for them, and re-layouts: 36.5 us -> none  [the longest x56 36.4 us: pivot_terms(): return lax.map(pivot_visit, jnp.arange(source.shape[1], dtype=jnp.int32))]
    all_gather x2 -> x0, blocking collectives: 26.1 us -> none  [entering(): gathered = jax.tree.map(lambda a: lax.all_gather(a, axis), part)]
    dot_general x64 -> x0, matrix products: 22.8 us -> none  [the longest x47 17.7 us: apply_block(): jnp.einsum('lab,lb->la', matrix, vector, precision=lax.Precision.HIGHEST)]
    ppermute x2 -> x6, waiting for transfers between devices: 0.01 us -> 19.4 us  [the longest x4 19.4 us: shards(): lax.ppermute(a, 'line', [(i, i ^ 1 << k) for i in range(count)])]
    pallas_call x0 -> x6, Pallas kernels: none -> 9.47 us  [the longest x1 3.3 us: shards(): call(maps_kernel, [f32(rows, cells, 2 * high, LANES), f32(rows, high, LAN...]
    ppermute x2 -> x6, starting transfers between devices: 5.17 us -> 8.78 us  [the longest x4 3.28 us: shards(): lax.ppermute(a, 'line', [(i, i ^ 1 << k) for i in range(count)])]
    while x19 -> x0, local copies, waits for them, and re-layouts: 3.51 us -> none  [the longest x2 1.69 us: chain_product(): lax.scan(chain_visit, identity, jnp.arange(blocks.shape[1], dtype=jnp.int...]
  transfers between devices with their start and end apart: 4 -> 6, of which waited for: 0 -> 4; matrix products, arithmetic and copies ran while one was open for 17% -> 5% of each run, Pallas kernels for 0% -> 8%
where the time goes in v1:
time: 43.5 us; the launch traced here: 43.3 us
  waiting for transfers between devices  19.4 us (45%)
  Pallas kernels  9.47 us (22%)
  starting transfers between devices  8.78 us (20%)
  local copies, waits for them, and re-layouts  5.32 us (12%)
    ppermute x4, waiting for transfers between devices, shards(): lax.ppermute(a, 'line', [(i, i ^ 1 << k) for i in range(count)])  19.4 us
    unnamed x19, local copies, waits for them, and re-layouts  5.29 us
    pallas_call x1, Pallas kernels, shards(): call(maps_kernel, [f32(rows, cells, 2 * high, LANES), f32(rows, high, LAN...  3.3 us
    ppermute x4, starting transfers between devices, shards(): lax.ppermute(a, 'line', [(i, i ^ 1 << k) for i in range(count)])  3.28 us
    ppermute x1, starting transfers between devices, shards(): first = lax.ppermute(previous, 'surf', pairs)  3.02 us
    pallas_call x1, Pallas kernels, shards(): call(segment_kernel, [f32(rows, cells, width), f32(3, high, LANES), f32(3...  2.51 us
    ppermute x1, starting transfers between devices, shards(): second = lax.ppermute(previous, 'surf', odd)  2.47 us
    pallas_call x1, Pallas kernels, shards(): call(final_kernel, [f32(rows, cells, width)], [SMEM] + [VMEM] * 4)  1.68 us
  transfers between devices with their start and end apart: 6, of which 4 were waited for; matrix products, arithmetic and copies ran while one was open for 5% of the time, Pallas kernels for 8%

profile of v1, /device:TPU:0, one launch (start us, length us, event | category | flops | bytes accessed | tf_op | source)
XLA Modules:
  0.0 43.3 jit_solution(3033313742128841358)
XLA Ops:
  0.0 3.0 %collective-permute-start = (f32[2,8,135]{2,1,0:T(8,128)}, f32[2,8,135]{2,1,0:T(8,128)S(1)}, u32[]{:S(2)}, u32[]{:S(2)}) collective-permute-start(f32[2,8,135]{2,1,0:T(8,128)} %own.1), channel_id=1, source_target_pairs={{0,1},{1,0},{2,3},{3,2},{4,5},{5,4},{6,7},{7,6},{8,9},{9,8},{10,11... | collective-permute-start | bytes 25928 | tf_op jit(solution)/shard_map/ppermute | solution.py:230
  3.0 2.5 %collective-permute-start.1 = (f32[2,8,135]{2,1,0:T(8,128)}, f32[2,8,135]{2,1,0:T(8,128)S(1)}, u32[]{:S(2)}, u32[]{:S(2)}) collective-permute-start(f32[2,8,135]{2,1,0:T(8,128)} %own.1), channel_id=1, source_target_pairs={{0,3},{1,2},{2,1},{3,0},{4,7},{5,6},{6,5},{7,4},{8,11},{9,10},{10,... | collective-permute-start | bytes 25928 | tf_op jit(solution)/shard_map/ppermute | solution.py:229
  5.5 0.0 copy-start.6
  5.5 0.1 pad_add_fusion.where
  5.6 1.5 %copy.11.lower = bf16[2,8,135,135]{3,2,1,0:T(8,128)(2,1)S(1)} copy(bf16[2,8,135,135]{3,1,2,0:T(8,128)(2,1)} %param.12) | data formatting | bytes 1166400 | tf_op args[5]
  7.1 0.0 copy-done.6
  7.1 0.0 copy-start.7
  7.1 0.2 copy.12.upper
  7.4 1.0 %copy-done.7 = bf16[2,8,135,135]{3,1,2,0:T(8,128)(2,1)S(1)} copy-done((bf16[2,8,135,135]{3,1,2,0:T(8,128)(2,1)S(1)}, bf16[2,8,135,135]{3,1,2,0:T(8,128)(2,1)}, u32[]{:S(2)}) %copy-start.7) | copy-done | bytes 583224
  8.4 0.2 copy.10.pivots
  8.6 0.0 copy-start.2
  8.6 0.0 copy-start.3
  8.6 0.0 copy-start.4
  8.6 0.0 copy-start.5
  8.7 3.3 %shard_map.73 = (f32[2,8,272,256]{3,2,1,0:T(8,128)S(1)}, f32[2,136,256]{2,1,0:T(8,128)S(1)}) custom-call(bf16[2,8,135,135]{3,2,1,0:T(8,128)(2,1)S(1)} %copy.11.lower, bf16[2,8,135,135]{3,2,1,0:T(8,128)(2,1)S(1)} %copy.12.upper), custom_call_target="tpu_custom_call" | custom-call | tf_op jit(solution)/shard_map/pallas_call | solution.py:233
  12.0 0.0 copy-start
  12.0 0.0 collective-permute-done.first
  12.0 0.0 collective-permute-done.1.second
  12.0 0.0 copy-done.2
  12.0 0.0 copy-done.3
  12.0 0.0 copy-done.4
  12.0 0.0 copy-done.5
  12.0 2.5 %shard_map.74 = (f32[2,8,135]{2,1,0:T(8,128)S(1)}, f32[3,136,256]{2,1,0:T(8,128)S(1)}, f32[3,136,256]{2,1,0:T(8,128)S(1)}) custom-call(s32[3]{0:T(128)S(1)} %pad_add_fusion.where, s32[2,4]{1,0:T(2,128)S(1)} %copy-done.5, f32[2,8,135]{2,1,0:T(8,128)S(1)} %copy-done.3, f32[2,8,135]{2,1,0:T(8,128)S(1)} %copy-done.4, ...), custom_call_target="tpu_custom_call" | custom-call | tf_op jit(solution)/shard_map/pallas_call | solution.py:238
  14.5 0.0 copy-done
  14.6 0.1 collective-permute-start.2
  14.6 1.7 %collective-permute-done.2.theirs = f32[3,136,256]{2,1,0:T(8,128)S(1)} collective-permute-done((f32[3,136,256]{2,1,0:T(8,128)S(1)}, f32[3,136,256]{2,1,0:T(8,128)S(1)}, u32[]{:S(2)}, u32[]{:S(2)}) %collective-permute-start.2) | collective-permute-done | bytes 417824 | tf_op jit(solution)/shard_map/ppermute | solution.py:247
  16.4 0.5 %shard_map.75 = (f32[3,136,256]{2,1,0:T(8,128)S(1)}, f32[3,136,256]{2,1,0:T(8,128)S(1)}) custom-call(s32[1]{0:T(128)} %bitcast.2.side, f32[3,136,256]{2,1,0:T(8,128)S(1)} %get-tuple-element.16.mine, f32[3,136,256]{2,1,0:T(8,128)S(1)} %collective-permute-done.2.theirs), custom_call_target="tpu_custom_call" | custom-call | tf_op jit(solution)/shard_map/pallas_call | solution.py:252
  16.9 1.6 %collective-permute-start.3 = (f32[3,136,256]{2,1,0:T(8,128)S(1)}, f32[3,136,256]{2,1,0:T(8,128)S(1)}, u32[]{:S(2)}, u32[]{:S(2)}) collective-permute-start(f32[3,136,256]{2,1,0:T(8,128)S(1)} %get-tuple-element.18.mine), channel_id=1, source_target_pairs={{0,8},{4,12},{8,0},{12,4},{16,24},{20,28},{24,16},{28,20},{1,9},{5... | collective-permute-start | bytes 1253384 | tf_op jit(solution)/shard_map/ppermute | solution.py:247
  18.4 10.2 %collective-permute-done.3.theirs = f32[3,136,256]{2,1,0:T(8,128)S(1)} collective-permute-done((f32[3,136,256]{2,1,0:T(8,128)S(1)}, f32[3,136,256]{2,1,0:T(8,128)S(1)}, u32[]{:S(2)}, u32[]{:S(2)}) %collective-permute-start.3) | collective-permute-done | bytes 417824 | tf_op jit(solution)/shard_map/ppermute | solution.py:247
  28.6 0.5 %shard_map.76 = (f32[3,136,256]{2,1,0:T(8,128)S(1)}, f32[3,136,256]{2,1,0:T(8,128)S(1)}) custom-call(s32[1]{0:T(128)} %bitcast.3.side, f32[3,136,256]{2,1,0:T(8,128)S(1)} %get-tuple-element.18.mine, f32[3,136,256]{2,1,0:T(8,128)S(1)} %collective-permute-done.3.theirs), custom_call_target="tpu_custom_call" | custom-call | tf_op jit(solution)/shard_map/pallas_call | solution.py:252
  29.2 1.6 %collective-permute-start.4 = (f32[2,136,256]{2,1,0:T(8,128)S(1)}, f32[2,136,256]{2,1,0:T(8,128)S(1)}, u32[]{:S(2)}, u32[]{:S(2)}) collective-permute-start(f32[2,136,256]{2,1,0:T(8,128)S(1)} %slice.9.mine), channel_id=1, source_target_pairs={{0,16},{4,20},{8,24},{12,28},{16,0},{20,4},{24,8},{28,12},{1,17},{... | collective-permute-start | bytes 835592 | tf_op jit(solution)/shard_map/ppermute | solution.py:247
  30.7 0.1 pad_add_fusion.1.sides
  30.8 6.3 %collective-permute-done.4.theirs = f32[2,136,256]{2,1,0:T(8,128)S(1)} collective-permute-done((f32[2,136,256]{2,1,0:T(8,128)S(1)}, f32[2,136,256]{2,1,0:T(8,128)S(1)}, u32[]{:S(2)}, u32[]{:S(2)}) %collective-permute-start.4) | collective-permute-done | bytes 278560 | tf_op jit(solution)/shard_map/ppermute | solution.py:247
  37.1 1.0 %shard_map.77 = f32[4,8,256]{2,1,0:T(8,128)S(1)} custom-call(s32[3]{0:T(128)S(1)} %pad_add_fusion.1.sides, f32[2,136,256]{2,1,0:T(8,128)S(1)} %slice.9.mine, f32[2,136,256]{2,1,0:T(8,128)S(1)} %collective-permute-done.4.theirs, f32[3,136,256]{2,1,0:T(8,128)S(1)} %get-tuple-element.20.refs_0_, f32[3,136,256]{2,1,0:T(8,128)S(1)} %get-tuple-element.21.refs_1_), custom_call_target="tpu_custom_call" | custom-call | tf_op jit(solution)/shard_map/pallas_call | solution.py:259
  38.1 0.1 collective-permute-start.5
  38.2 1.2 %collective-permute-done.5.theirs = f32[2,8,256]{2,1,0:T(8,128)S(1)} collective-permute-done((f32[2,8,256]{2,1,0:T(8,128)S(1)}, f32[2,8,256]{2,1,0:T(8,128)S(1)}, u32[]{:S(2)}, u32[]{:S(2)}) %collective-permute-start.5) | collective-permute-done | bytes 16416 | tf_op jit(solution)/shard_map/ppermute | solution.py:247
  39.4 0.0 copy-start.1
  39.4 2.3 %copy-done.1 = f32[2,8,272,256]{3,2,1,0:T(8,128)S(1)} copy-done((f32[2,8,272,256]{3,2,1,0:T(8,128)S(1)}, f32[2,8,272,256]{3,2,1,0:T(8,128)}, u32[]{:S(2)}) %copy-start.1) | copy-done | bytes 4456472
  41.6 1.7 %shard_map.78 = f32[2,8,135]{2,1,0:T(8,128)} custom-call(s32[3]{0:T(128)S(1)} %pad_add_fusion.where, f32[2,8,256]{2,1,0:T(8,128)S(1)} %get-tuple-element.24.mine, f32[2,8,256]{2,1,0:T(8,128)S(1)} %collective-permute-done.5.theirs, f32[2,8,135]{2,1,0:T(8,128)S(1)} %get-tuple-element.22.inner, f32[2,8,272,256]{3,2,1,0:T(8,128)S(1)} %copy-done.1), custom_call_target="tpu_custom_call" | custom-call | tf_op jit(solution)/shard_map/pallas_call | solution.py:263
  (2 shorter events, 0.0 us)
Async XLA Ops:
  0.0 12.0 %collective-permute-start = (f32[2,8,135]{2,1,0:T(8,128)}, f32[2,8,135]{2,1,0:T(8,128)S(1)}, u32[]{:S(2)}, u32[]{:S(2)}) collective-permute-start(f32[2,8,135]{2,1,0:T(8,128)} %own.1), channel_id=1, source_target_pairs={{0,1},{1,0},{2,3},{3,2},{4,5},{5,4},{6,7},{7,6},{8,9},{9,8},{10,11... | collective-permute-start | bytes 25928 | tf_op jit(solution)/shard_map/ppermute | solution.py:230
  3.0 9.0 %collective-permute-start.1 = (f32[2,8,135]{2,1,0:T(8,128)}, f32[2,8,135]{2,1,0:T(8,128)S(1)}, u32[]{:S(2)}, u32[]{:S(2)}) collective-permute-start(f32[2,8,135]{2,1,0:T(8,128)} %own.1), channel_id=1, source_target_pairs={{0,3},{1,2},{2,1},{3,0},{4,7},{5,6},{6,5},{7,4},{8,11},{9,10},{10,... | collective-permute-start | bytes 25928 | tf_op jit(solution)/shard_map/ppermute | solution.py:229
  5.5 1.6 %copy-start.6 = (bf16[2,8,135,135]{3,1,2,0:T(8,128)(2,1)S(1)}, bf16[2,8,135,135]{3,1,2,0:T(8,128)(2,1)}, u32[]{:S(2)}) copy-start(bf16[2,8,135,135]{3,1,2,0:T(8,128)(2,1)} %param.13) | copy-start | bytes 1749604
  7.1 1.2 %copy-start.7 = (bf16[2,8,135,135]{3,1,2,0:T(8,128)(2,1)S(1)}, bf16[2,8,135,135]{3,1,2,0:T(8,128)(2,1)}, u32[]{:S(2)}) copy-start(bf16[2,8,135,135]{3,1,2,0:T(8,128)(2,1)} %param.11) | copy-start | bytes 1749604
  8.6 3.4 %copy-start.2 = (f32[2,8,4,135]{3,2,1,0:T(4,128)S(1)}, f32[2,8,4,135]{3,2,1,0:T(4,128)}, u32[]{:S(2)}) copy-start(f32[2,8,4,135]{3,2,1,0:T(4,128)} %coupling.1) | copy-start | bytes 103684
  8.6 3.4 %copy-start.3 = (f32[2,8,135]{2,1,0:T(8,128)S(1)}, f32[2,8,135]{2,1,0:T(8,128)}, u32[]{:S(2)}) copy-start(f32[2,8,135]{2,1,0:T(8,128)} %right.1) | copy-start | bytes 25924
  8.6 3.4 %copy-start.4 = (f32[2,8,135]{2,1,0:T(8,128)S(1)}, f32[2,8,135]{2,1,0:T(8,128)}, u32[]{:S(2)}) copy-start(f32[2,8,135]{2,1,0:T(8,128)} %own.1) | copy-start | bytes 25924
  8.6 3.4 %copy-start.5 = (s32[2,4]{1,0:T(2,128)S(1)}, s32[2,4]{1,0:T(2,128)}, u32[]{:S(2)}) copy-start(s32[2,4]{1,0:T(2,128)} %neighbours.1) | copy-start | bytes 100
  12.0 2.6 %copy-start = (f32[2,8,272,256]{3,2,1,0:T(8,128)}, f32[2,8,272,256]{3,2,1,0:T(8,128)S(1)}, u32[]{:S(2)}) copy-start(f32[2,8,272,256]{3,2,1,0:T(8,128)S(1)} %get-tuple-element.15.tail) | copy-start | bytes 13369348
  14.6 1.8 %collective-permute-start.2 = (f32[3,136,256]{2,1,0:T(8,128)S(1)}, f32[3,136,256]{2,1,0:T(8,128)S(1)}, u32[]{:S(2)}, u32[]{:S(2)}) collective-permute-start(f32[3,136,256]{2,1,0:T(8,128)S(1)} %get-tuple-element.17), channel_id=1, source_target_pairs={{0,4},{4,0},{8,12},{12,8},{16,20},{20,16},{24,28},{28,24},{1,5},{5... | collective-permute-start | bytes 1253384 | tf_op jit(solution)/shard_map/ppermute | solution.py:247
  16.9 11.7 %collective-permute-start.3 = (f32[3,136,256]{2,1,0:T(8,128)S(1)}, f32[3,136,256]{2,1,0:T(8,128)S(1)}, u32[]{:S(2)}, u32[]{:S(2)}) collective-permute-start(f32[3,136,256]{2,1,0:T(8,128)S(1)} %get-tuple-element.18.mine), channel_id=1, source_target_pairs={{0,8},{4,12},{8,0},{12,4},{16,24},{20,28},{24,16},{28,20},{1,9},{5... | collective-permute-start | bytes 1253384 | tf_op jit(solution)/shard_map/ppermute | solution.py:247
  29.2 7.9 %collective-permute-start.4 = (f32[2,136,256]{2,1,0:T(8,128)S(1)}, f32[2,136,256]{2,1,0:T(8,128)S(1)}, u32[]{:S(2)}, u32[]{:S(2)}) collective-permute-start(f32[2,136,256]{2,1,0:T(8,128)S(1)} %slice.9.mine), channel_id=1, source_target_pairs={{0,16},{4,20},{8,24},{12,28},{16,0},{20,4},{24,8},{28,12},{1,17},{... | collective-permute-start | bytes 835592 | tf_op jit(solution)/shard_map/ppermute | solution.py:247
  38.1 1.2 %collective-permute-start.5 = (f32[2,8,256]{2,1,0:T(8,128)S(1)}, f32[2,8,256]{2,1,0:T(8,128)S(1)}, u32[]{:S(2)}, u32[]{:S(2)}) collective-permute-start(f32[2,8,256]{2,1,0:T(8,128)S(1)} %get-tuple-element.23), channel_id=1, source_target_pairs={{0,4},{4,0},{8,12},{12,8},{16,20},{20,16},{24,28},{28,24},{1,5},{5... | collective-permute-start | bytes 49160 | tf_op jit(solution)/shard_map/ppermute | solution.py:247
  39.4 2.3 %copy-start.1 = (f32[2,8,272,256]{3,2,1,0:T(8,128)S(1)}, f32[2,8,272,256]{3,2,1,0:T(8,128)}, u32[]{:S(2)}) copy-start(f32[2,8,272,256]{3,2,1,0:T(8,128)} %copy-done) | copy-start | bytes 13369348

commit v2 on v1

v2 whole, which is shorter than its diff:
```python
import functools

import jax
import jax.numpy as jnp
from jax import lax
from jax.experimental import pallas as pl
from jax.experimental.pallas import tpu as pltpu
from jax.sharding import PartitionSpec as P

F32 = jnp.float32
BF16 = jnp.bfloat16
VMEM = pl.BlockSpec(memory_space=pltpu.VMEM)
LANES = 256
LIMIT = 12 * 1024 * 1024


def dot_nt(a, b):
    return lax.dot_general(a, b, (((1,), (1,)), ((), ())), preferred_element_type=F32)


def dot_nn(a, b):
    return lax.dot_general(a, b, (((1,), (0,)), ((), ())), preferred_element_type=F32)


def stacked(x):
    rest = x - x.astype(BF16).astype(F32)
    return jnp.concatenate([x, rest], axis=0).astype(BF16)


def times_block(x, block):
    n = x.shape[0]
    r = dot_nt(stacked(x), block)
    return r[:n] + r[n:]


def times_map(x, m):
    n = x.shape[0]
    hi = m.astype(BF16)
    lo = (m - hi.astype(F32)).astype(BF16)
    a = stacked(x)
    r = dot_nn(a, hi)
    return r[:n] + r[n:] + dot_nn(a[:n], lo)


def vector(row):
    return jnp.broadcast_to(row, (8, row.shape[1]))


def packed(m):
    top = jnp.transpose(m[:128, 128:])[:8]
    return jnp.concatenate([m[:, :128], top, m[128:, 128:]], axis=0)


def unpacked(p):
    high = p.shape[0] - 16
    top = jnp.concatenate([p[high : high + 8], jnp.zeros((120, 128), F32)], axis=0)
    right = jnp.concatenate([jnp.transpose(top), p[high + 8 :]], axis=0)
    return jnp.concatenate([p[:high], right], axis=1)


def maps_kernel(lower, upper, tail, half, keep, send):
    rows, cells, width, _ = lower.shape
    high = keep.shape[1]
    per = cells // 2
    core = side(0)
    eye = (
        lax.broadcasted_iota(jnp.int32, (high, width), 0)
        == lax.broadcasted_iota(jnp.int32, (high, width), 1)
    ).astype(BF16)
    blank = jnp.zeros((high, LANES - 128), F32)
    for k in range(3):
        keep[k, :, 128:] = blank
        send[k, :, 128:] = blank
        for l in range(rows):
            half[l, k, :, 128:] = blank
    chains = [(l, p) for l in range(rows) for p in range(2)]
    ahead = {}
    for j in range(per):
        for l, p in chains:
            i = p * per + j
            block = lower[l, i]
            ahead[l, p] = times_block(ahead[l, p], block) if j else dot_nt(eye, block)
            tail[l, i, :high, :width] = ahead[l, p]
    back = {}
    for j in reversed(range(per)):
        for l, p in chains:
            i = p * per + j
            if j == per - 1:
                back[l, p] = jnp.concatenate([ahead[l, p], dot_nt(eye, upper[l, i])], axis=0)
            else:
                both = times_block(back[l, p], upper[l, i])
                front = tail[l, i, :high, :width] + both[:high]
                back[l, p] = jnp.concatenate([front, both[high:]], axis=0)
                tail[l, i, :high, :width] = front
            tail[l, i, high:, :width] = back[l, p][high:]
    joint = []
    for l in range(rows):
        f = ahead[l, 0], ahead[l, 1]
        g = back[l, 0][:high], back[l, 1][:high]
        b = back[l, 0][high:], back[l, 1][high:]
        inward = times_map(f[0], g[1][:width])
        both = times_map(jnp.concatenate([inward, b[1]], axis=0), b[0][:width])
        for k, m in enumerate([f[0], inward, f[1]]):
            half[l, k, :, :width] = m
        joint.append([times_map(f[0], f[1][:width]), g[0] + both[:high], both[high:]])
    for k in range(3):
        keep[k, :, :width] = jnp.where(core == 0, joint[0][k], joint[1][k])
        send[k, :, :width] = jnp.where(core == 0, joint[1][k], joint[0][k])


def segment_kernel(
    patches, neighbours, right, own, first, second, coupling, pivots, lower, upper,
    tail, half, inner, bias, keep, send, pad,
):
    rows, cells, width = right.shape
    high = half.shape[2]
    per = cells // 2
    core = side(0)
    here = lax.axis_index("surf")
    odd = lax.rem(here, 2)
    after = lax.rem(here + 1, patches)
    before = lax.rem(here + patches - 1, patches)
    met = [here, jnp.where(odd == 0, after, before), jnp.where(odd == 0, before, after)]
    driven = []
    for l in range(rows):
        total = right[l]
        for f in range(coupling.shape[2]):
            line = jnp.broadcast_to(neighbours[l : l + 1, f : f + 1], (cells, width))
            near = jnp.zeros((cells, width), F32)
            for patch, held in zip(met, (own, first, second)):
                for r in range(rows):
                    near = jnp.where(line == patch * rows + r, held[r], near)
            total = total - coupling[l, :, f, :] * near
        driven.append(total)
    lhs = [stacked(d) for d in driven]
    chains = [(l, p) for l in range(rows) for p in range(2)]
    value, values, corr = {}, {}, {}
    for j in range(per):
        for l, p in chains:
            i = p * per + j
            r = dot_nt(lhs[l], pivots[l, i])
            d = vector(r[i : i + 1] + r[cells + i : cells + i + 1])
            if j:
                d = d + times_block(value[l, p], lower[l, i])
            value[l, p] = values[l, i] = d
    for j in reversed(range(per)):
        for l, p in chains:
            i = p * per + j
            d = values[l, i]
            if j < per - 1:
                d = d + times_block(corr[l, p], upper[l, i])
            corr[l, p] = d
            inner[l, i : i + 1, :] = d[:1]
    pad[...] = jnp.zeros(pad.shape, F32)
    ends = []
    for l in range(rows):
        for p in range(2):
            pad[l, p, :, :width] = value[l, p]
            pad[l, 2 + p, :, :width] = corr[l, p]
        f = [pad[l, 0], pad[l, 1]]
        g = [pad[l, 2], pad[l, 3]]
        v = merged_vectors(f, g, half[l, 2], tail[l, per, :high], tail[l, 0, high:])
        bias[l, 0] = f[0]
        bias[l, 1] = v[2]
        ends.append(v)
    keep[...] = jnp.zeros(keep.shape, F32)
    send[...] = jnp.zeros(send.shape, F32)
    for k in range(2):
        a, b = ends[0][k][:1, :width], ends[1][k][:1, :width]
        keep[k : k + 1, :width] = jnp.where(core == 0, a, b)
        send[k : k + 1, :width] = jnp.where(core == 0, b, a)


def side(level):
    return (lax.axis_index("line") >> level) & 1


def ordered(s, mine, theirs):
    return jnp.where(s == 0, mine, theirs), jnp.where(s == 0, theirs, mine)


def merged_maps(f, g, b, lean):
    high = f[0].shape[0]
    lhs = f[0][:, :high]
    inward = times_map(lhs, g[1])
    if lean:
        return [g[0] + times_map(inward[:, :high], b[0])], inward
    both = times_map(jnp.concatenate([inward, b[1]], axis=0)[:, :high], b[0])
    return [times_map(lhs, f[1]), g[0] + both[:high], both[high:]], inward


def merged_vectors(f, g, f_right, g_right, b_left):
    high = f_right.shape[0]
    between = times_map(f[0][:, :high], g_right) + g[1]
    return times_map(f[0][:, :high], f_right) + f[1], g[0] + times_map(between[:, :high], b_left), between


def first_maps_kernel(mine, theirs, after, down, full, pack):
    s = side(0)
    f, g, b = (ordered(s, mine[k], theirs[k]) for k in range(3))
    joint, inward = merged_maps(f, g, b, False)
    for k, m in enumerate([f[0], inward, b[1], f[1], g[1], b[0]]):
        down[k] = m
    size = pack.shape[0] // len(joint)
    for k, m in enumerate(joint):
        full[k] = m
        pack[k * size : (k + 1) * size] = packed(m)


def first_vectors_kernel(down, mine, theirs, out, bias):
    s = side(0)
    f = [vector(v) for v in ordered(s, mine[0:1], theirs[0:1])]
    g = [vector(v) for v in ordered(s, mine[1:2], theirs[1:2])]
    joint = merged_vectors(f, g, down[3], down[4], down[5])
    out[...] = jnp.zeros(out.shape, F32)
    out[0:1] = joint[0][:1]
    out[1:2] = joint[1][:1]
    bias[0] = f[0]
    bias[1] = joint[2]


def level_kernel(level, split, lean, mine, theirs, vectors, others, down, full, bias, out):
    high = mine.shape[1]
    size = high + 16
    maps = [unpacked(theirs[k * size : (k + 1) * size]) for k in range(3)]
    s = side(level)
    f, g, b = (ordered(s, mine[k], maps[k]) for k in range(3))
    joint, inward = merged_maps(f, g, b, lean)
    for k, m in enumerate([f[0], inward, b[1]]):
        down[k] = m
    if split:
        other = [others[0:1], others[1:2]]
    else:
        other = tail_vectors(theirs, 3 * size)
    vf = [vector(v) for v in ordered(s, vectors[0:1], other[0])]
    vg = [vector(v) for v in ordered(s, vectors[1:2], other[1])]
    v = merged_vectors(vf, vg, f[1], g[1], b[0])
    bias[0] = vf[0]
    bias[1] = v[2]
    for k, m in enumerate(joint):
        out[k * size : (k + 1) * size] = packed(m)
        if not lean:
            full[k] = m
    base = len(joint) * size
    full_vectors = jnp.concatenate([v[0][:1], v[1][:1]], axis=0)
    out[base : base + 2] = full_vectors[:, :128]
    out[base + 2 : base + 4] = full_vectors[:, 128:]
    out[base + 4 : base + 8] = jnp.zeros((4, 128), F32)
    full[full.shape[0] - 1, 0:2] = full_vectors


def tail_vectors(theirs, base):
    return [
        jnp.concatenate([theirs[base + k : base + k + 1], theirs[base + 2 + k : base + 3 + k]], axis=1)
        for k in range(2)
    ]


def top_kernel(levels, *refs):
    sides = [side(k) for k in range(levels + 1)]
    mine, theirs = refs[:2]
    downs, biases = refs[2 : levels + 2], refs[levels + 2 : 2 * levels + 2]
    keep, send = refs[-2:]
    s = sides[levels]
    size = theirs.shape[0] - 8
    high = size - 16
    g = unpacked(theirs[:size])
    other = [vector(v) for v in tail_vectors(theirs, size)]
    ours = vector(mine[mine.shape[0] - 1, 0:1])
    back = times_map(ours[:, :high], g) + other[1]
    value = jnp.where(s == 0, 0.0, other[0])
    corr = jnp.where(s == 0, back, 0.0)
    for k in reversed(range(levels)):
        d = downs[k]
        lhs = value[:, :high]
        middle = times_map(lhs, d[0]) + biases[k][0]
        back = times_map(lhs, d[1]) + times_map(corr[:, :high], d[2]) + biases[k][1]
        if k:
            value = jnp.where(sides[k] == 0, value, middle)
            corr = jnp.where(sides[k] == 0, back, corr)
    left = sides[0] == 0
    keep[0] = jnp.where(left, value, middle)
    keep[1] = jnp.where(left, back, corr)
    send[0] = jnp.where(left, middle, value)
    send[1] = jnp.where(left, corr, back)


def final_kernel(mine, theirs, inner, tail, half, bias, out):
    rows, cells, width = inner.shape
    high = half.shape[2]
    per = cells // 2
    core = side(0)
    index = lax.broadcasted_iota(jnp.int32, (8, LANES), 0)
    gathered = jnp.zeros((8, LANES), F32)
    for l in range(rows):
        y = jnp.where(core == l, mine[0], theirs[0])
        c = jnp.where(core == l, mine[1], theirs[1])
        lhs = y[:, :high]
        middle = times_map(lhs, half[l, 0]) + bias[l, 0]
        between = (
            times_map(lhs, half[l, 1])
            + times_map(c[:, :high], tail[l, per, high:])
            + bias[l, 1]
        )
        for k, v in enumerate([y, between, middle, c]):
            gathered = jnp.where(index == 4 * l + k, v, gathered)
    columns = jnp.transpose(gathered)[:high]
    for l in range(rows):
        for p in range(2):
            k = 4 * l + 2 * p
            ycol = jnp.broadcast_to(columns[:, k : k + 1], (high, 128))
            ccol = jnp.broadcast_to(columns[:, k + 1 : k + 2], (high, 128))
            col = jnp.concatenate([ycol, ccol], axis=0)
            for i in range(p * per, p * per + per):
                for h in range(2):
                    at = slice(128 * h, min(width, 128 * h + 128))
                    t = tail[l, i, :, 128 * h : 128 * h + 128] * col
                    r = jnp.sum(t, axis=0, keepdims=True)
                    out[l, i : i + 1, at] = inner[l, i : i + 1, at] + r[:, : at.stop - at.start]


def call(body, outs, specs, scratch=()):
    return pl.pallas_call(
        body,
        out_shape=outs,
        in_specs=specs,
        out_specs=jax.tree.map(lambda _: VMEM, outs),
        scratch_shapes=scratch,
        compiler_params=pltpu.CompilerParams(vmem_limit_bytes=LIMIT),
    )


def f32(*shape):
    return jax.ShapeDtypeStruct(shape, F32)


def shards(right_side, previous, coupling, neighbours, pivots, lower_factor, upper_factor):
    rows, cells, width = right_side.shape
    high = width + 1
    size = high + 16
    patches = lax.axis_size("surf")
    count = lax.axis_size("line")
    levels = count.bit_length() - 1
    pairs = [(i, i + 1 - 2 * (i % 2)) for i in range(patches)]
    odd = [(i, (i - 1 + 2 * (i % 2)) % patches) for i in range(patches)]
    swap = lambda a, k: lax.ppermute(a, "line", [(i, i ^ (1 << k)) for i in range(count)])
    second = lax.ppermute(previous, "surf", odd)
    first = lax.ppermute(previous, "surf", pairs)
    full = f32(3, high, LANES)
    row = f32(8, LANES)
    tail, half, keep, send = call(
        maps_kernel,
        [f32(rows, cells, 2 * high, LANES), f32(rows, 3, high, LANES), full, full],
        [VMEM] * 2,
    )(lower_factor, upper_factor)
    theirs = swap(send, 0)
    inner, ends, vkeep, vsend = call(
        functools.partial(segment_kernel, patches),
        [f32(rows, cells, width), f32(rows, 2, 8, LANES), row, row],
        [VMEM] * 11,
        [pltpu.VMEM((rows, 4, 8, LANES), F32)],
    )(
        neighbours, right_side, previous, first, second, coupling, pivots,
        lower_factor, upper_factor, tail, half,
    )
    down, mine, pack = call(
        first_maps_kernel,
        [f32(6, high, LANES), full, f32(3 * size, 128)],
        [VMEM] * 3,
    )(keep, theirs, vkeep)
    theirs = swap(pack, 1)
    vtheirs = swap(vsend, 0)
    vectors, bias = call(
        first_vectors_kernel, [row, f32(2, 8, LANES)], [VMEM] * 3
    )(down, vkeep, vtheirs)
    others = swap(vectors, 1)
    downs = [down]
    biases = [bias]
    for k in range(1, levels - 1):
        lean = k == levels - 2
        down, mine, bias, pack = call(
            functools.partial(level_kernel, k, k == 1, lean),
            [
                full, f32(1 if lean else 4, high, LANES), f32(2, 8, LANES),
                f32((1 if lean else 3) * size + 8, 128),
            ],
            [VMEM] * 4,
        )(mine, theirs, vectors, others)
        downs.append(down)
        biases.append(bias)
        vectors = others = mine[-1, :8]
        theirs = swap(pack, k + 1)
    keep, send = call(
        functools.partial(top_kernel, levels - 1),
        [f32(2, 8, LANES)] * 2,
        [VMEM] * (2 + 2 * len(downs)),
    )(mine, theirs, *downs, *biases)
    return call(final_kernel, [f32(rows, cells, width)], [VMEM] * 6)(
        keep, swap(send, 0), inner, tail, half, ends
    )[0]


def solution(mesh):
    return jax.shard_map(
        shards,
        mesh=mesh,
        in_specs=(
            P("surf", "line", None),
            P("surf", "line", None),
            P("surf", "line", None, None),
            P("surf", None),
            P("surf", "line", None, None),
            P("surf", "line", None, None),
            P("surf", "line", None, None),
        ),
        out_specs=P("surf", "line", None),
        check_vma=False,
    )
```

time: 43.5 us -> 30.4 us (0.70)
  waiting for transfers between devices: 19.4 us -> 11.4 us
  local copies, waits for them, and re-layouts: 5.32 us -> 2.05 us
  Pallas kernels: 9.47 us -> 7.39 us
  starting transfers between devices: 8.78 us -> 9.26 us
    ppermute x4 -> x6, waiting for transfers between devices: 19.4 us -> 8.59 us  [shards(): lax.ppermute(a, 'line', [(i, i ^ 1 << k) for i in range(count)])]
    unnamed x19 -> x15, local copies, waits for them, and re-layouts: 5.29 us -> 2.05 us
    ppermute x1, waiting for transfers between devices: 0.01 us -> 2.82 us  [shards(): second = lax.ppermute(previous, 'surf', odd)]
    pallas_call x6 -> x7, Pallas kernels: 9.47 us -> 7.39 us  [the longest x1 2.53 us: shards(): call(maps_kernel, [f32(rows, cells, 2 * high, LANES), f32(rows, 3, high,...]
    ppermute x4 -> x6, starting transfers between devices: 3.28 us -> 4.13 us  [shards(): lax.ppermute(a, 'line', [(i, i ^ 1 << k) for i in range(count)])]
  transfers between devices with their start and end apart: 6 -> 8, of which waited for: 4 -> 5; matrix products, arithmetic and copies ran while one was open for 5% -> 1% of each run, Pallas kernels for 8% -> 6%
where the time goes in v2:
time: 30.4 us; the launch traced here: 30.2 us
  waiting for transfers between devices  11.4 us (38%)
  starting transfers between devices  9.26 us (30%)
  Pallas kernels  7.39 us (24%)
  local copies, waits for them, and re-layouts  2.05 us (7%)
    ppermute x6, waiting for transfers between devices, shards(): lax.ppermute(a, 'line', [(i, i ^ 1 << k) for i in range(count)])  8.59 us
    ppermute x6, starting transfers between devices, shards(): lax.ppermute(a, 'line', [(i, i ^ 1 << k) for i in range(count)])  4.13 us
    ppermute x1, waiting for transfers between devices, shards(): second = lax.ppermute(previous, 'surf', odd)  2.82 us
    ppermute x1, starting transfers between devices, shards(): first = lax.ppermute(previous, 'surf', pairs)  2.65 us
    pallas_call x1, Pallas kernels, shards(): call(maps_kernel, [f32(rows, cells, 2 * high, LANES), f32(rows, 3, high,...  2.53 us
    ppermute x1, starting transfers between devices, shards(): second = lax.ppermute(previous, 'surf', odd)  2.47 us
    unnamed x15, local copies, waits for them, and re-layouts  2.05 us
    pallas_call x1, Pallas kernels, shards(): call(final_kernel, [f32(rows, cells, width)], [VMEM] * 6)  1.46 us
  transfers between devices with their start and end apart: 8, of which 5 were waited for; matrix products, arithmetic and copies ran while one was open for 1% of the time, Pallas kernels for 6%

profile of v2, /device:TPU:0, one launch (start us, length us, event | category | flops | bytes accessed | tf_op | source)
XLA Modules:
  0.0 30.2 jit_solution(15439847158862197427)
XLA Ops:
  0.0 0.0 copy-start.4
  0.0 1.6 %copy.8.lower = bf16[2,8,135,135]{3,2,1,0:T(8,128)(2,1)S(1)} copy(bf16[2,8,135,135]{3,1,2,0:T(8,128)(2,1)} %param.12) | data formatting | bytes 1166400 | tf_op args[5]
  1.6 0.0 copy-done.4
  1.6 0.2 copy.9.upper
  1.8 0.0 copy-start.2
  1.8 0.0 copy-start.5
  1.8 2.5 %shard_map.73 = (f32[2,8,272,256]{3,2,1,0:T(8,128)S(1)}, f32[2,3,136,256]{3,2,1,0:T(8,128)S(1)}, f32[3,136,256]{2,1,0:T(8,128)S(1)}, f32[3,136,256]{2,1,0:T(8,128)S(1)}) custom-call(bf16[2,8,135,135]{3,2,1,0:T(8,128)(2,1)S(1)} %copy.8.lower, bf16[2,8,135,135]{3,2,1,0:T(8,128)(2,1)S(1)} %copy.9.upper), custom_call_target="tpu_custom_call" | custom-call | tf_op jit(solution)/shard_map/pallas_call | solution.py:351
  4.4 0.0 copy-start
  4.4 0.0 copy-start.1
  4.4 0.0 copy-start.3
  4.4 0.5 %collective-permute-start = (f32[3,136,256]{2,1,0:T(8,128)S(1)}, f32[3,136,256]{2,1,0:T(8,128)S(1)}, u32[]{:S(2)}, u32[]{:S(2)}) collective-permute-start(f32[3,136,256]{2,1,0:T(8,128)S(1)} %get-tuple-element.25), channel_id=1, source_target_pairs={{0,4},{4,0},{8,12},{12,8},{16,20},{20,16},{24,28},{28,24},{1,5},{5... | collective-permute-start | bytes 1253384 | tf_op jit(solution)/shard_map/ppermute | solution.py:346
  4.9 0.0 copy-done.2
  4.9 2.7 %collective-permute-start.1 = (f32[2,8,135]{2,1,0:T(8,128)S(1)}, f32[2,8,135]{2,1,0:T(8,128)S(1)}, u32[]{:S(2)}, u32[]{:S(2)}) collective-permute-start(f32[2,8,135]{2,1,0:T(8,128)S(1)} %copy-done.2), channel_id=1, source_target_pairs={{0,1},{1,0},{2,3},{3,2},{4,5},{5,4},{6,7},{7,6},{8,9},{9,8},{10,11... | collective-permute-start | bytes 25928 | tf_op jit(solution)/shard_map/ppermute | solution.py:348
  7.6 2.5 %collective-permute-start.2 = (f32[2,8,135]{2,1,0:T(8,128)S(1)}, f32[2,8,135]{2,1,0:T(8,128)S(1)}, u32[]{:S(2)}, u32[]{:S(2)}) collective-permute-start(f32[2,8,135]{2,1,0:T(8,128)S(1)} %copy-done.2), channel_id=1, source_target_pairs={{0,3},{1,2},{2,1},{3,0},{4,7},{5,6},{6,5},{7,4},{8,11},{9,10},{10,... | collective-permute-start | bytes 25928 | tf_op jit(solution)/shard_map/ppermute | solution.py:347
  10.0 0.0 copy-done.5
  10.1 0.2 copy.10.pivots
  10.3 0.0 collective-permute-done.1.first
  10.3 2.8 %collective-permute-done.2.second = f32[2,8,135]{2,1,0:T(8,128)S(1)} collective-permute-done((f32[2,8,135]{2,1,0:T(8,128)S(1)}, f32[2,8,135]{2,1,0:T(8,128)S(1)}, u32[]{:S(2)}, u32[]{:S(2)}) %collective-permute-start.2) | collective-permute-done | bytes 8672 | tf_op jit(solution)/shard_map/ppermute | solution.py:347
  13.1 0.0 copy-done
  13.1 0.0 copy-done.1
  13.1 0.0 copy-done.3
  13.1 1.4 %shard_map.74 = (f32[2,8,135]{2,1,0:T(8,128)S(1)}, f32[2,2,8,256]{3,2,1,0:T(8,128)S(1)}, f32[8,256]{1,0:T(8,128)S(1)}, f32[8,256]{1,0:T(8,128)S(1)}) custom-call(s32[2,4]{1,0:T(2,128)S(1)} %copy-done.3, f32[2,8,135]{2,1,0:T(8,128)S(1)} %copy-done.1, f32[2,8,135]{2,1,0:T(8,128)S(1)} %copy-done.2, f32[2,8,135]{2,1,0:T(8,128)S(1)} %collective-permute-done.1.first, ...), custom_call_target="tpu_custom_call" | custom-call | tf_op jit(solution)/shard_map/pallas_call | solution.py:357
  14.6 0.0 collective-permute-done.theirs
  14.6 0.6 %shard_map.75 = (f32[6,136,256]{2,1,0:T(8,128)S(1)}, f32[3,136,256]{2,1,0:T(8,128)S(1)}, f32[456,128]{1,0:T(8,128)S(1)}) custom-call(f32[3,136,256]{2,1,0:T(8,128)S(1)} %get-tuple-element.24.mine, f32[3,136,256]{2,1,0:T(8,128)S(1)} %collective-permute-done.theirs, f32[8,256]{1,0:T(8,128)S(1)} %get-tuple-element.28.after.mine), custom_call_target="tpu_custom_call" | custom-call | tf_op jit(solution)/shard_map/pallas_call | solution.py:366
  15.2 1.5 %collective-permute-start.3 = (f32[456,128]{1,0:T(8,128)S(1)}, f32[456,128]{1,0:T(8,128)S(1)}, u32[]{:S(2)}, u32[]{:S(2)}) collective-permute-start(f32[456,128]{1,0:T(8,128)S(1)} %get-tuple-element.30), channel_id=1, source_target_pairs={{0,8},{4,12},{8,0},{12,4},{16,24},{20,28},{24,16},{28,20},{1,9},{5... | collective-permute-start | bytes 700424 | tf_op jit(solution)/shard_map/ppermute | solution.py:346
  16.7 0.0 collective-permute-start.4
  16.7 1.2 %collective-permute-done.4.theirs = f32[8,256]{1,0:T(8,128)S(1)} collective-permute-done((f32[8,256]{1,0:T(8,128)S(1)}, f32[8,256]{1,0:T(8,128)S(1)}, u32[]{:S(2)}, u32[]{:S(2)}) %collective-permute-start.4) | collective-permute-done | bytes 8224 | tf_op jit(solution)/shard_map/ppermute | solution.py:346
  17.9 0.3 shard_map.76
  18.2 0.5 %collective-permute-start.5 = (f32[8,256]{1,0:T(8,128)S(1)}, f32[8,256]{1,0:T(8,128)S(1)}, u32[]{:S(2)}, u32[]{:S(2)}) collective-permute-start(f32[8,256]{1,0:T(8,128)S(1)} %get-tuple-element.33.vectors), channel_id=1, source_target_pairs={{0,8},{4,12},{8,0},{12,4},{16,24},{20,28},{24,16},{28,20},{1,9},{5... | collective-permute-start | bytes 24584 | tf_op jit(solution)/shard_map/ppermute | solution.py:346
  18.7 3.3 %collective-permute-done.5.others = f32[8,256]{1,0:T(8,128)S(1)} collective-permute-done((f32[8,256]{1,0:T(8,128)S(1)}, f32[8,256]{1,0:T(8,128)S(1)}, u32[]{:S(2)}, u32[]{:S(2)}) %collective-permute-start.5) | collective-permute-done | bytes 8224 | tf_op jit(solution)/shard_map/ppermute | solution.py:346
  22.0 0.0 collective-permute-done.3.theirs
  22.0 0.6 %shard_map.77 = (f32[3,136,256]{2,1,0:T(8,128)S(1)}, f32[1,136,256]{2,1,0:T(8,128)S(1)}, f32[2,8,256]{2,1,0:T(8,128)S(1)}, f32[160,128]{1,0:T(8,128)S(1)}) custom-call(f32[3,136,256]{2,1,0:T(8,128)S(1)} %get-tuple-element.29.mine, f32[456,128]{1,0:T(8,128)S(1)} %collective-permute-done.3.theirs, f32[8,256]{1,0:T(8,128)S(1)} %get-tuple-element.33.vectors, ...), custom_call_target="tpu_custom_call" | custom-call | tf_op jit(solution)/shard_map/pallas_call | solution.py:381
  22.6 1.5 %collective-permute-start.6 = (f32[160,128]{1,0:T(8,128)S(1)}, f32[160,128]{1,0:T(8,128)S(1)}, u32[]{:S(2)}, u32[]{:S(2)}) collective-permute-start(f32[160,128]{1,0:T(8,128)S(1)} %get-tuple-element.35), channel_id=1, source_target_pairs={{0,16},{4,20},{8,24},{12,28},{16,0},{20,4},{24,8},{28,12},{1,17},{... | collective-permute-start | bytes 245768 | tf_op jit(solution)/shard_map/ppermute | solution.py:346
  24.2 2.9 %collective-permute-done.6.refs_1_ = f32[160,128]{1,0:T(8,128)S(1)} collective-permute-done((f32[160,128]{1,0:T(8,128)S(1)}, f32[160,128]{1,0:T(8,128)S(1)}, u32[]{:S(2)}, u32[]{:S(2)}) %collective-permute-start.6) | collective-permute-done | bytes 81952 | tf_op jit(solution)/shard_map/ppermute | solution.py:346
  27.1 0.5 %shard_map.78 = (f32[2,8,256]{2,1,0:T(8,128)S(1)}, f32[2,8,256]{2,1,0:T(8,128)S(1)}) custom-call(f32[1,136,256]{2,1,0:T(8,128)S(1)} %get-tuple-element.34.refs_0_, f32[160,128]{1,0:T(8,128)S(1)} %collective-permute-done.6.refs_1_, f32[6,136,256]{2,1,0:T(8,128)S(1)} %get-tuple-element.31.down.refs_2_, f32[3,136,256]{2,1,0:T(8,128)S(1)} %get-tuple-element.36.refs_3_, ...), custom_call_target="tpu_custom_call" | custom-call | tf_op jit(solution)/shard_map/pallas_call | solution.py:393
  27.5 0.0 collective-permute-start.7
  27.6 1.2 %collective-permute-done.7.theirs = f32[2,8,256]{2,1,0:T(8,128)S(1)} collective-permute-done((f32[2,8,256]{2,1,0:T(8,128)S(1)}, f32[2,8,256]{2,1,0:T(8,128)S(1)}, u32[]{:S(2)}, u32[]{:S(2)}) %collective-permute-start.7) | collective-permute-done | bytes 16416 | tf_op jit(solution)/shard_map/ppermute | solution.py:346
  28.7 1.5 %shard_map.79 = f32[2,8,135]{2,1,0:T(8,128)} custom-call(f32[2,8,256]{2,1,0:T(8,128)S(1)} %get-tuple-element.39.mine, f32[2,8,256]{2,1,0:T(8,128)S(1)} %collective-permute-done.7.theirs, f32[2,8,135]{2,1,0:T(8,128)S(1)} %get-tuple-element.41.inner, f32[2,8,272,256]{3,2,1,0:T(8,128)S(1)} %get-tuple-element.26.tail, ...), custom_call_target="tpu_custom_call" | custom-call | tf_op jit(solution)/shard_map/pallas_call | solution.py:398
Async XLA Ops:
  0.0 1.6 %copy-start.4 = (bf16[2,8,135,135]{3,1,2,0:T(8,128)(2,1)S(1)}, bf16[2,8,135,135]{3,1,2,0:T(8,128)(2,1)}, u32[]{:S(2)}) copy-start(bf16[2,8,135,135]{3,1,2,0:T(8,128)(2,1)} %param.13) | copy-start | bytes 1749604
  1.8 3.1 %copy-start.2 = (f32[2,8,135]{2,1,0:T(8,128)S(1)}, f32[2,8,135]{2,1,0:T(8,128)}, u32[]{:S(2)}) copy-start(f32[2,8,135]{2,1,0:T(8,128)} %own.1) | copy-start | bytes 25924
  1.8 8.2 %copy-start.5 = (bf16[2,8,135,135]{3,1,2,0:T(8,128)(2,1)S(1)}, bf16[2,8,135,135]{3,1,2,0:T(8,128)(2,1)}, u32[]{:S(2)}) copy-start(bf16[2,8,135,135]{3,1,2,0:T(8,128)(2,1)} %param.11) | copy-start | bytes 1749604
  4.4 8.8 %copy-start = (f32[2,8,4,135]{3,2,1,0:T(4,128)S(1)}, f32[2,8,4,135]{3,2,1,0:T(4,128)}, u32[]{:S(2)}) copy-start(f32[2,8,4,135]{3,2,1,0:T(4,128)} %coupling.1) | copy-start | bytes 103684
  4.4 8.7 %copy-start.1 = (f32[2,8,135]{2,1,0:T(8,128)S(1)}, f32[2,8,135]{2,1,0:T(8,128)}, u32[]{:S(2)}) copy-start(f32[2,8,135]{2,1,0:T(8,128)} %right.1) | copy-start | bytes 25924
  4.4 8.7 %copy-start.3 = (s32[2,4]{1,0:T(2,128)S(1)}, s32[2,4]{1,0:T(2,128)}, u32[]{:S(2)}) copy-start(s32[2,4]{1,0:T(2,128)} %neighbours.1) | copy-start | bytes 100
  4.4 10.2 %collective-permute-start = (f32[3,136,256]{2,1,0:T(8,128)S(1)}, f32[3,136,256]{2,1,0:T(8,128)S(1)}, u32[]{:S(2)}, u32[]{:S(2)}) collective-permute-start(f32[3,136,256]{2,1,0:T(8,128)S(1)} %get-tuple-element.25), channel_id=1, source_target_pairs={{0,4},{4,0},{8,12},{12,8},{16,20},{20,16},{24,28},{28,24},{1,5},{5... | collective-permute-start | bytes 1253384 | tf_op jit(solution)/shard_map/ppermute | solution.py:346
  4.9 5.4 %collective-permute-start.1 = (f32[2,8,135]{2,1,0:T(8,128)S(1)}, f32[2,8,135]{2,1,0:T(8,128)S(1)}, u32[]{:S(2)}, u32[]{:S(2)}) collective-permute-start(f32[2,8,135]{2,1,0:T(8,128)S(1)} %copy-done.2), channel_id=1, source_target_pairs={{0,1},{1,0},{2,3},{3,2},{4,5},{5,4},{6,7},{7,6},{8,9},{9,8},{10,11... | collective-permute-start | bytes 25928 | tf_op jit(solution)/shard_map/ppermute | solution.py:348
  7.6 5.5 %collective-permute-start.2 = (f32[2,8,135]{2,1,0:T(8,128)S(1)}, f32[2,8,135]{2,1,0:T(8,128)S(1)}, u32[]{:S(2)}, u32[]{:S(2)}) collective-permute-start(f32[2,8,135]{2,1,0:T(8,128)S(1)} %copy-done.2), channel_id=1, source_target_pairs={{0,3},{1,2},{2,1},{3,0},{4,7},{5,6},{6,5},{7,4},{8,11},{9,10},{10,... | collective-permute-start | bytes 25928 | tf_op jit(solution)/shard_map/ppermute | solution.py:347
  15.2 6.8 %collective-permute-start.3 = (f32[456,128]{1,0:T(8,128)S(1)}, f32[456,128]{1,0:T(8,128)S(1)}, u32[]{:S(2)}, u32[]{:S(2)}) collective-permute-start(f32[456,128]{1,0:T(8,128)S(1)} %get-tuple-element.30), channel_id=1, source_target_pairs={{0,8},{4,12},{8,0},{12,4},{16,24},{20,28},{24,16},{28,20},{1,9},{5... | collective-permute-start | bytes 700424 | tf_op jit(solution)/shard_map/ppermute | solution.py:346
  16.7 1.2 %collective-permute-start.4 = (f32[8,256]{1,0:T(8,128)S(1)}, f32[8,256]{1,0:T(8,128)S(1)}, u32[]{:S(2)}, u32[]{:S(2)}) collective-permute-start(f32[8,256]{1,0:T(8,128)S(1)} %get-tuple-element.32), channel_id=1, source_target_pairs={{0,4},{4,0},{8,12},{12,8},{16,20},{20,16},{24,28},{28,24},{1,5},{5... | collective-permute-start | bytes 24584 | tf_op jit(solution)/shard_map/ppermute | solution.py:346
  18.2 3.9 %collective-permute-start.5 = (f32[8,256]{1,0:T(8,128)S(1)}, f32[8,256]{1,0:T(8,128)S(1)}, u32[]{:S(2)}, u32[]{:S(2)}) collective-permute-start(f32[8,256]{1,0:T(8,128)S(1)} %get-tuple-element.33.vectors), channel_id=1, source_target_pairs={{0,8},{4,12},{8,0},{12,4},{16,24},{20,28},{24,16},{28,20},{1,9},{5... | collective-permute-start | bytes 24584 | tf_op jit(solution)/shard_map/ppermute | solution.py:346
  22.6 4.4 %collective-permute-start.6 = (f32[160,128]{1,0:T(8,128)S(1)}, f32[160,128]{1,0:T(8,128)S(1)}, u32[]{:S(2)}, u32[]{:S(2)}) collective-permute-start(f32[160,128]{1,0:T(8,128)S(1)} %get-tuple-element.35), channel_id=1, source_target_pairs={{0,16},{4,20},{8,24},{12,28},{16,0},{20,4},{24,8},{28,12},{1,17},{... | collective-permute-start | bytes 245768 | tf_op jit(solution)/shard_map/ppermute | solution.py:346
  27.5 1.2 %collective-permute-start.7 = (f32[2,8,256]{2,1,0:T(8,128)S(1)}, f32[2,8,256]{2,1,0:T(8,128)S(1)}, u32[]{:S(2)}, u32[]{:S(2)}) collective-permute-start(f32[2,8,256]{2,1,0:T(8,128)S(1)} %get-tuple-element.40), channel_id=1, source_target_pairs={{0,4},{4,0},{8,12},{12,8},{16,20},{20,16},{24,28},{28,24},{1,5},{5... | collective-permute-start | bytes 49160 | tf_op jit(solution)/shard_map/ppermute | solution.py:346

commit v3 on v2

--- a/solution.py
+++ b/solution.py
@@ -58,44 +58,59 @@
     return jnp.concatenate([p[:high], right], axis=1)
 
 
-def maps_kernel(lower, upper, tail, half, keep, send):
+def unit_kernel(out):
+    out[...] = (
+        lax.broadcasted_iota(jnp.int32, out.shape, 0) == lax.broadcasted_iota(jnp.int32, out.shape, 1)
+    ).astype(BF16)
+
+
+def ahead_kernel(unit, lower, ahead):
     rows, cells, width, _ = lower.shape
+    per = cells // 2
+    eye = unit[...]
+    now = {}
+    for j in range(per):
+        for l in range(rows):
+            for p in range(2):
+                block = lower[l, p * per + j]
+                if j > 1:
+                    now[l, p] = times_block(now[l, p], block)
+                else:
+                    now[l, p] = dot_nt(now[l, p].astype(BF16) if j else eye, block)
+                ahead[l, p * per + j, :, :width] = now[l, p]
+
+
+def maps_kernel(unit, ahead, upper, tail, half, keep, send):
+    rows, cells, width, _ = upper.shape
     high = keep.shape[1]
     per = cells // 2
     core = side(0)
-    eye = (
-        lax.broadcasted_iota(jnp.int32, (high, width), 0)
-        == lax.broadcasted_iota(jnp.int32, (high, width), 1)
-    ).astype(BF16)
+    eye = unit[...]
     blank = jnp.zeros((high, LANES - 128), F32)
     for k in range(3):
         keep[k, :, 128:] = blank
         send[k, :, 128:] = blank
         for l in range(rows):
             half[l, k, :, 128:] = blank
-    chains = [(l, p) for l in range(rows) for p in range(2)]
-    ahead = {}
-    for j in range(per):
-        for l, p in chains:
-            i = p * per + j
-            block = lower[l, i]
-            ahead[l, p] = times_block(ahead[l, p], block) if j else dot_nt(eye, block)
-            tail[l, i, :high, :width] = ahead[l, p]
     back = {}
     for j in reversed(range(per)):
-        for l, p in chains:
-            i = p * per + j
-            if j == per - 1:
-                back[l, p] = jnp.concatenate([ahead[l, p], dot_nt(eye, upper[l, i])], axis=0)
-            else:
-                both = times_block(back[l, p], upper[l, i])
-                front = tail[l, i, :high, :width] + both[:high]
-                back[l, p] = jnp.concatenate([front, both[high:]], axis=0)
-                tail[l, i, :high, :width] = front
-            tail[l, i, high:, :width] = back[l, p][high:]
+        for l in range(rows):
+            for p in range(2):
+                i = p * per + j
+                if j == per - 1:
+                    now = jnp.concatenate(
+                        [ahead[l, i, :, :width], dot_nt(eye, upper[l, i])], axis=0
+                    )
+                else:
+                    both = times_block(back[l, p], upper[l, i])
+                    now = jnp.concatenate(
+                        [ahead[l, i, :, :width] + both[:high], both[high:]], axis=0
+                    )
+                back[l, p] = now
+                tail[l, i, :, :width] = now
     joint = []
     for l in range(rows):
-        f = ahead[l, 0], ahead[l, 1]
+        f = [ahead[l, p * per + per - 1, :, :width] for p in range(2)]
         g = back[l, 0][:high], back[l, 1][:high]
         b = back[l, 0][high:], back[l, 1][high:]
         inward = times_map(f[0], g[1][:width])
@@ -110,7 +125,7 @@
 
 def segment_kernel(
     patches, neighbours, right, own, first, second, coupling, pivots, lower, upper,
-    tail, half, inner, bias, keep, send, pad,
+    tail, half, after, inner, bias, keep, send, pad,
 ):
     rows, cells, width = right.shape
     high = half.shape[2]
@@ -195,7 +210,7 @@
     return times_map(f[0][:, :high], f_right) + f[1], g[0] + times_map(between[:, :high], b_left), between
 
 
-def first_maps_kernel(mine, theirs, after, down, full, pack):
+def first_maps_kernel(mine, theirs, down, full, pack):
     s = side(0)
     f, g, b = (ordered(s, mine[k], theirs[k]) for k in range(3))
     joint, inward = merged_maps(f, g, b, False)
@@ -319,13 +334,14 @@
                     out[l, i : i + 1, at] = inner[l, i : i + 1, at] + r[:, : at.stop - at.start]
 
 
-def call(body, outs, specs, scratch=()):
+def call(body, outs, specs, scratch=(), flops=None):
     return pl.pallas_call(
         body,
         out_shape=outs,
         in_specs=specs,
         out_specs=jax.tree.map(lambda _: VMEM, outs),
         scratch_shapes=scratch,
+        cost_estimate=flops and pl.CostEstimate(flops=flops, bytes_accessed=0, transcendentals=0),
         compiler_params=pltpu.CompilerParams(vmem_limit_bytes=LIMIT),
     )
 
@@ -348,27 +364,36 @@
     first = lax.ppermute(previous, "surf", pairs)
     full = f32(3, high, LANES)
     row = f32(8, LANES)
+    unit = call(unit_kernel, [jax.ShapeDtypeStruct((high, width), BF16)], [], flops=2000000000)()[0]
+    unit, lower_factor = lax.optimization_barrier((unit, lower_factor))
+    ahead = call(ahead_kernel, [f32(rows, cells, high, LANES)], [VMEM] * 2, flops=12000000000)(
+        unit, lower_factor
+    )[0]
+    ahead, upper_factor, pivots = lax.optimization_barrier((ahead, upper_factor, pivots))
     tail, half, keep, send = call(
         maps_kernel,
         [f32(rows, cells, 2 * high, LANES), f32(rows, 3, high, LANES), full, full],
+        [VMEM] * 3,
+        flops=12000000000,
+    )(unit, ahead, upper_factor)
+    send, first = lax.optimization_barrier((send, first))
+    theirs = swap(send, 0)
+    down, mine, pack = call(
+        first_maps_kernel,
+        [f32(6, high, LANES), full, f32(3 * size, 128)],
         [VMEM] * 2,
-    )(lower_factor, upper_factor)
-    theirs = swap(send, 0)
+    )(keep, theirs)
+    theirs = swap(pack, 1)
     inner, ends, vkeep, vsend = call(
         functools.partial(segment_kernel, patches),
         [f32(rows, cells, width), f32(rows, 2, 8, LANES), row, row],
-        [VMEM] * 11,
+        [VMEM] * 12,
         [pltpu.VMEM((rows, 4, 8, LANES), F32)],
+        50000000000,
     )(
         neighbours, right_side, previous, first, second, coupling, pivots,
-        lower_factor, upper_factor, tail, half,
+        lower_factor, upper_factor, tail, half, pack,
     )
-    down, mine, pack = call(
-        first_maps_kernel,
-        [f32(6, high, LANES), full, f32(3 * size, 128)],
-        [VMEM] * 3,
-    )(keep, theirs, vkeep)
-    theirs = swap(pack, 1)
     vtheirs = swap(vsend, 0)
     vectors, bias = call(
         first_vectors_kernel, [row, f32(2, 8, LANES)], [VMEM] * 3

time: 30.4 us -> 27.4 us (0.901)
  waiting for transfers between devices: 11.4 us -> 7.54 us
  starting transfers between devices: 9.26 us -> 10.9 us
  local copies, waits for them, and re-layouts: 2.05 us -> 1.2 us
    ppermute x1, waiting for transfers between devices: 2.82 us -> 0.01 us  [shards(): second = lax.ppermute(previous, 'surf', odd)]
    unnamed x15 -> x14, local copies, waits for them, and re-layouts: 2.05 us -> 0.53 us
    ppermute x6, waiting for transfers between devices: 8.59 us -> 7.54 us  [shards(): lax.ppermute(a, 'line', [(i, i ^ 1 << k) for i in range(count)])]
    ppermute x1, starting transfers between devices: 2.47 us -> 3.31 us  [shards(): second = lax.ppermute(previous, 'surf', odd)]
    pallas_call x0 -> x2, Pallas kernels: none -> 0.75 us  [the longest x1 0.73 us: shards(): call(ahead_kernel, [f32(rows, cells, high, LANES)], [VMEM] * 2, flops=120...]
    optimization_barrier x0 -> x3, local copies, waits for them, and re-layouts: none -> 0.67 us  [the longest x2 0.44 us: shards(): lax.optimization_barrier((ahead, upper_factor, pivots))]
    pallas_call x1, Pallas kernels: 2.53 us -> 1.87 us  [shards(): call(maps_kernel, [f32(rows, cells, 2 * high, LANES), f32(rows, 3, high,...]
    ppermute x6, starting transfers between devices: 4.13 us -> 4.53 us  [shards(): lax.ppermute(a, 'line', [(i, i ^ 1 << k) for i in range(count)])]
  transfers between devices with their start and end apart: 8 -> 8, of which waited for: 5 -> 4; matrix products, arithmetic and copies ran while one was open for 1% -> 2% of each run, Pallas kernels for 6% -> 18%
where the time goes in v3:
time: 27.4 us; the launch traced here: 27.2 us
  starting transfers between devices  10.9 us (40%)
  waiting for transfers between devices  7.54 us (28%)
  Pallas kernels  7.48 us (27%)
  local copies, waits for them, and re-layouts  1.2 us (4%)
    ppermute x6, waiting for transfers between devices, shards(): lax.ppermute(a, 'line', [(i, i ^ 1 << k) for i in range(count)])  7.54 us
    ppermute x6, starting transfers between devices, shards(): lax.ppermute(a, 'line', [(i, i ^ 1 << k) for i in range(count)])  4.53 us
    ppermute x1, starting transfers between devices, shards(): second = lax.ppermute(previous, 'surf', odd)  3.31 us
    ppermute x1, starting transfers between devices, shards(): first = lax.ppermute(previous, 'surf', pairs)  3.02 us
    pallas_call x1, Pallas kernels, shards(): call(maps_kernel, [f32(rows, cells, 2 * high, LANES), f32(rows, 3, high,...  1.87 us
    pallas_call x1, Pallas kernels, shards(): call(final_kernel, [f32(rows, cells, width)], [VMEM] * 6)  1.47 us
    pallas_call x1, Pallas kernels, shards(): call(functools.partial(segment_kernel, patches), [f32(rows, cells, width)...  1.43 us
    pallas_call x1, Pallas kernels, shards(): call(ahead_kernel, [f32(rows, cells, high, LANES)], [VMEM] * 2, flops=120...  0.73 us
  transfers between devices with their start and end apart: 8, of which 4 were waited for; matrix products, arithmetic and copies ran while one was open for 2% of the time, Pallas kernels for 18%

profile of v3, /device:TPU:0, one launch (start us, length us, event | category | flops | bytes accessed | tf_op | source)
XLA Modules:
  0.0 27.2 jit_solution(12134738141201373064)
XLA Ops:
  0.0 0.0 copy-start.4
  0.0 3.0 %collective-permute-start = (f32[2,8,135]{2,1,0:T(8,128)}, f32[2,8,135]{2,1,0:T(8,128)S(1)}, u32[]{:S(2)}, u32[]{:S(2)}) collective-permute-start(f32[2,8,135]{2,1,0:T(8,128)} %own.1), channel_id=1, source_target_pairs={{0,1},{1,0},{2,3},{3,2},{4,5},{5,4},{6,7},{7,6},{8,9},{9,8},{10,11... | collective-permute-start | bytes 25928 | tf_op jit(solution)/shard_map/ppermute | solution.py:364
  3.0 0.0 copy-done.4
  3.1 0.2 copy.8.lower
  3.3 0.0 copy-start.5
  3.3 0.7 %shard_map.74.ahead = f32[2,8,136,256]{3,2,1,0:T(8,128)S(1)} custom-call(bf16[136,135]{1,0:T(8,128)(2,1)S(1)} %shard_map.73.unit, bf16[2,8,135,135]{3,2,1,0:T(8,128)(2,1)S(1)} %copy.8.lower), custom_call_target="tpu_custom_call" | custom-call | flops 12000000000 | tf_op jit(solution)/shard_map/pallas_call | solution.py:369
  4.0 0.5 %copy-done.5 = bf16[2,8,135,135]{3,1,2,0:T(8,128)(2,1)S(1)} copy-done((bf16[2,8,135,135]{3,1,2,0:T(8,128)(2,1)S(1)}, bf16[2,8,135,135]{3,1,2,0:T(8,128)(2,1)}, u32[]{:S(2)}) %copy-start.5) | copy-done | bytes 583224
  4.5 0.2 copy.9.upper
  4.8 0.0 copy-start.2
  4.8 0.0 copy-start.6
  4.8 1.9 %shard_map.75 = (f32[2,8,272,256]{3,2,1,0:T(8,128)S(1)}, f32[2,3,136,256]{3,2,1,0:T(8,128)S(1)}, f32[3,136,256]{2,1,0:T(8,128)S(1)}, f32[3,136,256]{2,1,0:T(8,128)S(1)}) custom-call(bf16[136,135]{1,0:T(8,128)(2,1)S(1)} %shard_map.73.unit, f32[2,8,136,256]{3,2,1,0:T(8,128)S(1)} %shard_map.74.ahead, bf16[2,8,135,135]{3,2,1,0:T(8,128)(2,1)S(1)} %copy.9.upper), custom_call_target="tpu_custom_call" | custom-call | flops 12000000000 | tf_op jit(solution)/shard_map/pallas_call | solution.py:373
  6.7 0.0 collective-permute-done.first
  6.7 0.0 copy-start
  6.7 0.0 copy-start.1
  6.7 0.0 copy-start.3
  6.7 0.1 collective-permute-start.1
  6.8 0.0 copy-done.2
  6.8 3.3 %collective-permute-start.3 = (f32[2,8,135]{2,1,0:T(8,128)S(1)}, f32[2,8,135]{2,1,0:T(8,128)S(1)}, u32[]{:S(2)}, u32[]{:S(2)}) collective-permute-start(f32[2,8,135]{2,1,0:T(8,128)S(1)} %copy-done.2), channel_id=1, source_target_pairs={{0,3},{1,2},{2,1},{3,0},{4,7},{5,6},{6,5},{7,4},{8,11},{9,10},{10,... | collective-permute-start | bytes 25928 | tf_op jit(solution)/shard_map/ppermute | solution.py:363
  10.1 0.0 copy-done.6
  10.1 0.2 copy.10.pivots
  10.3 0.0 collective-permute-done.1.theirs
  10.3 0.6 %shard_map.76 = (f32[6,136,256]{2,1,0:T(8,128)S(1)}, f32[3,136,256]{2,1,0:T(8,128)S(1)}, f32[456,128]{1,0:T(8,128)S(1)}) custom-call(f32[3,136,256]{2,1,0:T(8,128)S(1)} %get-tuple-element.35.mine, f32[3,136,256]{2,1,0:T(8,128)S(1)} %collective-permute-done.1.theirs), custom_call_target="tpu_custom_call" | custom-call | tf_op jit(solution)/shard_map/pallas_call | solution.py:381
  11.0 1.5 %collective-permute-start.2 = (f32[456,128]{1,0:T(8,128)S(1)}, f32[456,128]{1,0:T(8,128)S(1)}, u32[]{:S(2)}, u32[]{:S(2)}) collective-permute-start(f32[456,128]{1,0:T(8,128)S(1)} %get-tuple-element.39.after), channel_id=1, source_target_pairs={{0,8},{4,12},{8,0},{12,4},{16,24},{20,28},{24,16},{28,20},{1,9},{5... | collective-permute-start | bytes 700424 | tf_op jit(solution)/shard_map/ppermute | solution.py:362
  12.5 0.0 collective-permute-done.3.second
  12.5 0.0 copy-done
  12.5 0.0 copy-done.1
  12.5 0.0 copy-done.3
  12.5 1.4 %shard_map.77 = (f32[2,8,135]{2,1,0:T(8,128)S(1)}, f32[2,2,8,256]{3,2,1,0:T(8,128)S(1)}, f32[8,256]{1,0:T(8,128)S(1)}, f32[8,256]{1,0:T(8,128)S(1)}) custom-call(s32[2,4]{1,0:T(2,128)S(1)} %copy-done.3, f32[2,8,135]{2,1,0:T(8,128)S(1)} %copy-done.1, f32[2,8,135]{2,1,0:T(8,128)S(1)} %copy-done.2, f32[2,8,135]{2,1,0:T(8,128)S(1)} %collective-permute-done.first, ...), custom_call_target="tpu_custom_call" | custom-call | flops 49999998976 | tf_op jit(solution)/shard_map/pallas_call | solution.py:387
  13.9 0.0 collective-permute-start.4
  14.0 1.2 %collective-permute-done.4.theirs = f32[8,256]{1,0:T(8,128)S(1)} collective-permute-done((f32[8,256]{1,0:T(8,128)S(1)}, f32[8,256]{1,0:T(8,128)S(1)}, u32[]{:S(2)}, u32[]{:S(2)}) %collective-permute-start.4) | collective-permute-done | bytes 8224 | tf_op jit(solution)/shard_map/ppermute | solution.py:362
  15.1 0.3 shard_map.78
  15.4 1.4 %collective-permute-start.5 = (f32[8,256]{1,0:T(8,128)S(1)}, f32[8,256]{1,0:T(8,128)S(1)}, u32[]{:S(2)}, u32[]{:S(2)}) collective-permute-start(f32[8,256]{1,0:T(8,128)S(1)} %get-tuple-element.47.vectors), channel_id=1, source_target_pairs={{0,8},{4,12},{8,0},{12,4},{16,24},{20,28},{24,16},{28,20},{1,9},{5... | collective-permute-start | bytes 24584 | tf_op jit(solution)/shard_map/ppermute | solution.py:362
  16.8 2.3 %collective-permute-done.5.others = f32[8,256]{1,0:T(8,128)S(1)} collective-permute-done((f32[8,256]{1,0:T(8,128)S(1)}, f32[8,256]{1,0:T(8,128)S(1)}, u32[]{:S(2)}, u32[]{:S(2)}) %collective-permute-start.5) | collective-permute-done | bytes 8224 | tf_op jit(solution)/shard_map/ppermute | solution.py:362
  19.0 0.0 collective-permute-done.2.theirs
  19.0 0.6 %shard_map.79 = (f32[3,136,256]{2,1,0:T(8,128)S(1)}, f32[1,136,256]{2,1,0:T(8,128)S(1)}, f32[2,8,256]{2,1,0:T(8,128)S(1)}, f32[160,128]{1,0:T(8,128)S(1)}) custom-call(f32[3,136,256]{2,1,0:T(8,128)S(1)} %get-tuple-element.38.mine, f32[456,128]{1,0:T(8,128)S(1)} %collective-permute-done.2.theirs, f32[8,256]{1,0:T(8,128)S(1)} %get-tuple-element.47.vectors, ...), custom_call_target="tpu_custom_call" | custom-call | tf_op jit(solution)/shard_map/pallas_call | solution.py:406
  19.7 1.5 %collective-permute-start.6 = (f32[160,128]{1,0:T(8,128)S(1)}, f32[160,128]{1,0:T(8,128)S(1)}, u32[]{:S(2)}, u32[]{:S(2)}) collective-permute-start(f32[160,128]{1,0:T(8,128)S(1)} %get-tuple-element.49), channel_id=1, source_target_pairs={{0,16},{4,20},{8,24},{12,28},{16,0},{20,4},{24,8},{28,12},{1,17},{... | collective-permute-start | bytes 245768 | tf_op jit(solution)/shard_map/ppermute | solution.py:362
  21.2 2.9 %collective-permute-done.6.refs_1_ = f32[160,128]{1,0:T(8,128)S(1)} collective-permute-done((f32[160,128]{1,0:T(8,128)S(1)}, f32[160,128]{1,0:T(8,128)S(1)}, u32[]{:S(2)}, u32[]{:S(2)}) %collective-permute-start.6) | collective-permute-done | bytes 81952 | tf_op jit(solution)/shard_map/ppermute | solution.py:362
  24.1 0.5 %shard_map.80 = (f32[2,8,256]{2,1,0:T(8,128)S(1)}, f32[2,8,256]{2,1,0:T(8,128)S(1)}) custom-call(f32[1,136,256]{2,1,0:T(8,128)S(1)} %get-tuple-element.48.refs_0_, f32[160,128]{1,0:T(8,128)S(1)} %collective-permute-done.6.refs_1_, f32[6,136,256]{2,1,0:T(8,128)S(1)} %get-tuple-element.40.down.refs_2_, f32[3,136,256]{2,1,0:T(8,128)S(1)} %get-tuple-element.50.refs_3_, ...), custom_call_target="tpu_custom_call" | custom-call | tf_op jit(solution)/shard_map/pallas_call | solution.py:418
  24.6 0.0 collective-permute-start.7
  24.6 1.2 %collective-permute-done.7.theirs = f32[2,8,256]{2,1,0:T(8,128)S(1)} collective-permute-done((f32[2,8,256]{2,1,0:T(8,128)S(1)}, f32[2,8,256]{2,1,0:T(8,128)S(1)}, u32[]{:S(2)}, u32[]{:S(2)}) %collective-permute-start.7) | collective-permute-done | bytes 16416 | tf_op jit(solution)/shard_map/ppermute | solution.py:362
  25.8 1.5 %shard_map.81 = f32[2,8,135]{2,1,0:T(8,128)} custom-call(f32[2,8,256]{2,1,0:T(8,128)S(1)} %get-tuple-element.53.mine, f32[2,8,256]{2,1,0:T(8,128)S(1)} %collective-permute-done.7.theirs, f32[2,8,135]{2,1,0:T(8,128)S(1)} %get-tuple-element.55.inner, f32[2,8,272,256]{3,2,1,0:T(8,128)S(1)} %get-tuple-element.43.tail, ...), custom_call_target="tpu_custom_call" | custom-call | tf_op jit(solution)/shard_map/pallas_call | solution.py:423
  (1 shorter events, 0.0 us)
Async XLA Ops:
  0.0 3.0 %copy-start.4 = (bf16[2,8,135,135]{3,1,2,0:T(8,128)(2,1)S(1)}, bf16[2,8,135,135]{3,1,2,0:T(8,128)(2,1)}, u32[]{:S(2)}) copy-start(bf16[2,8,135,135]{3,1,2,0:T(8,128)(2,1)} %param.12) | copy-start | bytes 1749604
  0.0 6.7 %collective-permute-start = (f32[2,8,135]{2,1,0:T(8,128)}, f32[2,8,135]{2,1,0:T(8,128)S(1)}, u32[]{:S(2)}, u32[]{:S(2)}) collective-permute-start(f32[2,8,135]{2,1,0:T(8,128)} %own.1), channel_id=1, source_target_pairs={{0,1},{1,0},{2,3},{3,2},{4,5},{5,4},{6,7},{7,6},{8,9},{9,8},{10,11... | collective-permute-start | bytes 25928 | tf_op jit(solution)/shard_map/ppermute | solution.py:364
  3.3 1.2 %copy-start.5 = (bf16[2,8,135,135]{3,1,2,0:T(8,128)(2,1)S(1)}, bf16[2,8,135,135]{3,1,2,0:T(8,128)(2,1)}, u32[]{:S(2)}) copy-start(bf16[2,8,135,135]{3,1,2,0:T(8,128)(2,1)} %param.13) | copy-start | bytes 1749604
  4.8 2.0 %copy-start.2 = (f32[2,8,135]{2,1,0:T(8,128)S(1)}, f32[2,8,135]{2,1,0:T(8,128)}, u32[]{:S(2)}) copy-start(f32[2,8,135]{2,1,0:T(8,128)} %own.1) | copy-start | bytes 25924
  4.8 5.3 %copy-start.6 = (bf16[2,8,135,135]{3,1,2,0:T(8,128)(2,1)S(1)}, bf16[2,8,135,135]{3,1,2,0:T(8,128)(2,1)}, u32[]{:S(2)}) copy-start(bf16[2,8,135,135]{3,1,2,0:T(8,128)(2,1)} %param.11) | copy-start | bytes 1749604
  6.7 5.8 %copy-start = (f32[2,8,4,135]{3,2,1,0:T(4,128)S(1)}, f32[2,8,4,135]{3,2,1,0:T(4,128)}, u32[]{:S(2)}) copy-start(f32[2,8,4,135]{3,2,1,0:T(4,128)} %coupling.1) | copy-start | bytes 103684
  6.7 5.8 %copy-start.1 = (f32[2,8,135]{2,1,0:T(8,128)S(1)}, f32[2,8,135]{2,1,0:T(8,128)}, u32[]{:S(2)}) copy-start(f32[2,8,135]{2,1,0:T(8,128)} %right.1) | copy-start | bytes 25924
  6.7 5.8 %copy-start.3 = (s32[2,4]{1,0:T(2,128)S(1)}, s32[2,4]{1,0:T(2,128)}, u32[]{:S(2)}) copy-start(s32[2,4]{1,0:T(2,128)} %neighbours.1) | copy-start | bytes 100
  6.7 3.6 %collective-permute-start.1 = (f32[3,136,256]{2,1,0:T(8,128)S(1)}, f32[3,136,256]{2,1,0:T(8,128)S(1)}, u32[]{:S(2)}, u32[]{:S(2)}) collective-permute-start(f32[3,136,256]{2,1,0:T(8,128)S(1)} %get-tuple-element.37), channel_id=1, source_target_pairs={{0,4},{4,0},{8,12},{12,8},{16,20},{20,16},{24,28},{28,24},{1,5},{5... | collective-permute-start | bytes 1253384 | tf_op jit(solution)/shard_map/ppermute | solution.py:362
  6.8 5.7 %collective-permute-start.3 = (f32[2,8,135]{2,1,0:T(8,128)S(1)}, f32[2,8,135]{2,1,0:T(8,128)S(1)}, u32[]{:S(2)}, u32[]{:S(2)}) collective-permute-start(f32[2,8,135]{2,1,0:T(8,128)S(1)} %copy-done.2), channel_id=1, source_target_pairs={{0,3},{1,2},{2,1},{3,0},{4,7},{5,6},{6,5},{7,4},{8,11},{9,10},{10,... | collective-permute-start | bytes 25928 | tf_op jit(solution)/shard_map/ppermute | solution.py:363
  11.0 8.1 %collective-permute-start.2 = (f32[456,128]{1,0:T(8,128)S(1)}, f32[456,128]{1,0:T(8,128)S(1)}, u32[]{:S(2)}, u32[]{:S(2)}) collective-permute-start(f32[456,128]{1,0:T(8,128)S(1)} %get-tuple-element.39.after), channel_id=1, source_target_pairs={{0,8},{4,12},{8,0},{12,4},{16,24},{20,28},{24,16},{28,20},{1,9},{5... | collective-permute-start | bytes 700424 | tf_op jit(solution)/shard_map/ppermute | solution.py:362
  13.9 1.2 %collective-permute-start.4 = (f32[8,256]{1,0:T(8,128)S(1)}, f32[8,256]{1,0:T(8,128)S(1)}, u32[]{:S(2)}, u32[]{:S(2)}) collective-permute-start(f32[8,256]{1,0:T(8,128)S(1)} %get-tuple-element.46), channel_id=1, source_target_pairs={{0,4},{4,0},{8,12},{12,8},{16,20},{20,16},{24,28},{28,24},{1,5},{5... | collective-permute-start | bytes 24584 | tf_op jit(solution)/shard_map/ppermute | solution.py:362
  15.4 3.7 %collective-permute-start.5 = (f32[8,256]{1,0:T(8,128)S(1)}, f32[8,256]{1,0:T(8,128)S(1)}, u32[]{:S(2)}, u32[]{:S(2)}) collective-permute-start(f32[8,256]{1,0:T(8,128)S(1)} %get-tuple-element.47.vectors), channel_id=1, source_target_pairs={{0,8},{4,12},{8,0},{12,4},{16,24},{20,28},{24,16},{28,20},{1,9},{5... | collective-permute-start | bytes 24584 | tf_op jit(solution)/shard_map/ppermute | solution.py:362
  19.7 4.4 %collective-permute-start.6 = (f32[160,128]{1,0:T(8,128)S(1)}, f32[160,128]{1,0:T(8,128)S(1)}, u32[]{:S(2)}, u32[]{:S(2)}) collective-permute-start(f32[160,128]{1,0:T(8,128)S(1)} %get-tuple-element.49), channel_id=1, source_target_pairs={{0,16},{4,20},{8,24},{12,28},{16,0},{20,4},{24,8},{28,12},{1,17},{... | collective-permute-start | bytes 245768 | tf_op jit(solution)/shard_map/ppermute | solution.py:362
  24.6 1.2 %collective-permute-start.7 = (f32[2,8,256]{2,1,0:T(8,128)S(1)}, f32[2,8,256]{2,1,0:T(8,128)S(1)}, u32[]{:S(2)}, u32[]{:S(2)}) collective-permute-start(f32[2,8,256]{2,1,0:T(8,128)S(1)} %get-tuple-element.54), channel_id=1, source_target_pairs={{0,4},{4,0},{8,12},{12,8},{16,20},{20,16},{24,28},{28,24},{1,5},{5... | collective-permute-start | bytes 49160 | tf_op jit(solution)/shard_map/ppermute | solution.py:362

commit v4 on v3

--- a/solution.py
+++ b/solution.py
@@ -46,22 +46,41 @@
     return jnp.broadcast_to(row, (8, row.shape[1]))
 
 
-def packed(m):
-    top = jnp.transpose(m[:128, 128:])[:8]
-    return jnp.concatenate([m[:, :128], top, m[128:, 128:]], axis=0)
-
-
-def unpacked(p):
-    high = p.shape[0] - 16
-    top = jnp.concatenate([p[high : high + 8], jnp.zeros((120, 128), F32)], axis=0)
-    right = jnp.concatenate([jnp.transpose(top), p[high + 8 :]], axis=0)
-    return jnp.concatenate([p[:high], right], axis=1)
+def packed(maps):
+    parts = [m[:, :128] for m in maps]
+    parts += [jnp.transpose(m[:128, 128:])[:8] for m in maps]
+    corner = maps[0][128:, 128:]
+    for k, m in enumerate(maps[1:]):
+        corner = corner + pltpu.roll(m[128:, 128:], 8 * k + 8, 1)
+    return jnp.concatenate(parts + [corner], axis=0)
+
+
+def length(count, high):
+    return count * (high + 8) + 8
+
+
+def unpacked(p, count, high):
+    base = count * (high + 8)
+    corner = p[base : base + 8]
+    lane = lax.broadcasted_iota(jnp.int32, (8, 128), 1)
+    maps = []
+    for k in range(count):
+        top = p[count * high + 8 * k : count * high + 8 * k + 8]
+        top = jnp.transpose(jnp.concatenate([top, jnp.zeros((120, 128), F32)], axis=0))
+        own = pltpu.roll(corner, 128 - 8 * k, 1) if k else corner
+        right = jnp.concatenate([top, jnp.where(lane < 8, own, 0.0)], axis=0)
+        maps.append(jnp.concatenate([p[k * high : k * high + high], right], axis=1))
+    return maps
 
 
 def unit_kernel(out):
     out[...] = (
         lax.broadcasted_iota(jnp.int32, out.shape, 0) == lax.broadcasted_iota(jnp.int32, out.shape, 1)
     ).astype(BF16)
+
+
+def ready_kernel(unit, lower, upper, out):
+    out[...] = unit[...]
 
 
 def ahead_kernel(unit, lower, ahead):
@@ -214,19 +233,18 @@
     s = side(0)
     f, g, b = (ordered(s, mine[k], theirs[k]) for k in range(3))
     joint, inward = merged_maps(f, g, b, False)
-    for k, m in enumerate([f[0], inward, b[1], f[1], g[1], b[0]]):
-        down[k] = m
-    size = pack.shape[0] // len(joint)
+    down[...] = inward
     for k, m in enumerate(joint):
         full[k] = m
-        pack[k * size : (k + 1) * size] = packed(m)
-
-
-def first_vectors_kernel(down, mine, theirs, out, bias):
+    pack[...] = packed(joint)
+
+
+def first_vectors_kernel(maps, others, mine, theirs, out, bias):
     s = side(0)
     f = [vector(v) for v in ordered(s, mine[0:1], theirs[0:1])]
     g = [vector(v) for v in ordered(s, mine[1:2], theirs[1:2])]
-    joint = merged_vectors(f, g, down[3], down[4], down[5])
+    right = [jnp.where(s == 0, others[k], maps[k]) for k in range(2)]
+    joint = merged_vectors(f, g, right[0], right[1], jnp.where(s == 0, maps[2], others[2]))
     out[...] = jnp.zeros(out.shape, F32)
     out[0:1] = joint[0][:1]
     out[1:2] = joint[1][:1]
@@ -234,34 +252,33 @@
     bias[1] = joint[2]
 
 
-def level_kernel(level, split, lean, mine, theirs, vectors, others, down, full, bias, out):
-    high = mine.shape[1]
-    size = high + 16
-    maps = [unpacked(theirs[k * size : (k + 1) * size]) for k in range(3)]
+def level_maps_kernel(level, lean, mine, theirs, down, full, pack):
+    maps = unpacked(theirs, 3, mine.shape[1])
     s = side(level)
     f, g, b = (ordered(s, mine[k], maps[k]) for k in range(3))
     joint, inward = merged_maps(f, g, b, lean)
-    for k, m in enumerate([f[0], inward, b[1]]):
+    for k, m in enumerate([f[0], inward, b[1], f[1], g[1], b[0]]):
         down[k] = m
-    if split:
-        other = [others[0:1], others[1:2]]
-    else:
-        other = tail_vectors(theirs, 3 * size)
+    pack[...] = packed(joint)
+    for k, m in enumerate(joint if not lean else []):
+        full[k] = m
+
+
+def level_vectors_kernel(level, split, down, pack, vectors, theirs, out, bias, ends):
+    s = side(level)
+    base = pack.shape[0]
+    other = [theirs[0:1], theirs[1:2]] if split else tail_vectors(theirs, theirs.shape[0] - 8)
     vf = [vector(v) for v in ordered(s, vectors[0:1], other[0])]
     vg = [vector(v) for v in ordered(s, vectors[1:2], other[1])]
-    v = merged_vectors(vf, vg, f[1], g[1], b[0])
+    v = merged_vectors(vf, vg, down[3], down[4], down[5])
     bias[0] = vf[0]
     bias[1] = v[2]
-    for k, m in enumerate(joint):
-        out[k * size : (k + 1) * size] = packed(m)
-        if not lean:
-            full[k] = m
-    base = len(joint) * size
-    full_vectors = jnp.concatenate([v[0][:1], v[1][:1]], axis=0)
-    out[base : base + 2] = full_vectors[:, :128]
-    out[base + 2 : base + 4] = full_vectors[:, 128:]
+    both = jnp.concatenate([v[0][:1], v[1][:1]], axis=0)
+    out[:base] = pack[...]
+    out[base : base + 2] = both[:, :128]
+    out[base + 2 : base + 4] = both[:, 128:]
     out[base + 4 : base + 8] = jnp.zeros((4, 128), F32)
-    full[full.shape[0] - 1, 0:2] = full_vectors
+    ends[0:2] = both
 
 
 def tail_vectors(theirs, base):
@@ -273,20 +290,27 @@
 
 def top_kernel(levels, *refs):
     sides = [side(k) for k in range(levels + 1)]
-    mine, theirs = refs[:2]
-    downs, biases = refs[2 : levels + 2], refs[levels + 2 : 2 * levels + 2]
+    vectors, theirs, maps, others = refs[:4]
+    downs, biases = refs[4 : levels + 4], refs[levels + 4 : 2 * levels + 4]
     keep, send = refs[-2:]
     s = sides[levels]
-    size = theirs.shape[0] - 8
-    high = size - 16
-    g = unpacked(theirs[:size])
+    high = maps.shape[1]
+    size = length(1, high)
+    g = unpacked(theirs, 1, high)[0]
     other = [vector(v) for v in tail_vectors(theirs, size)]
-    ours = vector(mine[mine.shape[0] - 1, 0:1])
+    ours = vector(vectors[0:1])
     back = times_map(ours[:, :high], g) + other[1]
     value = jnp.where(s == 0, 0.0, other[0])
     corr = jnp.where(s == 0, back, 0.0)
     for k in reversed(range(levels)):
-        d = downs[k]
+        if k:
+            d = downs[k]
+        else:
+            d = [
+                jnp.where(sides[0] == 0, maps[0], others[0]),
+                downs[0][...],
+                jnp.where(sides[0] == 0, others[2], maps[2]),
+            ]
         lhs = value[:, :high]
         middle = times_map(lhs, d[0]) + biases[k][0]
         back = times_map(lhs, d[1]) + times_map(corr[:, :high], d[2]) + biases[k][1]
@@ -300,38 +324,49 @@
     send[1] = jnp.where(left, corr, back)
 
 
-def final_kernel(mine, theirs, inner, tail, half, bias, out):
-    rows, cells, width = inner.shape
+def solved(line, ends, inner, tail, half, bias):
+    _, cells, width = inner.shape
     high = half.shape[2]
     per = cells // 2
-    core = side(0)
+    y, c = ends[0], ends[1]
+    lhs = y[:, :high]
+    middle = times_map(lhs, half[line, 0]) + bias[line, 0]
+    between = (
+        times_map(lhs, half[line, 1])
+        + times_map(c[:, :high], tail[line, per, high:])
+        + bias[line, 1]
+    )
     index = lax.broadcasted_iota(jnp.int32, (8, LANES), 0)
     gathered = jnp.zeros((8, LANES), F32)
-    for l in range(rows):
-        y = jnp.where(core == l, mine[0], theirs[0])
-        c = jnp.where(core == l, mine[1], theirs[1])
-        lhs = y[:, :high]
-        middle = times_map(lhs, half[l, 0]) + bias[l, 0]
-        between = (
-            times_map(lhs, half[l, 1])
-            + times_map(c[:, :high], tail[l, per, high:])
-            + bias[l, 1]
-        )
-        for k, v in enumerate([y, between, middle, c]):
-            gathered = jnp.where(index == 4 * l + k, v, gathered)
+    for k, v in enumerate([y, between, middle, c]):
+        gathered = jnp.where(index == k, v, gathered)
     columns = jnp.transpose(gathered)[:high]
-    for l in range(rows):
-        for p in range(2):
-            k = 4 * l + 2 * p
-            ycol = jnp.broadcast_to(columns[:, k : k + 1], (high, 128))
-            ccol = jnp.broadcast_to(columns[:, k + 1 : k + 2], (high, 128))
-            col = jnp.concatenate([ycol, ccol], axis=0)
-            for i in range(p * per, p * per + per):
-                for h in range(2):
-                    at = slice(128 * h, min(width, 128 * h + 128))
-                    t = tail[l, i, :, 128 * h : 128 * h + 128] * col
-                    r = jnp.sum(t, axis=0, keepdims=True)
-                    out[l, i : i + 1, at] = inner[l, i : i + 1, at] + r[:, : at.stop - at.start]
+    parts = []
+    for h in range(2):
+        at = slice(128 * h, min(width, 128 * h + 128))
+        sums = []
+        for i in range(cells):
+            k = 2 * (i // per)
+            t = (
+                tail[line, i, :high, 128 * h : 128 * h + 128] * columns[:, k : k + 1]
+                + tail[line, i, high:, 128 * h : 128 * h + 128] * columns[:, k + 1 : k + 2]
+            )
+            sums.append(jnp.sum(t, axis=0, keepdims=True)[:, : at.stop - at.start])
+        parts.append((at, jnp.concatenate(sums, axis=0) + inner[line, :, at]))
+    return parts
+
+
+def own_kernel(ends, inner, tail, half, bias, out):
+    for at, value in solved(side(0), ends, inner, tail, half, bias):
+        out[:, at] = value
+
+
+def final_kernel(ends, own, inner, tail, half, bias, out):
+    core = side(0)
+    other = 1 - core
+    out[core] = own[...]
+    for at, value in solved(other, ends, inner, tail, half, bias):
+        out[other, :, at] = value
 
 
 def call(body, outs, specs, scratch=(), flops=None):
@@ -353,7 +388,6 @@
 def shards(right_side, previous, coupling, neighbours, pivots, lower_factor, upper_factor):
     rows, cells, width = right_side.shape
     high = width + 1
-    size = high + 16
     patches = lax.axis_size("surf")
     count = lax.axis_size("line")
     levels = count.bit_length() - 1
@@ -365,11 +399,15 @@
     full = f32(3, high, LANES)
     row = f32(8, LANES)
     unit = call(unit_kernel, [jax.ShapeDtypeStruct((high, width), BF16)], [], flops=2000000000)()[0]
-    unit, lower_factor = lax.optimization_barrier((unit, lower_factor))
+    unit = call(ready_kernel, [jax.ShapeDtypeStruct((high, width), BF16)], [VMEM] * 3)(
+        unit, jnp.transpose(lower_factor, (0, 2, 1, 3)), jnp.transpose(upper_factor, (0, 2, 1, 3))
+    )[0]
+    unit, lower_factor, upper_factor = lax.optimization_barrier(
+        (unit, lower_factor, upper_factor)
+    )
     ahead = call(ahead_kernel, [f32(rows, cells, high, LANES)], [VMEM] * 2, flops=12000000000)(
         unit, lower_factor
     )[0]
-    ahead, upper_factor, pivots = lax.optimization_barrier((ahead, upper_factor, pivots))
     tail, half, keep, send = call(
         maps_kernel,
         [f32(rows, cells, 2 * high, LANES), f32(rows, 3, high, LANES), full, full],
@@ -378,12 +416,14 @@
     )(unit, ahead, upper_factor)
     send, first = lax.optimization_barrier((send, first))
     theirs = swap(send, 0)
+    first_maps = keep, theirs
     down, mine, pack = call(
         first_maps_kernel,
-        [f32(6, high, LANES), full, f32(3 * size, 128)],
+        [f32(high, LANES), full, f32(length(3, high), 128)],
         [VMEM] * 2,
     )(keep, theirs)
     theirs = swap(pack, 1)
+    pack, pivots = lax.optimization_barrier((pack, pivots))
     inner, ends, vkeep, vsend = call(
         functools.partial(segment_kernel, patches),
         [f32(rows, cells, width), f32(rows, 2, 8, LANES), row, row],
@@ -396,32 +436,42 @@
     )
     vtheirs = swap(vsend, 0)
     vectors, bias = call(
-        first_vectors_kernel, [row, f32(2, 8, LANES)], [VMEM] * 3
-    )(down, vkeep, vtheirs)
+        first_vectors_kernel, [row, f32(2, 8, LANES)], [VMEM] * 4
+    )(*first_maps, vkeep, vtheirs)
     others = swap(vectors, 1)
     downs = [down]
     biases = [bias]
     for k in range(1, levels - 1):
         lean = k == levels - 2
-        down, mine, bias, pack = call(
-            functools.partial(level_kernel, k, k == 1, lean),
+        count_maps = 1 if lean else 3
+        down, mine, pack = call(
+            functools.partial(level_maps_kernel, k, lean),
             [
-                full, f32(1 if lean else 4, high, LANES), f32(2, 8, LANES),
-                f32((1 if lean else 3) * size + 8, 128),
+                f32(6, high, LANES), f32(1 if lean else 3, high, LANES),
+                f32(length(count_maps, high), 128),
             ],
+            [VMEM] * 2,
+            flops=20000000000,
+        )(mine, theirs)
+        pack, bias, vectors = call(
+            functools.partial(level_vectors_kernel, k, k == 1),
+            [f32(length(count_maps, high) + 8, 128), f32(2, 8, LANES), row],
             [VMEM] * 4,
-        )(mine, theirs, vectors, others)
+        )(down, pack, vectors, others if k == 1 else theirs)
         downs.append(down)
         biases.append(bias)
-        vectors = others = mine[-1, :8]
         theirs = swap(pack, k + 1)
     keep, send = call(
         functools.partial(top_kernel, levels - 1),
         [f32(2, 8, LANES)] * 2,
-        [VMEM] * (2 + 2 * len(downs)),
-    )(mine, theirs, *downs, *biases)
+        [VMEM] * (4 + 2 * len(downs)),
+    )(vectors, theirs, *first_maps, *downs, *biases)
+    theirs = swap(send, 0)
+    own = call(own_kernel, [f32(cells, width)], [VMEM] * 5, flops=2000000000)(
+        keep, inner, tail, half, ends
+    )[0]
     return call(final_kernel, [f32(rows, cells, width)], [VMEM] * 6)(
-        keep, swap(send, 0), inner, tail, half, ends
+        theirs, own, inner, tail, half, ends
     )[0]
 
 

time: 27.4 us -> 26.6 us (0.971)
  waiting for transfers between devices: 7.54 us -> 6.73 us
  Pallas kernels: 7.48 us -> 8.01 us
  local copies, waits for them, and re-layouts: 1.2 us -> 0.7 us
    pallas_call x3 -> x6, Pallas kernels: 1.5 us -> 2.38 us  [the longest x1 0.67 us: shards(): call(functools.partial(level_maps_kernel, k, lean), [f32(6, high, LANES),...]
    ppermute x6, waiting for transfers between devices: 7.54 us -> 6.73 us  [shards(): lax.ppermute(a, 'line', [(i, i ^ 1 << k) for i in range(count)])]
    unnamed x14, local copies, waits for them, and re-layouts: 0.53 us -> 0.04 us
    ppermute x6, starting transfers between devices: 4.53 us -> 4.19 us  [shards(): lax.ppermute(a, 'line', [(i, i ^ 1 << k) for i in range(count)])]
    pallas_call x1, Pallas kernels: 1.47 us -> 1.13 us  [shards(): call(final_kernel, [f32(rows, cells, width)], [VMEM] * 6)]
    ppermute x1, starting transfers between devices: 3.31 us -> 3.61 us  [shards(): second = lax.ppermute(previous, 'surf', odd)]
  transfers between devices with their start and end apart: 8 -> 8, of which waited for: 4 -> 4; matrix products, arithmetic and copies ran while one was open for 2% -> 3% of each run, Pallas kernels for 18% -> 23%
where the time goes in v4:
time: 26.6 us; the launch traced here: 26.4 us
  starting transfers between devices  10.8 us (41%)
  Pallas kernels  8.01 us (30%)
  waiting for transfers between devices  6.73 us (25%)
  local copies, waits for them, and re-layouts  0.7 us (3%)
    ppermute x6, waiting for transfers between devices, shards(): lax.ppermute(a, 'line', [(i, i ^ 1 << k) for i in range(count)])  6.73 us
    ppermute x6, starting transfers between devices, shards(): lax.ppermute(a, 'line', [(i, i ^ 1 << k) for i in range(count)])  4.19 us
    ppermute x1, starting transfers between devices, shards(): second = lax.ppermute(previous, 'surf', odd)  3.61 us
    ppermute x1, starting transfers between devices, shards(): first = lax.ppermute(previous, 'surf', pairs)  3.02 us
    pallas_call x1, Pallas kernels, shards(): call(maps_kernel, [f32(rows, cells, 2 * high, LANES), f32(rows, 3, high,...  1.86 us
    pallas_call x1, Pallas kernels, shards(): call(functools.partial(segment_kernel, patches), [f32(rows, cells, width)...  1.43 us
    pallas_call x1, Pallas kernels, shards(): call(final_kernel, [f32(rows, cells, width)], [VMEM] * 6)  1.13 us
    pallas_call x1, Pallas kernels, shards(): call(ahead_kernel, [f32(rows, cells, high, LANES)], [VMEM] * 2, flops=120...  0.73 us
  transfers between devices with their start and end apart: 8, of which 4 were waited for; matrix products, arithmetic and copies ran while one was open for 3% of the time, Pallas kernels for 23%

profile of v4, /device:TPU:0, one launch (start us, length us, event | category | flops | bytes accessed | tf_op | source)
XLA Modules:
  0.0 26.4 jit_solution(14545211808793061080)
XLA Ops:
  0.0 0.0 copy-start
  0.0 0.0 copy-start.1
  0.0 3.0 %collective-permute-start = (f32[2,8,135]{2,1,0:T(8,128)}, f32[2,8,135]{2,1,0:T(8,128)S(1)}, u32[]{:S(2)}, u32[]{:S(2)}) collective-permute-start(f32[2,8,135]{2,1,0:T(8,128)} %own.1), channel_id=1, source_target_pairs={{0,1},{1,0},{2,3},{3,2},{4,5},{5,4},{6,7},{7,6},{8,9},{9,8},{10,11... | collective-permute-start | bytes 25928 | tf_op jit(solution)/shard_map/ppermute | solution.py:398
  3.0 0.0 copy-done
  3.1 0.0 copy-done.1
  3.1 0.2 copy.8.lower
  3.3 0.2 copy.9.upper
  3.5 0.7 %shard_map.75.ahead = f32[2,8,136,256]{3,2,1,0:T(8,128)S(1)} custom-call(bf16[136,135]{1,0:T(8,128)(2,1)S(1)} %shard_map.74.unit, bf16[2,8,135,135]{3,2,1,0:T(8,128)(2,1)S(1)} %copy.8.lower), custom_call_target="tpu_custom_call" | custom-call | flops 12000000000 | tf_op jit(solution)/shard_map/pallas_call | solution.py:408
  4.3 0.0 copy-start.4
  4.3 0.0 copy-start.6
  4.3 1.9 %shard_map.76 = (f32[2,8,272,256]{3,2,1,0:T(8,128)S(1)}, f32[2,3,136,256]{3,2,1,0:T(8,128)S(1)}, f32[3,136,256]{2,1,0:T(8,128)S(1)}, f32[3,136,256]{2,1,0:T(8,128)S(1)}) custom-call(bf16[136,135]{1,0:T(8,128)(2,1)S(1)} %shard_map.74.unit, f32[2,8,136,256]{3,2,1,0:T(8,128)S(1)} %shard_map.75.ahead, bf16[2,8,135,135]{3,2,1,0:T(8,128)(2,1)S(1)} %copy.9.upper), custom_call_target="tpu_custom_call" | custom-call | flops 12000000000 | tf_op jit(solution)/shard_map/pallas_call | solution.py:411
  6.2 0.0 collective-permute-done.first
  6.2 0.1 collective-permute-start.1
  6.3 0.0 copy-done.4
  6.3 3.6 %collective-permute-start.3 = (f32[2,8,135]{2,1,0:T(8,128)S(1)}, f32[2,8,135]{2,1,0:T(8,128)S(1)}, u32[]{:S(2)}, u32[]{:S(2)}) collective-permute-start(f32[2,8,135]{2,1,0:T(8,128)S(1)} %copy-done.4), channel_id=1, source_target_pairs={{0,3},{1,2},{2,1},{3,0},{4,7},{5,6},{6,5},{7,4},{8,11},{9,10},{10,... | collective-permute-start | bytes 25928 | tf_op jit(solution)/shard_map/ppermute | solution.py:397
  9.9 0.0 collective-permute-done.1.theirs.others.refs_3_
  9.9 0.6 %shard_map.77 = (f32[136,256]{1,0:T(8,128)S(1)}, f32[3,136,256]{2,1,0:T(8,128)S(1)}, f32[440,128]{1,0:T(8,128)S(1)}) custom-call(f32[3,136,256]{2,1,0:T(8,128)S(1)} %get-tuple-element.35.mine.maps.refs_2_, f32[3,136,256]{2,1,0:T(8,128)S(1)} %collective-permute-done.1.theirs.others.refs_3_), custom_call_target="tpu_custom_call" | custom-call | tf_op jit(solution)/shard_map/pallas_call | solution.py:420
  10.5 0.0 copy-start.2
  10.5 0.0 copy-start.3
  10.5 0.0 copy-start.5
  10.5 1.6 %collective-permute-start.2 = (f32[440,128]{1,0:T(8,128)S(1)}, f32[440,128]{1,0:T(8,128)S(1)}, u32[]{:S(2)}, u32[]{:S(2)}) collective-permute-start(f32[440,128]{1,0:T(8,128)S(1)} %get-tuple-element.46.after), channel_id=1, source_target_pairs={{0,8},{4,12},{8,0},{12,4},{16,24},{20,28},{24,16},{28,20},{1,9},{5... | collective-permute-start | bytes 675848 | tf_op jit(solution)/shard_map/ppermute | solution.py:396
  12.1 0.0 copy-done.6
  12.1 0.2 copy.10.pivots
  12.3 0.0 collective-permute-done.3.second
  12.3 0.0 copy-done.2
  12.3 0.0 copy-done.3
  12.4 0.0 copy-done.5
  12.4 1.4 %shard_map.79 = (f32[2,8,135]{2,1,0:T(8,128)S(1)}, f32[2,2,8,256]{3,2,1,0:T(8,128)S(1)}, f32[8,256]{1,0:T(8,128)S(1)}, f32[8,256]{1,0:T(8,128)S(1)}) custom-call(s32[2,4]{1,0:T(2,128)S(1)} %copy-done.5, f32[2,8,135]{2,1,0:T(8,128)S(1)} %copy-done.3, f32[2,8,135]{2,1,0:T(8,128)S(1)} %copy-done.4, f32[2,8,135]{2,1,0:T(8,128)S(1)} %collective-permute-done.first, ...), custom_call_target="tpu_custom_call" | custom-call | flops 49999998976 | tf_op jit(solution)/shard_map/pallas_call | solution.py:427
  13.8 0.0 collective-permute-start.4
  13.8 1.2 %collective-permute-done.4.theirs = f32[8,256]{1,0:T(8,128)S(1)} collective-permute-done((f32[8,256]{1,0:T(8,128)S(1)}, f32[8,256]{1,0:T(8,128)S(1)}, u32[]{:S(2)}, u32[]{:S(2)}) %collective-permute-start.4) | collective-permute-done | bytes 8224 | tf_op jit(solution)/shard_map/ppermute | solution.py:396
  15.0 0.3 %shard_map.80 = (f32[8,256]{1,0:T(8,128)S(1)}, f32[2,8,256]{2,1,0:T(8,128)S(1)}) custom-call(f32[3,136,256]{2,1,0:T(8,128)S(1)} %get-tuple-element.35.mine.maps.refs_2_, f32[3,136,256]{2,1,0:T(8,128)S(1)} %collective-permute-done.1.theirs.others.refs_3_, f32[8,256]{1,0:T(8,128)S(1)} %get-tuple-element.47.mine, f32[8,256]{1,0:T(8,128)S(1)} %collective-permute-done.4.theirs), custom_call_target="tpu_custom_call" | custom-call | tf_op jit(solution)/shard_map/pallas_call | solution.py:438
  15.3 1.0 %collective-permute-start.5 = (f32[8,256]{1,0:T(8,128)S(1)}, f32[8,256]{1,0:T(8,128)S(1)}, u32[]{:S(2)}, u32[]{:S(2)}) collective-permute-start(f32[8,256]{1,0:T(8,128)S(1)} %get-tuple-element.49.vectors), channel_id=1, source_target_pairs={{0,8},{4,12},{8,0},{12,4},{16,24},{20,28},{24,16},{28,20},{1,9},{5... | collective-permute-start | bytes 24584 | tf_op jit(solution)/shard_map/ppermute | solution.py:396
  16.3 2.0 %collective-permute-done.2.theirs = f32[440,128]{1,0:T(8,128)S(1)} collective-permute-done((f32[440,128]{1,0:T(8,128)S(1)}, f32[440,128]{1,0:T(8,128)S(1)}, u32[]{:S(2)}, u32[]{:S(2)}) %collective-permute-start.2) | collective-permute-done | bytes 225312 | tf_op jit(solution)/shard_map/ppermute | solution.py:396
  18.3 0.7 %shard_map.78 = (f32[6,136,256]{2,1,0:T(8,128)S(1)}, f32[1,136,256]{2,1,0:T(8,128)}, f32[152,128]{1,0:T(8,128)S(1)}) custom-call(f32[3,136,256]{2,1,0:T(8,128)S(1)} %get-tuple-element.38.mine, f32[440,128]{1,0:T(8,128)S(1)} %collective-permute-done.2.theirs), custom_call_target="tpu_custom_call" | custom-call | flops 20000000000 | tf_op jit(solution)/shard_map/pallas_call | solution.py:447
  18.9 0.0 collective-permute-done.5.theirs
  18.9 0.3 shard_map.81
  19.2 1.5 %collective-permute-start.6 = (f32[160,128]{1,0:T(8,128)S(1)}, f32[160,128]{1,0:T(8,128)S(1)}, u32[]{:S(2)}, u32[]{:S(2)}) collective-permute-start(f32[160,128]{1,0:T(8,128)S(1)} %get-tuple-element.51), channel_id=1, source_target_pairs={{0,16},{4,20},{8,24},{12,28},{16,0},{20,4},{24,8},{28,12},{1,17},{... | collective-permute-start | bytes 245768 | tf_op jit(solution)/shard_map/ppermute | solution.py:396
  20.7 2.9 %collective-permute-done.6.refs_1_ = f32[160,128]{1,0:T(8,128)S(1)} collective-permute-done((f32[160,128]{1,0:T(8,128)S(1)}, f32[160,128]{1,0:T(8,128)S(1)}, u32[]{:S(2)}, u32[]{:S(2)}) %collective-permute-start.6) | collective-permute-done | bytes 81952 | tf_op jit(solution)/shard_map/ppermute | solution.py:396
  23.6 0.5 %shard_map.82 = (f32[2,8,256]{2,1,0:T(8,128)S(1)}, f32[2,8,256]{2,1,0:T(8,128)S(1)}) custom-call(f32[8,256]{1,0:T(8,128)S(1)} %get-tuple-element.50.refs_0_, f32[160,128]{1,0:T(8,128)S(1)} %collective-permute-done.6.refs_1_, f32[3,136,256]{2,1,0:T(8,128)S(1)} %get-tuple-element.35.mine.maps.refs_2_, ...), custom_call_target="tpu_custom_call" | custom-call | tf_op jit(solution)/shard_map/pallas_call | solution.py:464
  24.1 0.0 collective-permute-start.7
  24.1 0.5 %shard_map.83.own = f32[8,135]{1,0:T(8,128)S(1)} custom-call(f32[2,8,256]{2,1,0:T(8,128)S(1)} %get-tuple-element.56.ends, f32[2,8,135]{2,1,0:T(8,128)S(1)} %get-tuple-element.57.inner, f32[2,8,272,256]{3,2,1,0:T(8,128)S(1)} %get-tuple-element.44.tail, f32[2,3,136,256]{3,2,1,0:T(8,128)S(1)} %get-tuple-element.45.half, f32[2,2,8,256]{3,2,1,0:T(8,128)S(1)} %get-tuple-element.58.bias), custom_call_target="tpu_custom_call" | custom-call | flops 2000000000 | tf_op jit(solution)/shard_map/pallas_call | solution.py:470
  24.7 0.6 %collective-permute-done.7.ends = f32[2,8,256]{2,1,0:T(8,128)S(1)} collective-permute-done((f32[2,8,256]{2,1,0:T(8,128)S(1)}, f32[2,8,256]{2,1,0:T(8,128)S(1)}, u32[]{:S(2)}, u32[]{:S(2)}) %collective-permute-start.7) | collective-permute-done | bytes 16416 | tf_op jit(solution)/shard_map/ppermute | solution.py:396
  25.3 1.1 %shard_map.84 = f32[2,8,135]{2,1,0:T(8,128)} custom-call(f32[2,8,256]{2,1,0:T(8,128)S(1)} %collective-permute-done.7.ends, f32[8,135]{1,0:T(8,128)S(1)} %shard_map.83.own, f32[2,8,135]{2,1,0:T(8,128)S(1)} %get-tuple-element.57.inner, f32[2,8,272,256]{3,2,1,0:T(8,128)S(1)} %get-tuple-element.44.tail, f32[2,3,136,256]{3,2,1,0:T(8,128)S(1)} %get-tuple-element.45.half, ...), custom_call_target="tpu_custom_call" | custom-call | tf_op jit(solution)/shard_map/pallas_call | solution.py:473
  (2 shorter events, 0.0 us)
Async XLA Ops:
  0.0 3.0 %copy-start = (bf16[2,8,135,135]{3,1,2,0:T(8,128)(2,1)S(1)}, bf16[2,8,135,135]{3,1,2,0:T(8,128)(2,1)}, u32[]{:S(2)}) copy-start(bf16[2,8,135,135]{3,1,2,0:T(8,128)(2,1)} %param.12) | copy-start | bytes 1749604
  0.0 3.1 %copy-start.1 = (bf16[2,8,135,135]{3,1,2,0:T(8,128)(2,1)S(1)}, bf16[2,8,135,135]{3,1,2,0:T(8,128)(2,1)}, u32[]{:S(2)}) copy-start(bf16[2,8,135,135]{3,1,2,0:T(8,128)(2,1)} %param.13) | copy-start | bytes 1749604
  0.0 6.2 %collective-permute-start = (f32[2,8,135]{2,1,0:T(8,128)}, f32[2,8,135]{2,1,0:T(8,128)S(1)}, u32[]{:S(2)}, u32[]{:S(2)}) collective-permute-start(f32[2,8,135]{2,1,0:T(8,128)} %own.1), channel_id=1, source_target_pairs={{0,1},{1,0},{2,3},{3,2},{4,5},{5,4},{6,7},{7,6},{8,9},{9,8},{10,11... | collective-permute-start | bytes 25928 | tf_op jit(solution)/shard_map/ppermute | solution.py:398
  4.3 2.0 %copy-start.4 = (f32[2,8,135]{2,1,0:T(8,128)S(1)}, f32[2,8,135]{2,1,0:T(8,128)}, u32[]{:S(2)}) copy-start(f32[2,8,135]{2,1,0:T(8,128)} %own.1) | copy-start | bytes 25924
  4.3 7.8 %copy-start.6 = (bf16[2,8,135,135]{3,1,2,0:T(8,128)(2,1)S(1)}, bf16[2,8,135,135]{3,1,2,0:T(8,128)(2,1)}, u32[]{:S(2)}) copy-start(bf16[2,8,135,135]{3,1,2,0:T(8,128)(2,1)} %param.11) | copy-start | bytes 1749604
  6.2 3.7 %collective-permute-start.1 = (f32[3,136,256]{2,1,0:T(8,128)S(1)}, f32[3,136,256]{2,1,0:T(8,128)S(1)}, u32[]{:S(2)}, u32[]{:S(2)}) collective-permute-start(f32[3,136,256]{2,1,0:T(8,128)S(1)} %get-tuple-element.37), channel_id=1, source_target_pairs={{0,4},{4,0},{8,12},{12,8},{16,20},{20,16},{24,28},{28,24},{1,5},{5... | collective-permute-start | bytes 1253384 | tf_op jit(solution)/shard_map/ppermute | solution.py:396
  6.3 6.1 %collective-permute-start.3 = (f32[2,8,135]{2,1,0:T(8,128)S(1)}, f32[2,8,135]{2,1,0:T(8,128)S(1)}, u32[]{:S(2)}, u32[]{:S(2)}) collective-permute-start(f32[2,8,135]{2,1,0:T(8,128)S(1)} %copy-done.4), channel_id=1, source_target_pairs={{0,3},{1,2},{2,1},{3,0},{4,7},{5,6},{6,5},{7,4},{8,11},{9,10},{10,... | collective-permute-start | bytes 25928 | tf_op jit(solution)/shard_map/ppermute | solution.py:397
  10.5 1.8 %copy-start.2 = (f32[2,8,4,135]{3,2,1,0:T(4,128)S(1)}, f32[2,8,4,135]{3,2,1,0:T(4,128)}, u32[]{:S(2)}) copy-start(f32[2,8,4,135]{3,2,1,0:T(4,128)} %coupling.1) | copy-start | bytes 103684
  10.5 1.8 %copy-start.3 = (f32[2,8,135]{2,1,0:T(8,128)S(1)}, f32[2,8,135]{2,1,0:T(8,128)}, u32[]{:S(2)}) copy-start(f32[2,8,135]{2,1,0:T(8,128)} %right.1) | copy-start | bytes 25924
  10.5 1.8 %copy-start.5 = (s32[2,4]{1,0:T(2,128)S(1)}, s32[2,4]{1,0:T(2,128)}, u32[]{:S(2)}) copy-start(s32[2,4]{1,0:T(2,128)} %neighbours.1) | copy-start | bytes 100
  10.5 7.7 %collective-permute-start.2 = (f32[440,128]{1,0:T(8,128)S(1)}, f32[440,128]{1,0:T(8,128)S(1)}, u32[]{:S(2)}, u32[]{:S(2)}) collective-permute-start(f32[440,128]{1,0:T(8,128)S(1)} %get-tuple-element.46.after), channel_id=1, source_target_pairs={{0,8},{4,12},{8,0},{12,4},{16,24},{20,28},{24,16},{28,20},{1,9},{5... | collective-permute-start | bytes 675848 | tf_op jit(solution)/shard_map/ppermute | solution.py:396
  13.8 1.2 %collective-permute-start.4 = (f32[8,256]{1,0:T(8,128)S(1)}, f32[8,256]{1,0:T(8,128)S(1)}, u32[]{:S(2)}, u32[]{:S(2)}) collective-permute-start(f32[8,256]{1,0:T(8,128)S(1)} %get-tuple-element.48), channel_id=1, source_target_pairs={{0,4},{4,0},{8,12},{12,8},{16,20},{20,16},{24,28},{28,24},{1,5},{5... | collective-permute-start | bytes 24584 | tf_op jit(solution)/shard_map/ppermute | solution.py:396
  15.3 3.7 %collective-permute-start.5 = (f32[8,256]{1,0:T(8,128)S(1)}, f32[8,256]{1,0:T(8,128)S(1)}, u32[]{:S(2)}, u32[]{:S(2)}) collective-permute-start(f32[8,256]{1,0:T(8,128)S(1)} %get-tuple-element.49.vectors), channel_id=1, source_target_pairs={{0,8},{4,12},{8,0},{12,4},{16,24},{20,28},{24,16},{28,20},{1,9},{5... | collective-permute-start | bytes 24584 | tf_op jit(solution)/shard_map/ppermute | solution.py:396
  19.2 4.4 %collective-permute-start.6 = (f32[160,128]{1,0:T(8,128)S(1)}, f32[160,128]{1,0:T(8,128)S(1)}, u32[]{:S(2)}, u32[]{:S(2)}) collective-permute-start(f32[160,128]{1,0:T(8,128)S(1)} %get-tuple-element.51), channel_id=1, source_target_pairs={{0,16},{4,20},{8,24},{12,28},{16,0},{20,4},{24,8},{28,12},{1,17},{... | collective-permute-start | bytes 245768 | tf_op jit(solution)/shard_map/ppermute | solution.py:396
  24.1 1.2 %collective-permute-start.7 = (f32[2,8,256]{2,1,0:T(8,128)S(1)}, f32[2,8,256]{2,1,0:T(8,128)S(1)}, u32[]{:S(2)}, u32[]{:S(2)}) collective-permute-start(f32[2,8,256]{2,1,0:T(8,128)S(1)} %get-tuple-element.55), channel_id=1, source_target_pairs={{0,4},{4,0},{8,12},{12,8},{16,20},{20,16},{24,28},{28,24},{1,5},{5... | collective-permute-start | bytes 49160 | tf_op jit(solution)/shard_map/ppermute | solution.py:396

commit v5 on v4

--- a/solution.py
+++ b/solution.py
@@ -111,32 +111,42 @@
         send[k, :, 128:] = blank
         for l in range(rows):
             half[l, k, :, 128:] = blank
+    ends = [[ahead[l, p * per + per - 1, :, :width] for p in range(2)] for l in range(rows)]
     back = {}
+
+    def step(l, p, j):
+        i = p * per + j
+        if j == per - 1:
+            g, b = ends[l][p], dot_nt(eye, upper[l, i])
+        elif j == per - 2:
+            g, b = back[l, p]
+            rest = g - g.astype(BF16).astype(F32)
+            r = dot_nt(jnp.concatenate([g, rest, b], axis=0).astype(BF16), upper[l, i])
+            g = ahead[l, i, :, :width] + (r[:high] + r[high : 2 * high])
+            b = r[2 * high :]
+        else:
+            both = times_block(jnp.concatenate(back[l, p], axis=0), upper[l, i])
+            g = ahead[l, i, :, :width] + both[:high]
+            b = both[high:]
+        back[l, p] = g, b
+        tail[l, i, :high, :width] = g
+        tail[l, i, high:, :width] = b
+
     for j in reversed(range(per)):
-        for l in range(rows):
-            for p in range(2):
-                i = p * per + j
-                if j == per - 1:
-                    now = jnp.concatenate(
-                        [ahead[l, i, :, :width], dot_nt(eye, upper[l, i])], axis=0
-                    )
-                else:
-                    both = times_block(back[l, p], upper[l, i])
-                    now = jnp.concatenate(
-                        [ahead[l, i, :, :width] + both[:high], both[high:]], axis=0
-                    )
-                back[l, p] = now
-                tail[l, i, :, :width] = now
+        for p in (1, 0):
+            for l in range(rows):
+                step(l, p, j)
+        if j == per - 1:
+            front = [times_map(f[0], f[1][:width]) for f in ends]
     joint = []
     for l in range(rows):
-        f = [ahead[l, p * per + per - 1, :, :width] for p in range(2)]
-        g = back[l, 0][:high], back[l, 1][:high]
-        b = back[l, 0][high:], back[l, 1][high:]
-        inward = times_map(f[0], g[1][:width])
+        g = back[l, 0][0], back[l, 1][0]
+        b = back[l, 0][1], back[l, 1][1]
+        inward = times_map(ends[l][0], g[1][:width])
         both = times_map(jnp.concatenate([inward, b[1]], axis=0), b[0][:width])
-        for k, m in enumerate([f[0], inward, f[1]]):
+        for k, m in enumerate([ends[l][0], inward, ends[l][1]]):
             half[l, k, :, :width] = m
-        joint.append([times_map(f[0], f[1][:width]), g[0] + both[:high], both[high:]])
+        joint.append([front[l], g[0] + both[:high], both[high:]])
     for k in range(3):
         keep[k, :, :width] = jnp.where(core == 0, joint[0][k], joint[1][k])
         send[k, :, :width] = jnp.where(core == 0, joint[1][k], joint[0][k])
@@ -213,12 +223,10 @@
     return jnp.where(s == 0, mine, theirs), jnp.where(s == 0, theirs, mine)
 
 
-def merged_maps(f, g, b, lean):
+def merged_maps(f, g, b):
     high = f[0].shape[0]
     lhs = f[0][:, :high]
     inward = times_map(lhs, g[1])
-    if lean:
-        return [g[0] + times_map(inward[:, :high], b[0])], inward
     both = times_map(jnp.concatenate([inward, b[1]], axis=0)[:, :high], b[0])
     return [times_map(lhs, f[1]), g[0] + both[:high], both[high:]], inward
 
@@ -232,7 +240,7 @@
 def first_maps_kernel(mine, theirs, down, full, pack):
     s = side(0)
     f, g, b = (ordered(s, mine[k], theirs[k]) for k in range(3))
-    joint, inward = merged_maps(f, g, b, False)
+    joint, inward = merged_maps(f, g, b)
     down[...] = inward
     for k, m in enumerate(joint):
         full[k] = m
@@ -253,13 +261,21 @@
 
 
 def level_maps_kernel(level, lean, mine, theirs, down, full, pack):
-    maps = unpacked(theirs, 3, mine.shape[1])
+    high = mine.shape[1]
+    maps = unpacked(theirs, 3, high)
     s = side(level)
     f, g, b = (ordered(s, mine[k], maps[k]) for k in range(3))
-    joint, inward = merged_maps(f, g, b, lean)
-    for k, m in enumerate([f[0], inward, b[1], f[1], g[1], b[0]]):
+    lhs = f[0][:, :high]
+    if lean:
+        through = times_map(g[1][:, :high], b[0])
+        joint = [g[0] + times_map(lhs, through)]
+    else:
+        both = times_map(jnp.concatenate([g[1], b[1]], axis=0)[:, :high], b[0])
+        through = both[:high]
+        joint = [times_map(lhs, f[1]), g[0] + times_map(lhs, through), both[high:]]
+    pack[...] = packed(joint)
+    for k, m in enumerate([f[0], b[1], f[1], g[1], b[0], through]):
         down[k] = m
-    pack[...] = packed(joint)
     for k, m in enumerate(joint if not lean else []):
         full[k] = m
 
@@ -270,7 +286,13 @@
     other = [theirs[0:1], theirs[1:2]] if split else tail_vectors(theirs, theirs.shape[0] - 8)
     vf = [vector(v) for v in ordered(s, vectors[0:1], other[0])]
     vg = [vector(v) for v in ordered(s, vectors[1:2], other[1])]
-    v = merged_vectors(vf, vg, down[3], down[4], down[5])
+    high = down.shape[1]
+    lhs = vf[0][:, :high]
+    v = (
+        times_map(lhs, down[2]) + vf[1],
+        vg[0] + times_map(lhs, down[5]) + times_map(vg[1][:, :high], down[4]),
+        times_map(lhs, down[3]) + vg[1],
+    )
     bias[0] = vf[0]
     bias[1] = v[2]
     both = jnp.concatenate([v[0][:1], v[1][:1]], axis=0)
@@ -288,40 +310,69 @@
     ]
 
 
-def top_kernel(levels, *refs):
-    sides = [side(k) for k in range(levels + 1)]
-    vectors, theirs, maps, others = refs[:4]
-    downs, biases = refs[4 : levels + 4], refs[levels + 4 : 2 * levels + 4]
-    keep, send = refs[-2:]
-    s = sides[levels]
+def paths_kernel(levels, *refs):
+    maps, others, first_inward = refs[:3]
+    downs, biases = refs[3 : levels + 2], refs[levels + 2 : 2 * levels + 2]
+    hi, lo, add = refs[-3:]
     high = maps.shape[1]
-    size = length(1, high)
+    top = side(levels) == 1
+    s = side(0)
+    eye = (
+        lax.broadcasted_iota(jnp.int32, (high, LANES), 0)
+        == lax.broadcasted_iota(jnp.int32, (high, LANES), 1)
+    ).astype(F32)
+    nothing = jnp.zeros((8, LANES), F32)
+    value = jnp.concatenate([jnp.where(top, eye, 0.0), nothing], axis=0)
+    corr = jnp.concatenate([jnp.where(top, 0.0, eye), nothing], axis=0)
+    for k in reversed(range(levels)):
+        if k:
+            d = downs[k - 1]
+            f, b = d[0], d[1]
+            inward = times_map(f[:, :high], d[3])
+        else:
+            f = jnp.where(s == 0, maps[0], others[0])
+            b = jnp.where(s == 0, others[2], maps[2])
+            inward = first_inward[...]
+        if k == levels - 1:
+            middle, back = jnp.where(top, f, 0.0), jnp.where(top, inward, b)
+            middle = jnp.concatenate([middle, nothing], axis=0)
+            back = jnp.concatenate([back, nothing], axis=0)
+        else:
+            lhs = value[:, :high]
+            middle = times_map(lhs, f)
+            back = times_map(lhs, inward) + times_map(corr[:, :high], b)
+        base = jnp.zeros((high, LANES), F32)
+        middle = middle + jnp.concatenate([base, biases[k][0]], axis=0)
+        back = back + jnp.concatenate([base, biases[k][1]], axis=0)
+        if k:
+            value = jnp.where(side(k) == 0, value, middle)
+            corr = jnp.where(side(k) == 0, back, corr)
+    paths = [
+        jnp.where(s == 0, value, middle), jnp.where(s == 0, back, corr),
+        jnp.where(s == 0, middle, value), jnp.where(s == 0, corr, back),
+    ]
+    for k, m in enumerate(paths):
+        top_term = m[:high].astype(BF16)
+        hi[k] = top_term
+        lo[k] = (m[:high] - top_term.astype(F32)).astype(BF16)
+        add[k] = m[high:]
+
+
+def top_kernel(level, vectors, theirs, hi, lo, add, keep, send):
+    high = hi.shape[1]
     g = unpacked(theirs, 1, high)[0]
-    other = [vector(v) for v in tail_vectors(theirs, size)]
+    other = [vector(v) for v in tail_vectors(theirs, length(1, high))]
     ours = vector(vectors[0:1])
     back = times_map(ours[:, :high], g) + other[1]
-    value = jnp.where(s == 0, 0.0, other[0])
-    corr = jnp.where(s == 0, back, 0.0)
-    for k in reversed(range(levels)):
-        if k:
-            d = downs[k]
+    x = jnp.where(side(level) == 0, back, other[0])[:, :high]
+    a = stacked(x)
+    for k in range(4):
+        r = dot_nn(a, hi[k])
+        r = r[:8] + r[8:] + dot_nn(a[:8], lo[k]) + add[k]
+        if k < 2:
+            keep[k] = r
         else:
-            d = [
-                jnp.where(sides[0] == 0, maps[0], others[0]),
-                downs[0][...],
-                jnp.where(sides[0] == 0, others[2], maps[2]),
-            ]
-        lhs = value[:, :high]
-        middle = times_map(lhs, d[0]) + biases[k][0]
-        back = times_map(lhs, d[1]) + times_map(corr[:, :high], d[2]) + biases[k][1]
-        if k:
-            value = jnp.where(sides[k] == 0, value, middle)
-            corr = jnp.where(sides[k] == 0, back, corr)
-    left = sides[0] == 0
-    keep[0] = jnp.where(left, value, middle)
-    keep[1] = jnp.where(left, back, corr)
-    send[0] = jnp.where(left, middle, value)
-    send[1] = jnp.where(left, corr, back)
+            send[k - 2] = r
 
 
 def solved(line, ends, inner, tail, half, bias):
@@ -461,11 +512,15 @@
         downs.append(down)
         biases.append(bias)
         theirs = swap(pack, k + 1)
+    hi, lo, add = call(
+        functools.partial(paths_kernel, levels - 1),
+        [jax.ShapeDtypeStruct((4, high, LANES), BF16)] * 2 + [f32(4, 8, LANES)],
+        [VMEM] * (2 + len(downs) + len(biases)),
+        flops=3000000000,
+    )(*first_maps, *downs, *biases)
     keep, send = call(
-        functools.partial(top_kernel, levels - 1),
-        [f32(2, 8, LANES)] * 2,
-        [VMEM] * (4 + 2 * len(downs)),
-    )(vectors, theirs, *first_maps, *downs, *biases)
+        functools.partial(top_kernel, levels - 1), [f32(2, 8, LANES)] * 2, [VMEM] * 5
+    )(vectors, theirs, hi, lo, add)
     theirs = swap(send, 0)
     own = call(own_kernel, [f32(cells, width)], [VMEM] * 5, flops=2000000000)(
         keep, inner, tail, half, ends

time: 26.6 us -> 26.5 us (level)
  waiting for transfers between devices: 6.73 us -> 6.25 us
    ppermute x6, waiting for transfers between devices: 6.73 us -> 6.24 us  [shards(): lax.ppermute(a, 'line', [(i, i ^ 1 << k) for i in range(count)])]
    pallas_call x0 -> x1, Pallas kernels: none -> 0.47 us  [shards(): call(functools.partial(paths_kernel, levels - 1), [jax.ShapeDtypeStruct((...]
  transfers between devices with their start and end apart: 8 -> 8, of which waited for: 4 -> 4; matrix products, arithmetic and copies ran while one was open for 3% -> 3% of each run, Pallas kernels for 23% -> 25%
where the time goes in v5:
time: 26.5 us; the launch traced here: 26.3 us
  starting transfers between devices  10.9 us (41%)
  Pallas kernels  8.23 us (31%)
  waiting for transfers between devices  6.25 us (24%)
  local copies, waits for them, and re-layouts  0.7 us (3%)
    ppermute x6, waiting for transfers between devices, shards(): lax.ppermute(a, 'line', [(i, i ^ 1 << k) for i in range(count)])  6.24 us
    ppermute x6, starting transfers between devices, shards(): lax.ppermute(a, 'line', [(i, i ^ 1 << k) for i in range(count)])  4.3 us
    ppermute x1, starting transfers between devices, shards(): second = lax.ppermute(previous, 'surf', odd)  3.62 us
    ppermute x1, starting transfers between devices, shards(): first = lax.ppermute(previous, 'surf', pairs)  3.02 us
    pallas_call x1, Pallas kernels, shards(): call(maps_kernel, [f32(rows, cells, 2 * high, LANES), f32(rows, 3, high,...  1.78 us
    pallas_call x1, Pallas kernels, shards(): call(functools.partial(segment_kernel, patches), [f32(rows, cells, width)...  1.43 us
    pallas_call x1, Pallas kernels, shards(): call(final_kernel, [f32(rows, cells, width)], [VMEM] * 6)  1.13 us
    pallas_call x1, Pallas kernels, shards(): call(ahead_kernel, [f32(rows, cells, high, LANES)], [VMEM] * 2, flops=120...  0.73 us
  transfers between devices with their start and end apart: 8, of which 4 were waited for; matrix products, arithmetic and copies ran while one was open for 3% of the time, Pallas kernels for 25%

profile of v5, /device:TPU:0, one launch (start us, length us, event | category | flops | bytes accessed | tf_op | source)
XLA Modules:
  0.0 26.3 jit_solution(3438741330995287483)
XLA Ops:
  0.0 0.0 copy-start
  0.0 0.0 copy-start.1
  0.0 3.0 %collective-permute-start = (f32[2,8,135]{2,1,0:T(8,128)}, f32[2,8,135]{2,1,0:T(8,128)S(1)}, u32[]{:S(2)}, u32[]{:S(2)}) collective-permute-start(f32[2,8,135]{2,1,0:T(8,128)} %own.1), channel_id=1, source_target_pairs={{0,1},{1,0},{2,3},{3,2},{4,5},{5,4},{6,7},{7,6},{8,9},{9,8},{10,11... | collective-permute-start | bytes 25928 | tf_op jit(solution)/shard_map/ppermute | solution.py:449
  3.0 0.0 copy-done
  3.1 0.0 copy-done.1
  3.1 0.2 copy.8.lower
  3.3 0.2 copy.9.upper
  3.5 0.7 %shard_map.75.ahead = f32[2,8,136,256]{3,2,1,0:T(8,128)S(1)} custom-call(bf16[136,135]{1,0:T(8,128)(2,1)S(1)} %shard_map.74.unit, bf16[2,8,135,135]{3,2,1,0:T(8,128)(2,1)S(1)} %copy.8.lower), custom_call_target="tpu_custom_call" | custom-call | flops 12000000000 | tf_op jit(solution)/shard_map/pallas_call | solution.py:459
  4.3 0.0 copy-start.4
  4.3 0.0 copy-start.6
  4.3 1.8 %shard_map.76 = (f32[2,8,272,256]{3,2,1,0:T(8,128)S(1)}, f32[2,3,136,256]{3,2,1,0:T(8,128)S(1)}, f32[3,136,256]{2,1,0:T(8,128)S(1)}, f32[3,136,256]{2,1,0:T(8,128)S(1)}) custom-call(bf16[136,135]{1,0:T(8,128)(2,1)S(1)} %shard_map.74.unit, f32[2,8,136,256]{3,2,1,0:T(8,128)S(1)} %shard_map.75.ahead, bf16[2,8,135,135]{3,2,1,0:T(8,128)(2,1)S(1)} %copy.9.upper), custom_call_target="tpu_custom_call" | custom-call | flops 12000000000 | tf_op jit(solution)/shard_map/pallas_call | solution.py:462
  6.1 0.0 collective-permute-done.first
  6.1 0.1 collective-permute-start.1
  6.2 0.0 copy-done.4
  6.2 3.6 %collective-permute-start.3 = (f32[2,8,135]{2,1,0:T(8,128)S(1)}, f32[2,8,135]{2,1,0:T(8,128)S(1)}, u32[]{:S(2)}, u32[]{:S(2)}) collective-permute-start(f32[2,8,135]{2,1,0:T(8,128)S(1)} %copy-done.4), channel_id=1, source_target_pairs={{0,3},{1,2},{2,1},{3,0},{4,7},{5,6},{6,5},{7,4},{8,11},{9,10},{10,... | collective-permute-start | bytes 25928 | tf_op jit(solution)/shard_map/ppermute | solution.py:448
  9.8 0.0 collective-permute-done.1.theirs.others.refs_1_
  9.8 0.6 %shard_map.77 = (f32[136,256]{1,0:T(8,128)S(1)}, f32[3,136,256]{2,1,0:T(8,128)S(1)}, f32[440,128]{1,0:T(8,128)S(1)}) custom-call(f32[3,136,256]{2,1,0:T(8,128)S(1)} %get-tuple-element.38.mine.maps.refs_0_, f32[3,136,256]{2,1,0:T(8,128)S(1)} %collective-permute-done.1.theirs.others.refs_1_), custom_call_target="tpu_custom_call" | custom-call | tf_op jit(solution)/shard_map/pallas_call | solution.py:471
  10.4 0.0 copy-start.2
  10.4 0.0 copy-start.3
  10.4 0.0 copy-start.5
  10.5 1.6 %collective-permute-start.2 = (f32[440,128]{1,0:T(8,128)S(1)}, f32[440,128]{1,0:T(8,128)S(1)}, u32[]{:S(2)}, u32[]{:S(2)}) collective-permute-start(f32[440,128]{1,0:T(8,128)S(1)} %get-tuple-element.49.after), channel_id=1, source_target_pairs={{0,8},{4,12},{8,0},{12,4},{16,24},{20,28},{24,16},{28,20},{1,9},{5... | collective-permute-start | bytes 675848 | tf_op jit(solution)/shard_map/ppermute | solution.py:447
  12.0 0.0 copy-done.6
  12.0 0.2 copy.10.pivots
  12.2 0.0 collective-permute-done.3.second
  12.3 0.0 copy-done.2
  12.3 0.0 copy-done.3
  12.3 0.0 copy-done.5
  12.3 1.4 %shard_map.79 = (f32[2,8,135]{2,1,0:T(8,128)S(1)}, f32[2,2,8,256]{3,2,1,0:T(8,128)S(1)}, f32[8,256]{1,0:T(8,128)S(1)}, f32[8,256]{1,0:T(8,128)S(1)}) custom-call(s32[2,4]{1,0:T(2,128)S(1)} %copy-done.5, f32[2,8,135]{2,1,0:T(8,128)S(1)} %copy-done.3, f32[2,8,135]{2,1,0:T(8,128)S(1)} %copy-done.4, f32[2,8,135]{2,1,0:T(8,128)S(1)} %collective-permute-done.first, ...), custom_call_target="tpu_custom_call" | custom-call | flops 49999998976 | tf_op jit(solution)/shard_map/pallas_call | solution.py:478
  13.7 0.0 collective-permute-start.4
  13.7 1.2 %collective-permute-done.4.theirs = f32[8,256]{1,0:T(8,128)S(1)} collective-permute-done((f32[8,256]{1,0:T(8,128)S(1)}, f32[8,256]{1,0:T(8,128)S(1)}, u32[]{:S(2)}, u32[]{:S(2)}) %collective-permute-start.4) | collective-permute-done | bytes 8224 | tf_op jit(solution)/shard_map/ppermute | solution.py:447
  14.9 0.3 %shard_map.80 = (f32[8,256]{1,0:T(8,128)S(1)}, f32[2,8,256]{2,1,0:T(8,128)S(1)}) custom-call(f32[3,136,256]{2,1,0:T(8,128)S(1)} %get-tuple-element.38.mine.maps.refs_0_, f32[3,136,256]{2,1,0:T(8,128)S(1)} %collective-permute-done.1.theirs.others.refs_1_, f32[8,256]{1,0:T(8,128)S(1)} %get-tuple-element.50.mine, f32[8,256]{1,0:T(8,128)S(1)} %collective-permute-done.4.theirs), custom_call_target="tpu_custom_call" | custom-call | tf_op jit(solution)/shard_map/pallas_call | solution.py:489
  15.2 1.0 %collective-permute-start.5 = (f32[8,256]{1,0:T(8,128)S(1)}, f32[8,256]{1,0:T(8,128)S(1)}, u32[]{:S(2)}, u32[]{:S(2)}) collective-permute-start(f32[8,256]{1,0:T(8,128)S(1)} %get-tuple-element.52.vectors), channel_id=1, source_target_pairs={{0,8},{4,12},{8,0},{12,4},{16,24},{20,28},{24,16},{28,20},{1,9},{5... | collective-permute-start | bytes 24584 | tf_op jit(solution)/shard_map/ppermute | solution.py:447
  16.2 2.0 %collective-permute-done.2.theirs = f32[440,128]{1,0:T(8,128)S(1)} collective-permute-done((f32[440,128]{1,0:T(8,128)S(1)}, f32[440,128]{1,0:T(8,128)S(1)}, u32[]{:S(2)}, u32[]{:S(2)}) %collective-permute-start.2) | collective-permute-done | bytes 225312 | tf_op jit(solution)/shard_map/ppermute | solution.py:447
  18.2 0.7 %shard_map.78 = (f32[6,136,256]{2,1,0:T(8,128)S(1)}, f32[1,136,256]{2,1,0:T(8,128)}, f32[152,128]{1,0:T(8,128)S(1)}) custom-call(f32[3,136,256]{2,1,0:T(8,128)S(1)} %get-tuple-element.41.mine, f32[440,128]{1,0:T(8,128)S(1)} %collective-permute-done.2.theirs), custom_call_target="tpu_custom_call" | custom-call | flops 20000000000 | tf_op jit(solution)/shard_map/pallas_call | solution.py:498
  18.8 0.0 collective-permute-done.5.theirs
  18.8 0.2 shard_map.81
  19.0 1.6 %collective-permute-start.6 = (f32[160,128]{1,0:T(8,128)S(1)}, f32[160,128]{1,0:T(8,128)S(1)}, u32[]{:S(2)}, u32[]{:S(2)}) collective-permute-start(f32[160,128]{1,0:T(8,128)S(1)} %get-tuple-element.54), channel_id=1, source_target_pairs={{0,16},{4,20},{8,24},{12,28},{16,0},{20,4},{24,8},{28,12},{1,17},{... | collective-permute-start | bytes 245768 | tf_op jit(solution)/shard_map/ppermute | solution.py:447
  20.6 0.5 %shard_map.82 = (bf16[4,136,256]{2,1,0:T(8,128)(2,1)S(1)}, bf16[4,136,256]{2,1,0:T(8,128)(2,1)S(1)}, f32[4,8,256]{2,1,0:T(8,128)S(1)}) custom-call(f32[3,136,256]{2,1,0:T(8,128)S(1)} %get-tuple-element.38.mine.maps.refs_0_, f32[3,136,256]{2,1,0:T(8,128)S(1)} %collective-permute-done.1.theirs.others.refs_1_, f32[136,256]{1,0:T(8,128)S(1)} %get-tuple-element.55.refs_2_, ...), custom_call_target="tpu_custom_call" | custom-call | flops 3000000000 | tf_op jit(solution)/shard_map/pallas_call | solution.py:515
  21.1 2.4 %collective-permute-done.6.theirs = f32[160,128]{1,0:T(8,128)S(1)} collective-permute-done((f32[160,128]{1,0:T(8,128)S(1)}, f32[160,128]{1,0:T(8,128)S(1)}, u32[]{:S(2)}, u32[]{:S(2)}) %collective-permute-start.6) | collective-permute-done | bytes 81952 | tf_op jit(solution)/shard_map/ppermute | solution.py:447
  23.5 0.4 %shard_map.83 = (f32[2,8,256]{2,1,0:T(8,128)S(1)}, f32[2,8,256]{2,1,0:T(8,128)S(1)}) custom-call(f32[8,256]{1,0:T(8,128)S(1)} %get-tuple-element.53.vectors, f32[160,128]{1,0:T(8,128)S(1)} %collective-permute-done.6.theirs, bf16[4,136,256]{2,1,0:T(8,128)(2,1)S(1)} %get-tuple-element.58.hi, bf16[4,136,256]{2,1,0:T(8,128)(2,1)S(1)} %get-tuple-element.59.lo, ...), custom_call_target="tpu_custom_call" | custom-call | tf_op jit(solution)/shard_map/pallas_call | solution.py:521
  23.9 0.1 collective-permute-start.7
  24.0 0.5 %shard_map.84.own = f32[8,135]{1,0:T(8,128)S(1)} custom-call(f32[2,8,256]{2,1,0:T(8,128)S(1)} %get-tuple-element.62.ends, f32[2,8,135]{2,1,0:T(8,128)S(1)} %get-tuple-element.63.inner, f32[2,8,272,256]{3,2,1,0:T(8,128)S(1)} %get-tuple-element.47.tail, f32[2,3,136,256]{3,2,1,0:T(8,128)S(1)} %get-tuple-element.48.half, f32[2,2,8,256]{3,2,1,0:T(8,128)S(1)} %get-tuple-element.64.bias), custom_call_target="tpu_custom_call" | custom-call | flops 2000000000 | tf_op jit(solution)/shard_map/pallas_call | solution.py:525
  24.6 0.6 %collective-permute-done.7.ends = f32[2,8,256]{2,1,0:T(8,128)S(1)} collective-permute-done((f32[2,8,256]{2,1,0:T(8,128)S(1)}, f32[2,8,256]{2,1,0:T(8,128)S(1)}, u32[]{:S(2)}, u32[]{:S(2)}) %collective-permute-start.7) | collective-permute-done | bytes 16416 | tf_op jit(solution)/shard_map/ppermute | solution.py:447
  25.2 1.1 %shard_map.85 = f32[2,8,135]{2,1,0:T(8,128)} custom-call(f32[2,8,256]{2,1,0:T(8,128)S(1)} %collective-permute-done.7.ends, f32[8,135]{1,0:T(8,128)S(1)} %shard_map.84.own, f32[2,8,135]{2,1,0:T(8,128)S(1)} %get-tuple-element.63.inner, f32[2,8,272,256]{3,2,1,0:T(8,128)S(1)} %get-tuple-element.47.tail, f32[2,3,136,256]{3,2,1,0:T(8,128)S(1)} %get-tuple-element.48.half, ...), custom_call_target="tpu_custom_call" | custom-call | tf_op jit(solution)/shard_map/pallas_call | solution.py:528
  (2 shorter events, 0.0 us)
Async XLA Ops:
  0.0 3.0 %copy-start = (bf16[2,8,135,135]{3,1,2,0:T(8,128)(2,1)S(1)}, bf16[2,8,135,135]{3,1,2,0:T(8,128)(2,1)}, u32[]{:S(2)}) copy-start(bf16[2,8,135,135]{3,1,2,0:T(8,128)(2,1)} %param.12) | copy-start | bytes 1749604
  0.0 3.1 %copy-start.1 = (bf16[2,8,135,135]{3,1,2,0:T(8,128)(2,1)S(1)}, bf16[2,8,135,135]{3,1,2,0:T(8,128)(2,1)}, u32[]{:S(2)}) copy-start(bf16[2,8,135,135]{3,1,2,0:T(8,128)(2,1)} %param.13) | copy-start | bytes 1749604
  0.0 6.1 %collective-permute-start = (f32[2,8,135]{2,1,0:T(8,128)}, f32[2,8,135]{2,1,0:T(8,128)S(1)}, u32[]{:S(2)}, u32[]{:S(2)}) collective-permute-start(f32[2,8,135]{2,1,0:T(8,128)} %own.1), channel_id=1, source_target_pairs={{0,1},{1,0},{2,3},{3,2},{4,5},{5,4},{6,7},{7,6},{8,9},{9,8},{10,11... | collective-permute-start | bytes 25928 | tf_op jit(solution)/shard_map/ppermute | solution.py:449
  4.3 1.9 %copy-start.4 = (f32[2,8,135]{2,1,0:T(8,128)S(1)}, f32[2,8,135]{2,1,0:T(8,128)}, u32[]{:S(2)}) copy-start(f32[2,8,135]{2,1,0:T(8,128)} %own.1) | copy-start | bytes 25924
  4.3 7.7 %copy-start.6 = (bf16[2,8,135,135]{3,1,2,0:T(8,128)(2,1)S(1)}, bf16[2,8,135,135]{3,1,2,0:T(8,128)(2,1)}, u32[]{:S(2)}) copy-start(bf16[2,8,135,135]{3,1,2,0:T(8,128)(2,1)} %param.11) | copy-start | bytes 1749604
  6.1 3.7 %collective-permute-start.1 = (f32[3,136,256]{2,1,0:T(8,128)S(1)}, f32[3,136,256]{2,1,0:T(8,128)S(1)}, u32[]{:S(2)}, u32[]{:S(2)}) collective-permute-start(f32[3,136,256]{2,1,0:T(8,128)S(1)} %get-tuple-element.40), channel_id=1, source_target_pairs={{0,4},{4,0},{8,12},{12,8},{16,20},{20,16},{24,28},{28,24},{1,5},{5... | collective-permute-start | bytes 1253384 | tf_op jit(solution)/shard_map/ppermute | solution.py:447
  6.2 6.1 %collective-permute-start.3 = (f32[2,8,135]{2,1,0:T(8,128)S(1)}, f32[2,8,135]{2,1,0:T(8,128)S(1)}, u32[]{:S(2)}, u32[]{:S(2)}) collective-permute-start(f32[2,8,135]{2,1,0:T(8,128)S(1)} %copy-done.4), channel_id=1, source_target_pairs={{0,3},{1,2},{2,1},{3,0},{4,7},{5,6},{6,5},{7,4},{8,11},{9,10},{10,... | collective-permute-start | bytes 25928 | tf_op jit(solution)/shard_map/ppermute | solution.py:448
  10.4 1.8 %copy-start.2 = (f32[2,8,4,135]{3,2,1,0:T(4,128)S(1)}, f32[2,8,4,135]{3,2,1,0:T(4,128)}, u32[]{:S(2)}) copy-start(f32[2,8,4,135]{3,2,1,0:T(4,128)} %coupling.1) | copy-start | bytes 103684
  10.4 1.8 %copy-start.3 = (f32[2,8,135]{2,1,0:T(8,128)S(1)}, f32[2,8,135]{2,1,0:T(8,128)}, u32[]{:S(2)}) copy-start(f32[2,8,135]{2,1,0:T(8,128)} %right.1) | copy-start | bytes 25924
  10.4 1.8 %copy-start.5 = (s32[2,4]{1,0:T(2,128)S(1)}, s32[2,4]{1,0:T(2,128)}, u32[]{:S(2)}) copy-start(s32[2,4]{1,0:T(2,128)} %neighbours.1) | copy-start | bytes 100
  10.5 7.7 %collective-permute-start.2 = (f32[440,128]{1,0:T(8,128)S(1)}, f32[440,128]{1,0:T(8,128)S(1)}, u32[]{:S(2)}, u32[]{:S(2)}) collective-permute-start(f32[440,128]{1,0:T(8,128)S(1)} %get-tuple-element.49.after), channel_id=1, source_target_pairs={{0,8},{4,12},{8,0},{12,4},{16,24},{20,28},{24,16},{28,20},{1,9},{5... | collective-permute-start | bytes 675848 | tf_op jit(solution)/shard_map/ppermute | solution.py:447
  13.7 1.2 %collective-permute-start.4 = (f32[8,256]{1,0:T(8,128)S(1)}, f32[8,256]{1,0:T(8,128)S(1)}, u32[]{:S(2)}, u32[]{:S(2)}) collective-permute-start(f32[8,256]{1,0:T(8,128)S(1)} %get-tuple-element.51), channel_id=1, source_target_pairs={{0,4},{4,0},{8,12},{12,8},{16,20},{20,16},{24,28},{28,24},{1,5},{5... | collective-permute-start | bytes 24584 | tf_op jit(solution)/shard_map/ppermute | solution.py:447
  15.2 3.7 %collective-permute-start.5 = (f32[8,256]{1,0:T(8,128)S(1)}, f32[8,256]{1,0:T(8,128)S(1)}, u32[]{:S(2)}, u32[]{:S(2)}) collective-permute-start(f32[8,256]{1,0:T(8,128)S(1)} %get-tuple-element.52.vectors), channel_id=1, source_target_pairs={{0,8},{4,12},{8,0},{12,4},{16,24},{20,28},{24,16},{28,20},{1,9},{5... | collective-permute-start | bytes 24584 | tf_op jit(solution)/shard_map/ppermute | solution.py:447
  19.0 4.5 %collective-permute-start.6 = (f32[160,128]{1,0:T(8,128)S(1)}, f32[160,128]{1,0:T(8,128)S(1)}, u32[]{:S(2)}, u32[]{:S(2)}) collective-permute-start(f32[160,128]{1,0:T(8,128)S(1)} %get-tuple-element.54), channel_id=1, source_target_pairs={{0,16},{4,20},{8,24},{12,28},{16,0},{20,4},{24,8},{28,12},{1,17},{... | collective-permute-start | bytes 245768 | tf_op jit(solution)/shard_map/ppermute | solution.py:447
  23.9 1.2 %collective-permute-start.7 = (f32[2,8,256]{2,1,0:T(8,128)S(1)}, f32[2,8,256]{2,1,0:T(8,128)S(1)}, u32[]{:S(2)}, u32[]{:S(2)}) collective-permute-start(f32[2,8,256]{2,1,0:T(8,128)S(1)} %get-tuple-element.61), channel_id=1, source_target_pairs={{0,4},{4,0},{8,12},{12,8},{16,20},{20,16},{24,28},{28,24},{1,5},{5... | collective-permute-start | bytes 49160 | tf_op jit(solution)/shard_map/ppermute | solution.py:447

commit v6 on v5

--- a/solution.py
+++ b/solution.py
@@ -260,7 +260,7 @@
     bias[1] = joint[2]
 
 
-def level_maps_kernel(level, lean, mine, theirs, down, full, pack):
+def level_maps_kernel(level, lean, mine, theirs, down, pack, full=None):
     high = mine.shape[1]
     maps = unpacked(theirs, 3, high)
     s = side(level)
@@ -392,6 +392,7 @@
     for k, v in enumerate([y, between, middle, c]):
         gathered = jnp.where(index == k, v, gathered)
     columns = jnp.transpose(gathered)[:high]
+    columns = [jnp.broadcast_to(columns[:, k : k + 1], (high, 128)) for k in range(4)]
     parts = []
     for h in range(2):
         at = slice(128 * h, min(width, 128 * h + 128))
@@ -399,8 +400,8 @@
         for i in range(cells):
             k = 2 * (i // per)
             t = (
-                tail[line, i, :high, 128 * h : 128 * h + 128] * columns[:, k : k + 1]
-                + tail[line, i, high:, 128 * h : 128 * h + 128] * columns[:, k + 1 : k + 2]
+                tail[line, i, :high, 128 * h : 128 * h + 128] * columns[k]
+                + tail[line, i, high:, 128 * h : 128 * h + 128] * columns[k + 1]
             )
             sums.append(jnp.sum(t, axis=0, keepdims=True)[:, : at.stop - at.start])
         parts.append((at, jnp.concatenate(sums, axis=0) + inner[line, :, at]))
@@ -495,15 +496,15 @@
     for k in range(1, levels - 1):
         lean = k == levels - 2
         count_maps = 1 if lean else 3
-        down, mine, pack = call(
+        down, pack, *joint = call(
             functools.partial(level_maps_kernel, k, lean),
             [
-                f32(6, high, LANES), f32(1 if lean else 3, high, LANES),
-                f32(length(count_maps, high), 128),
-            ],
+                f32(6, high, LANES), f32(length(count_maps, high), 128),
+            ] + ([] if lean else [full]),
             [VMEM] * 2,
             flops=20000000000,
         )(mine, theirs)
+        mine = None if lean else joint[0]
         pack, bias, vectors = call(
             functools.partial(level_vectors_kernel, k, k == 1),
             [f32(length(count_maps, high) + 8, 128), f32(2, 8, LANES), row],

time: 26.5 us -> 26.4 us (level)
  transfers between devices with their start and end apart: 8 -> 8, of which waited for: 4 -> 5; matrix products, arithmetic and copies ran while one was open for 3% -> 3% of each run, Pallas kernels for 25% -> 24%
where the time goes in v6:
time: 26.4 us; the launch traced here: 26.3 us
  starting transfers between devices  10.9 us (41%)
  Pallas kernels  8.14 us (31%)
  waiting for transfers between devices  6.33 us (24%)
  local copies, waits for them, and re-layouts  0.7 us (3%)
    ppermute x6, waiting for transfers between devices, shards(): lax.ppermute(a, 'line', [(i, i ^ 1 << k) for i in range(count)])  6.32 us
    ppermute x6, starting transfers between devices, shards(): lax.ppermute(a, 'line', [(i, i ^ 1 << k) for i in range(count)])  4.3 us
    ppermute x1, starting transfers between devices, shards(): second = lax.ppermute(previous, 'surf', odd)  3.62 us
    ppermute x1, starting transfers between devices, shards(): first = lax.ppermute(previous, 'surf', pairs)  3.02 us
    pallas_call x1, Pallas kernels, shards(): call(maps_kernel, [f32(rows, cells, 2 * high, LANES), f32(rows, 3, high,...  1.78 us
    pallas_call x1, Pallas kernels, shards(): call(functools.partial(segment_kernel, patches), [f32(rows, cells, width)...  1.43 us
    pallas_call x1, Pallas kernels, shards(): call(final_kernel, [f32(rows, cells, width)], [VMEM] * 6)  1.13 us
    pallas_call x1, Pallas kernels, shards(): call(ahead_kernel, [f32(rows, cells, high, LANES)], [VMEM] * 2, flops=120...  0.73 us
  transfers between devices with their start and end apart: 8, of which 5 were waited for; matrix products, arithmetic and copies ran while one was open for 3% of the time, Pallas kernels for 24%

profile of v6, /device:TPU:0, one launch (start us, length us, event | category | flops | bytes accessed | tf_op | source)
XLA Modules:
  0.0 26.3 jit_solution(9936385024217983791)
XLA Ops:
  0.0 0.0 copy-start
  0.0 0.0 copy-start.1
  0.0 3.0 %collective-permute-start = (f32[2,8,135]{2,1,0:T(8,128)}, f32[2,8,135]{2,1,0:T(8,128)S(1)}, u32[]{:S(2)}, u32[]{:S(2)}) collective-permute-start(f32[2,8,135]{2,1,0:T(8,128)} %own.1), channel_id=1, source_target_pairs={{0,1},{1,0},{2,3},{3,2},{4,5},{5,4},{6,7},{7,6},{8,9},{9,8},{10,11... | collective-permute-start | bytes 25928 | tf_op jit(solution)/shard_map/ppermute | solution.py:450
  3.0 0.0 copy-done
  3.1 0.0 copy-done.1
  3.1 0.2 copy.8.lower
  3.3 0.2 copy.9.upper
  3.5 0.7 %shard_map.75.ahead = f32[2,8,136,256]{3,2,1,0:T(8,128)S(1)} custom-call(bf16[136,135]{1,0:T(8,128)(2,1)S(1)} %shard_map.74.unit, bf16[2,8,135,135]{3,2,1,0:T(8,128)(2,1)S(1)} %copy.8.lower), custom_call_target="tpu_custom_call" | custom-call | flops 12000000000 | tf_op jit(solution)/shard_map/pallas_call | solution.py:460
  4.3 0.0 copy-start.4
  4.3 0.0 copy-start.6
  4.3 1.8 %shard_map.76 = (f32[2,8,272,256]{3,2,1,0:T(8,128)S(1)}, f32[2,3,136,256]{3,2,1,0:T(8,128)S(1)}, f32[3,136,256]{2,1,0:T(8,128)S(1)}, f32[3,136,256]{2,1,0:T(8,128)S(1)}) custom-call(bf16[136,135]{1,0:T(8,128)(2,1)S(1)} %shard_map.74.unit, f32[2,8,136,256]{3,2,1,0:T(8,128)S(1)} %shard_map.75.ahead, bf16[2,8,135,135]{3,2,1,0:T(8,128)(2,1)S(1)} %copy.9.upper), custom_call_target="tpu_custom_call" | custom-call | flops 12000000000 | tf_op jit(solution)/shard_map/pallas_call | solution.py:463
  6.1 0.0 collective-permute-done.first
  6.1 0.1 collective-permute-start.1
  6.2 0.0 copy-done.4
  6.2 3.6 %collective-permute-start.3 = (f32[2,8,135]{2,1,0:T(8,128)S(1)}, f32[2,8,135]{2,1,0:T(8,128)S(1)}, u32[]{:S(2)}, u32[]{:S(2)}) collective-permute-start(f32[2,8,135]{2,1,0:T(8,128)S(1)} %copy-done.4), channel_id=1, source_target_pairs={{0,3},{1,2},{2,1},{3,0},{4,7},{5,6},{6,5},{7,4},{8,11},{9,10},{10,... | collective-permute-start | bytes 25928 | tf_op jit(solution)/shard_map/ppermute | solution.py:449
  9.8 0.0 collective-permute-done.1.theirs.others.refs_1_
  9.8 0.6 %shard_map.77 = (f32[136,256]{1,0:T(8,128)S(1)}, f32[3,136,256]{2,1,0:T(8,128)S(1)}, f32[440,128]{1,0:T(8,128)S(1)}) custom-call(f32[3,136,256]{2,1,0:T(8,128)S(1)} %get-tuple-element.38.mine.maps.refs_0_, f32[3,136,256]{2,1,0:T(8,128)S(1)} %collective-permute-done.1.theirs.others.refs_1_), custom_call_target="tpu_custom_call" | custom-call | tf_op jit(solution)/shard_map/pallas_call | solution.py:472
  10.4 0.0 copy-start.2
  10.4 0.0 copy-start.3
  10.4 0.0 copy-start.5
  10.5 1.6 %collective-permute-start.2 = (f32[440,128]{1,0:T(8,128)S(1)}, f32[440,128]{1,0:T(8,128)S(1)}, u32[]{:S(2)}, u32[]{:S(2)}) collective-permute-start(f32[440,128]{1,0:T(8,128)S(1)} %get-tuple-element.49.after), channel_id=1, source_target_pairs={{0,8},{4,12},{8,0},{12,4},{16,24},{20,28},{24,16},{28,20},{1,9},{5... | collective-permute-start | bytes 675848 | tf_op jit(solution)/shard_map/ppermute | solution.py:448
  12.0 0.0 copy-done.6
  12.0 0.2 copy.10.pivots
  12.2 0.0 collective-permute-done.3.second
  12.3 0.0 copy-done.2
  12.3 0.0 copy-done.3
  12.3 0.0 copy-done.5
  12.3 1.4 %shard_map.79 = (f32[2,8,135]{2,1,0:T(8,128)S(1)}, f32[2,2,8,256]{3,2,1,0:T(8,128)S(1)}, f32[8,256]{1,0:T(8,128)S(1)}, f32[8,256]{1,0:T(8,128)S(1)}) custom-call(s32[2,4]{1,0:T(2,128)S(1)} %copy-done.5, f32[2,8,135]{2,1,0:T(8,128)S(1)} %copy-done.3, f32[2,8,135]{2,1,0:T(8,128)S(1)} %copy-done.4, f32[2,8,135]{2,1,0:T(8,128)S(1)} %collective-permute-done.first, ...), custom_call_target="tpu_custom_call" | custom-call | flops 49999998976 | tf_op jit(solution)/shard_map/pallas_call | solution.py:479
  13.7 0.0 collective-permute-start.4
  13.7 1.2 %collective-permute-done.4.theirs = f32[8,256]{1,0:T(8,128)S(1)} collective-permute-done((f32[8,256]{1,0:T(8,128)S(1)}, f32[8,256]{1,0:T(8,128)S(1)}, u32[]{:S(2)}, u32[]{:S(2)}) %collective-permute-start.4) | collective-permute-done | bytes 8224 | tf_op jit(solution)/shard_map/ppermute | solution.py:448
  14.9 0.3 %shard_map.80 = (f32[8,256]{1,0:T(8,128)S(1)}, f32[2,8,256]{2,1,0:T(8,128)S(1)}) custom-call(f32[3,136,256]{2,1,0:T(8,128)S(1)} %get-tuple-element.38.mine.maps.refs_0_, f32[3,136,256]{2,1,0:T(8,128)S(1)} %collective-permute-done.1.theirs.others.refs_1_, f32[8,256]{1,0:T(8,128)S(1)} %get-tuple-element.50.mine, f32[8,256]{1,0:T(8,128)S(1)} %collective-permute-done.4.theirs), custom_call_target="tpu_custom_call" | custom-call | tf_op jit(solution)/shard_map/pallas_call | solution.py:490
  15.2 1.0 %collective-permute-start.5 = (f32[8,256]{1,0:T(8,128)S(1)}, f32[8,256]{1,0:T(8,128)S(1)}, u32[]{:S(2)}, u32[]{:S(2)}) collective-permute-start(f32[8,256]{1,0:T(8,128)S(1)} %get-tuple-element.52.vectors), channel_id=1, source_target_pairs={{0,8},{4,12},{8,0},{12,4},{16,24},{20,28},{24,16},{28,20},{1,9},{5... | collective-permute-start | bytes 24584 | tf_op jit(solution)/shard_map/ppermute | solution.py:448
  16.2 2.0 %collective-permute-done.2.theirs = f32[440,128]{1,0:T(8,128)S(1)} collective-permute-done((f32[440,128]{1,0:T(8,128)S(1)}, f32[440,128]{1,0:T(8,128)S(1)}, u32[]{:S(2)}, u32[]{:S(2)}) %collective-permute-start.2) | collective-permute-done | bytes 225312 | tf_op jit(solution)/shard_map/ppermute | solution.py:448
  18.2 0.6 %shard_map.78 = (f32[6,136,256]{2,1,0:T(8,128)S(1)}, f32[152,128]{1,0:T(8,128)S(1)}) custom-call(f32[3,136,256]{2,1,0:T(8,128)S(1)} %get-tuple-element.41.mine, f32[440,128]{1,0:T(8,128)S(1)} %collective-permute-done.2.theirs), custom_call_target="tpu_custom_call" | custom-call | flops 20000000000 | tf_op jit(solution)/shard_map/pallas_call | solution.py:499
  18.8 0.1 collective-permute-done.5.theirs
  18.8 0.2 shard_map.81
  19.0 1.6 %collective-permute-start.6 = (f32[160,128]{1,0:T(8,128)S(1)}, f32[160,128]{1,0:T(8,128)S(1)}, u32[]{:S(2)}, u32[]{:S(2)}) collective-permute-start(f32[160,128]{1,0:T(8,128)S(1)} %get-tuple-element.54), channel_id=1, source_target_pairs={{0,16},{4,20},{8,24},{12,28},{16,0},{20,4},{24,8},{28,12},{1,17},{... | collective-permute-start | bytes 245768 | tf_op jit(solution)/shard_map/ppermute | solution.py:448
  20.6 0.5 %shard_map.82 = (bf16[4,136,256]{2,1,0:T(8,128)(2,1)S(1)}, bf16[4,136,256]{2,1,0:T(8,128)(2,1)S(1)}, f32[4,8,256]{2,1,0:T(8,128)S(1)}) custom-call(f32[3,136,256]{2,1,0:T(8,128)S(1)} %get-tuple-element.38.mine.maps.refs_0_, f32[3,136,256]{2,1,0:T(8,128)S(1)} %collective-permute-done.1.theirs.others.refs_1_, f32[136,256]{1,0:T(8,128)S(1)} %get-tuple-element.55.refs_2_, ...), custom_call_target="tpu_custom_call" | custom-call | flops 3000000000 | tf_op jit(solution)/shard_map/pallas_call | solution.py:516
  21.1 2.4 %collective-permute-done.6.theirs = f32[160,128]{1,0:T(8,128)S(1)} collective-permute-done((f32[160,128]{1,0:T(8,128)S(1)}, f32[160,128]{1,0:T(8,128)S(1)}, u32[]{:S(2)}, u32[]{:S(2)}) %collective-permute-start.6) | collective-permute-done | bytes 81952 | tf_op jit(solution)/shard_map/ppermute | solution.py:448
  23.5 0.4 %shard_map.83 = (f32[2,8,256]{2,1,0:T(8,128)S(1)}, f32[2,8,256]{2,1,0:T(8,128)S(1)}) custom-call(f32[8,256]{1,0:T(8,128)S(1)} %get-tuple-element.53.vectors, f32[160,128]{1,0:T(8,128)S(1)} %collective-permute-done.6.theirs, bf16[4,136,256]{2,1,0:T(8,128)(2,1)S(1)} %get-tuple-element.58.hi, bf16[4,136,256]{2,1,0:T(8,128)(2,1)S(1)} %get-tuple-element.59.lo, ...), custom_call_target="tpu_custom_call" | custom-call | tf_op jit(solution)/shard_map/pallas_call | solution.py:522
  23.9 0.1 collective-permute-start.7
  24.0 0.5 %shard_map.84.own = f32[8,135]{1,0:T(8,128)S(1)} custom-call(f32[2,8,256]{2,1,0:T(8,128)S(1)} %get-tuple-element.62.ends, f32[2,8,135]{2,1,0:T(8,128)S(1)} %get-tuple-element.63.inner, f32[2,8,272,256]{3,2,1,0:T(8,128)S(1)} %get-tuple-element.47.tail, f32[2,3,136,256]{3,2,1,0:T(8,128)S(1)} %get-tuple-element.48.half, f32[2,2,8,256]{3,2,1,0:T(8,128)S(1)} %get-tuple-element.64.bias), custom_call_target="tpu_custom_call" | custom-call | flops 2000000000 | tf_op jit(solution)/shard_map/pallas_call | solution.py:526
  24.5 0.6 %collective-permute-done.7.ends = f32[2,8,256]{2,1,0:T(8,128)S(1)} collective-permute-done((f32[2,8,256]{2,1,0:T(8,128)S(1)}, f32[2,8,256]{2,1,0:T(8,128)S(1)}, u32[]{:S(2)}, u32[]{:S(2)}) %collective-permute-start.7) | collective-permute-done | bytes 16416 | tf_op jit(solution)/shard_map/ppermute | solution.py:448
  25.2 1.1 %shard_map.85 = f32[2,8,135]{2,1,0:T(8,128)} custom-call(f32[2,8,256]{2,1,0:T(8,128)S(1)} %collective-permute-done.7.ends, f32[8,135]{1,0:T(8,128)S(1)} %shard_map.84.own, f32[2,8,135]{2,1,0:T(8,128)S(1)} %get-tuple-element.63.inner, f32[2,8,272,256]{3,2,1,0:T(8,128)S(1)} %get-tuple-element.47.tail, f32[2,3,136,256]{3,2,1,0:T(8,128)S(1)} %get-tuple-element.48.half, ...), custom_call_target="tpu_custom_call" | custom-call | tf_op jit(solution)/shard_map/pallas_call | solution.py:529
  (2 shorter events, 0.0 us)
Async XLA Ops:
  0.0 3.0 %copy-start = (bf16[2,8,135,135]{3,1,2,0:T(8,128)(2,1)S(1)}, bf16[2,8,135,135]{3,1,2,0:T(8,128)(2,1)}, u32[]{:S(2)}) copy-start(bf16[2,8,135,135]{3,1,2,0:T(8,128)(2,1)} %param.12) | copy-start | bytes 1749604
  0.0 3.1 %copy-start.1 = (bf16[2,8,135,135]{3,1,2,0:T(8,128)(2,1)S(1)}, bf16[2,8,135,135]{3,1,2,0:T(8,128)(2,1)}, u32[]{:S(2)}) copy-start(bf16[2,8,135,135]{3,1,2,0:T(8,128)(2,1)} %param.13) | copy-start | bytes 1749604
  0.0 6.1 %collective-permute-start = (f32[2,8,135]{2,1,0:T(8,128)}, f32[2,8,135]{2,1,0:T(8,128)S(1)}, u32[]{:S(2)}, u32[]{:S(2)}) collective-permute-start(f32[2,8,135]{2,1,0:T(8,128)} %own.1), channel_id=1, source_target_pairs={{0,1},{1,0},{2,3},{3,2},{4,5},{5,4},{6,7},{7,6},{8,9},{9,8},{10,11... | collective-permute-start | bytes 25928 | tf_op jit(solution)/shard_map/ppermute | solution.py:450
  4.3 1.9 %copy-start.4 = (f32[2,8,135]{2,1,0:T(8,128)S(1)}, f32[2,8,135]{2,1,0:T(8,128)}, u32[]{:S(2)}) copy-start(f32[2,8,135]{2,1,0:T(8,128)} %own.1) | copy-start | bytes 25924
  4.3 7.7 %copy-start.6 = (bf16[2,8,135,135]{3,1,2,0:T(8,128)(2,1)S(1)}, bf16[2,8,135,135]{3,1,2,0:T(8,128)(2,1)}, u32[]{:S(2)}) copy-start(bf16[2,8,135,135]{3,1,2,0:T(8,128)(2,1)} %param.11) | copy-start | bytes 1749604
  6.1 3.7 %collective-permute-start.1 = (f32[3,136,256]{2,1,0:T(8,128)S(1)}, f32[3,136,256]{2,1,0:T(8,128)S(1)}, u32[]{:S(2)}, u32[]{:S(2)}) collective-permute-start(f32[3,136,256]{2,1,0:T(8,128)S(1)} %get-tuple-element.40), channel_id=1, source_target_pairs={{0,4},{4,0},{8,12},{12,8},{16,20},{20,16},{24,28},{28,24},{1,5},{5... | collective-permute-start | bytes 1253384 | tf_op jit(solution)/shard_map/ppermute | solution.py:448
  6.2 6.1 %collective-permute-start.3 = (f32[2,8,135]{2,1,0:T(8,128)S(1)}, f32[2,8,135]{2,1,0:T(8,128)S(1)}, u32[]{:S(2)}, u32[]{:S(2)}) collective-permute-start(f32[2,8,135]{2,1,0:T(8,128)S(1)} %copy-done.4), channel_id=1, source_target_pairs={{0,3},{1,2},{2,1},{3,0},{4,7},{5,6},{6,5},{7,4},{8,11},{9,10},{10,... | collective-permute-start | bytes 25928 | tf_op jit(solution)/shard_map/ppermute | solution.py:449
  10.4 1.8 %copy-start.2 = (f32[2,8,4,135]{3,2,1,0:T(4,128)S(1)}, f32[2,8,4,135]{3,2,1,0:T(4,128)}, u32[]{:S(2)}) copy-start(f32[2,8,4,135]{3,2,1,0:T(4,128)} %coupling.1) | copy-start | bytes 103684
  10.4 1.8 %copy-start.3 = (f32[2,8,135]{2,1,0:T(8,128)S(1)}, f32[2,8,135]{2,1,0:T(8,128)}, u32[]{:S(2)}) copy-start(f32[2,8,135]{2,1,0:T(8,128)} %right.1) | copy-start | bytes 25924
  10.4 1.8 %copy-start.5 = (s32[2,4]{1,0:T(2,128)S(1)}, s32[2,4]{1,0:T(2,128)}, u32[]{:S(2)}) copy-start(s32[2,4]{1,0:T(2,128)} %neighbours.1) | copy-start | bytes 100
  10.5 7.7 %collective-permute-start.2 = (f32[440,128]{1,0:T(8,128)S(1)}, f32[440,128]{1,0:T(8,128)S(1)}, u32[]{:S(2)}, u32[]{:S(2)}) collective-permute-start(f32[440,128]{1,0:T(8,128)S(1)} %get-tuple-element.49.after), channel_id=1, source_target_pairs={{0,8},{4,12},{8,0},{12,4},{16,24},{20,28},{24,16},{28,20},{1,9},{5... | collective-permute-start | bytes 675848 | tf_op jit(solution)/shard_map/ppermute | solution.py:448
  13.7 1.2 %collective-permute-start.4 = (f32[8,256]{1,0:T(8,128)S(1)}, f32[8,256]{1,0:T(8,128)S(1)}, u32[]{:S(2)}, u32[]{:S(2)}) collective-permute-start(f32[8,256]{1,0:T(8,128)S(1)} %get-tuple-element.51), channel_id=1, source_target_pairs={{0,4},{4,0},{8,12},{12,8},{16,20},{20,16},{24,28},{28,24},{1,5},{5... | collective-permute-start | bytes 24584 | tf_op jit(solution)/shard_map/ppermute | solution.py:448
  15.2 3.7 %collective-permute-start.5 = (f32[8,256]{1,0:T(8,128)S(1)}, f32[8,256]{1,0:T(8,128)S(1)}, u32[]{:S(2)}, u32[]{:S(2)}) collective-permute-start(f32[8,256]{1,0:T(8,128)S(1)} %get-tuple-element.52.vectors), channel_id=1, source_target_pairs={{0,8},{4,12},{8,0},{12,4},{16,24},{20,28},{24,16},{28,20},{1,9},{5... | collective-permute-start | bytes 24584 | tf_op jit(solution)/shard_map/ppermute | solution.py:448
  19.0 4.5 %collective-permute-start.6 = (f32[160,128]{1,0:T(8,128)S(1)}, f32[160,128]{1,0:T(8,128)S(1)}, u32[]{:S(2)}, u32[]{:S(2)}) collective-permute-start(f32[160,128]{1,0:T(8,128)S(1)} %get-tuple-element.54), channel_id=1, source_target_pairs={{0,16},{4,20},{8,24},{12,28},{16,0},{20,4},{24,8},{28,12},{1,17},{... | collective-permute-start | bytes 245768 | tf_op jit(solution)/shard_map/ppermute | solution.py:448
  23.9 1.2 %collective-permute-start.7 = (f32[2,8,256]{2,1,0:T(8,128)S(1)}, f32[2,8,256]{2,1,0:T(8,128)S(1)}, u32[]{:S(2)}, u32[]{:S(2)}) collective-permute-start(f32[2,8,256]{2,1,0:T(8,128)S(1)} %get-tuple-element.61), channel_id=1, source_target_pairs={{0,4},{4,0},{8,12},{12,8},{16,20},{20,16},{24,28},{28,24},{1,5},{5... | collective-permute-start | bytes 49160 | tf_op jit(solution)/shard_map/ppermute | solution.py:448

commit v7 on v6

--- a/solution.py
+++ b/solution.py
@@ -99,7 +99,7 @@
                 ahead[l, p * per + j, :, :width] = now[l, p]
 
 
-def maps_kernel(unit, ahead, upper, tail, half, keep, send):
+def maps_kernel(unit, ahead, upper, right, own, coupling, neighbours, tail, half, keep, send):
     rows, cells, width, _ = upper.shape
     high = keep.shape[1]
     per = cells // 2
@@ -463,9 +463,9 @@
     tail, half, keep, send = call(
         maps_kernel,
         [f32(rows, cells, 2 * high, LANES), f32(rows, 3, high, LANES), full, full],
-        [VMEM] * 3,
+        [VMEM] * 7,
         flops=12000000000,
-    )(unit, ahead, upper_factor)
+    )(unit, ahead, upper_factor, right_side, previous, coupling, neighbours)
     send, first = lax.optimization_barrier((send, first))
     theirs = swap(send, 0)
     first_maps = keep, theirs

time: 26.4 us -> 26.5 us (level)
  transfers between devices with their start and end apart: 8 -> 8, of which waited for: 5 -> 4; matrix products, arithmetic and copies ran while one was open for 3% -> 3% of each run, Pallas kernels for 24% -> 25%
where the time goes in v7:
time: 26.5 us; the launch traced here: 26.3 us
  starting transfers between devices  11 us (42%)
  Pallas kernels  8.18 us (31%)
  waiting for transfers between devices  6.26 us (24%)
  local copies, waits for them, and re-layouts  0.76 us (3%)
    ppermute x6, waiting for transfers between devices, shards(): lax.ppermute(a, 'line', [(i, i ^ 1 << k) for i in range(count)])  6.25 us
    ppermute x6, starting transfers between devices, shards(): lax.ppermute(a, 'line', [(i, i ^ 1 << k) for i in range(count)])  4.36 us
    ppermute x1, starting transfers between devices, shards(): second = lax.ppermute(previous, 'surf', odd)  3.6 us
    ppermute x1, starting transfers between devices, shards(): first = lax.ppermute(previous, 'surf', pairs)  3.02 us
    pallas_call x1, Pallas kernels, shards(): call(maps_kernel, [f32(rows, cells, 2 * high, LANES), f32(rows, 3, high,...  1.8 us
    pallas_call x1, Pallas kernels, shards(): call(functools.partial(segment_kernel, patches), [f32(rows, cells, width)...  1.43 us
    pallas_call x1, Pallas kernels, shards(): call(final_kernel, [f32(rows, cells, width)], [VMEM] * 6)  1.14 us
    pallas_call x1, Pallas kernels, shards(): call(ahead_kernel, [f32(rows, cells, high, LANES)], [VMEM] * 2, flops=120...  0.73 us
  transfers between devices with their start and end apart: 8, of which 4 were waited for; matrix products, arithmetic and copies ran while one was open for 3% of the time, Pallas kernels for 25%

profile of v7, /device:TPU:0, one launch (start us, length us, event | category | flops | bytes accessed | tf_op | source)
XLA Modules:
  0.0 26.3 jit_solution(930620915074653374)
XLA Ops:
  0.0 0.0 copy-start
  0.0 0.0 copy-start.1
  0.0 3.0 %collective-permute-start = (f32[2,8,135]{2,1,0:T(8,128)}, f32[2,8,135]{2,1,0:T(8,128)S(1)}, u32[]{:S(2)}, u32[]{:S(2)}) collective-permute-start(f32[2,8,135]{2,1,0:T(8,128)} %own.3), channel_id=1, source_target_pairs={{0,1},{1,0},{2,3},{3,2},{4,5},{5,4},{6,7},{7,6},{8,9},{9,8},{10,11... | collective-permute-start | bytes 25928 | tf_op jit(solution)/shard_map/ppermute | solution.py:450
  3.0 0.0 copy-done
  3.1 0.0 copy-done.1
  3.1 0.2 copy.8.lower
  3.3 0.2 copy.9.upper
  3.5 0.0 copy-start.2
  3.6 0.0 copy-start.3
  3.6 0.0 copy-start.4
  3.6 0.0 copy-start.5
  3.6 0.7 %shard_map.75.ahead = f32[2,8,136,256]{3,2,1,0:T(8,128)S(1)} custom-call(bf16[136,135]{1,0:T(8,128)(2,1)S(1)} %shard_map.74.unit, bf16[2,8,135,135]{3,2,1,0:T(8,128)(2,1)S(1)} %copy.8.lower), custom_call_target="tpu_custom_call" | custom-call | flops 12000000000 | tf_op jit(solution)/shard_map/pallas_call | solution.py:460
  4.3 0.1 copy-done.2
  4.4 0.0 copy-done.3
  4.4 0.0 copy-done.4
  4.4 0.0 copy-done.5
  4.4 0.0 copy-start.6
  4.4 1.8 %shard_map.76 = (f32[2,8,272,256]{3,2,1,0:T(8,128)S(1)}, f32[2,3,136,256]{3,2,1,0:T(8,128)S(1)}, f32[3,136,256]{2,1,0:T(8,128)S(1)}, f32[3,136,256]{2,1,0:T(8,128)S(1)}) custom-call(bf16[136,135]{1,0:T(8,128)(2,1)S(1)} %shard_map.74.unit, f32[2,8,136,256]{3,2,1,0:T(8,128)S(1)} %shard_map.75.ahead, bf16[2,8,135,135]{3,2,1,0:T(8,128)(2,1)S(1)} %copy.9.upper, ...), custom_call_target="tpu_custom_call" | custom-call | flops 12000000000 | tf_op jit(solution)/shard_map/pallas_call | solution.py:463
  6.2 0.0 collective-permute-done.first
  6.2 0.1 collective-permute-start.1
  6.3 3.6 %collective-permute-start.3 = (f32[2,8,135]{2,1,0:T(8,128)S(1)}, f32[2,8,135]{2,1,0:T(8,128)S(1)}, u32[]{:S(2)}, u32[]{:S(2)}) collective-permute-start(f32[2,8,135]{2,1,0:T(8,128)S(1)} %copy-done.4), channel_id=1, source_target_pairs={{0,3},{1,2},{2,1},{3,0},{4,7},{5,6},{6,5},{7,4},{8,11},{9,10},{10,... | collective-permute-start | bytes 25928 | tf_op jit(solution)/shard_map/ppermute | solution.py:449
  9.9 0.0 collective-permute-done.1.theirs.others.refs_1_
  9.9 0.6 %shard_map.77 = (f32[136,256]{1,0:T(8,128)S(1)}, f32[3,136,256]{2,1,0:T(8,128)S(1)}, f32[440,128]{1,0:T(8,128)S(1)}) custom-call(f32[3,136,256]{2,1,0:T(8,128)S(1)} %get-tuple-element.38.mine.maps.refs_0_, f32[3,136,256]{2,1,0:T(8,128)S(1)} %collective-permute-done.1.theirs.others.refs_1_), custom_call_target="tpu_custom_call" | custom-call | tf_op jit(solution)/shard_map/pallas_call | solution.py:472
  10.5 1.5 %collective-permute-start.2 = (f32[440,128]{1,0:T(8,128)S(1)}, f32[440,128]{1,0:T(8,128)S(1)}, u32[]{:S(2)}, u32[]{:S(2)}) collective-permute-start(f32[440,128]{1,0:T(8,128)S(1)} %get-tuple-element.49.after), channel_id=1, source_target_pairs={{0,8},{4,12},{8,0},{12,4},{16,24},{20,28},{24,16},{28,20},{1,9},{5... | collective-permute-start | bytes 675848 | tf_op jit(solution)/shard_map/ppermute | solution.py:448
  12.1 0.0 copy-done.6
  12.1 0.2 copy.10.pivots
  12.3 0.0 collective-permute-done.3.second
  12.3 1.4 %shard_map.79 = (f32[2,8,135]{2,1,0:T(8,128)S(1)}, f32[2,2,8,256]{3,2,1,0:T(8,128)S(1)}, f32[8,256]{1,0:T(8,128)S(1)}, f32[8,256]{1,0:T(8,128)S(1)}) custom-call(s32[2,4]{1,0:T(2,128)S(1)} %copy-done.5, f32[2,8,135]{2,1,0:T(8,128)S(1)} %copy-done.3, f32[2,8,135]{2,1,0:T(8,128)S(1)} %copy-done.4, f32[2,8,135]{2,1,0:T(8,128)S(1)} %collective-permute-done.first, ...), custom_call_target="tpu_custom_call" | custom-call | flops 49999998976 | tf_op jit(solution)/shard_map/pallas_call | solution.py:479
  13.7 0.0 collective-permute-start.4
  13.8 1.2 %collective-permute-done.4.theirs = f32[8,256]{1,0:T(8,128)S(1)} collective-permute-done((f32[8,256]{1,0:T(8,128)S(1)}, f32[8,256]{1,0:T(8,128)S(1)}, u32[]{:S(2)}, u32[]{:S(2)}) %collective-permute-start.4) | collective-permute-done | bytes 8224 | tf_op jit(solution)/shard_map/ppermute | solution.py:448
  14.9 0.3 %shard_map.80 = (f32[8,256]{1,0:T(8,128)S(1)}, f32[2,8,256]{2,1,0:T(8,128)S(1)}) custom-call(f32[3,136,256]{2,1,0:T(8,128)S(1)} %get-tuple-element.38.mine.maps.refs_0_, f32[3,136,256]{2,1,0:T(8,128)S(1)} %collective-permute-done.1.theirs.others.refs_1_, f32[8,256]{1,0:T(8,128)S(1)} %get-tuple-element.50.mine, f32[8,256]{1,0:T(8,128)S(1)} %collective-permute-done.4.theirs), custom_call_target="tpu_custom_call" | custom-call | tf_op jit(solution)/shard_map/pallas_call | solution.py:490
  15.2 1.1 %collective-permute-start.5 = (f32[8,256]{1,0:T(8,128)S(1)}, f32[8,256]{1,0:T(8,128)S(1)}, u32[]{:S(2)}, u32[]{:S(2)}) collective-permute-start(f32[8,256]{1,0:T(8,128)S(1)} %get-tuple-element.52.vectors), channel_id=1, source_target_pairs={{0,8},{4,12},{8,0},{12,4},{16,24},{20,28},{24,16},{28,20},{1,9},{5... | collective-permute-start | bytes 24584 | tf_op jit(solution)/shard_map/ppermute | solution.py:448
  16.3 2.0 %collective-permute-done.2.theirs = f32[440,128]{1,0:T(8,128)S(1)} collective-permute-done((f32[440,128]{1,0:T(8,128)S(1)}, f32[440,128]{1,0:T(8,128)S(1)}, u32[]{:S(2)}, u32[]{:S(2)}) %collective-permute-start.2) | collective-permute-done | bytes 225312 | tf_op jit(solution)/shard_map/ppermute | solution.py:448
  18.3 0.6 %shard_map.78 = (f32[6,136,256]{2,1,0:T(8,128)S(1)}, f32[152,128]{1,0:T(8,128)S(1)}) custom-call(f32[3,136,256]{2,1,0:T(8,128)S(1)} %get-tuple-element.41.mine, f32[440,128]{1,0:T(8,128)S(1)} %collective-permute-done.2.theirs), custom_call_target="tpu_custom_call" | custom-call | flops 20000000000 | tf_op jit(solution)/shard_map/pallas_call | solution.py:499
  18.8 0.0 collective-permute-done.5.theirs
  18.9 0.2 shard_map.81
  19.1 1.6 %collective-permute-start.6 = (f32[160,128]{1,0:T(8,128)S(1)}, f32[160,128]{1,0:T(8,128)S(1)}, u32[]{:S(2)}, u32[]{:S(2)}) collective-permute-start(f32[160,128]{1,0:T(8,128)S(1)} %get-tuple-element.54), channel_id=1, source_target_pairs={{0,16},{4,20},{8,24},{12,28},{16,0},{20,4},{24,8},{28,12},{1,17},{... | collective-permute-start | bytes 245768 | tf_op jit(solution)/shard_map/ppermute | solution.py:448
  20.6 0.5 %shard_map.82 = (bf16[4,136,256]{2,1,0:T(8,128)(2,1)S(1)}, bf16[4,136,256]{2,1,0:T(8,128)(2,1)S(1)}, f32[4,8,256]{2,1,0:T(8,128)S(1)}) custom-call(f32[3,136,256]{2,1,0:T(8,128)S(1)} %get-tuple-element.38.mine.maps.refs_0_, f32[3,136,256]{2,1,0:T(8,128)S(1)} %collective-permute-done.1.theirs.others.refs_1_, f32[136,256]{1,0:T(8,128)S(1)} %get-tuple-element.55.refs_2_, ...), custom_call_target="tpu_custom_call" | custom-call | flops 3000000000 | tf_op jit(solution)/shard_map/pallas_call | solution.py:516
  21.1 2.4 %collective-permute-done.6.theirs = f32[160,128]{1,0:T(8,128)S(1)} collective-permute-done((f32[160,128]{1,0:T(8,128)S(1)}, f32[160,128]{1,0:T(8,128)S(1)}, u32[]{:S(2)}, u32[]{:S(2)}) %collective-permute-start.6) | collective-permute-done | bytes 81952 | tf_op jit(solution)/shard_map/ppermute | solution.py:448
  23.6 0.4 %shard_map.83 = (f32[2,8,256]{2,1,0:T(8,128)S(1)}, f32[2,8,256]{2,1,0:T(8,128)S(1)}) custom-call(f32[8,256]{1,0:T(8,128)S(1)} %get-tuple-element.53.vectors, f32[160,128]{1,0:T(8,128)S(1)} %collective-permute-done.6.theirs, bf16[4,136,256]{2,1,0:T(8,128)(2,1)S(1)} %get-tuple-element.58.hi, bf16[4,136,256]{2,1,0:T(8,128)(2,1)S(1)} %get-tuple-element.59.lo, ...), custom_call_target="tpu_custom_call" | custom-call | tf_op jit(solution)/shard_map/pallas_call | solution.py:522
  24.0 0.1 collective-permute-start.7
  24.0 0.5 %shard_map.84.own = f32[8,135]{1,0:T(8,128)S(1)} custom-call(f32[2,8,256]{2,1,0:T(8,128)S(1)} %get-tuple-element.62.ends, f32[2,8,135]{2,1,0:T(8,128)S(1)} %get-tuple-element.63.inner, f32[2,8,272,256]{3,2,1,0:T(8,128)S(1)} %get-tuple-element.47.tail, f32[2,3,136,256]{3,2,1,0:T(8,128)S(1)} %get-tuple-element.48.half, f32[2,2,8,256]{3,2,1,0:T(8,128)S(1)} %get-tuple-element.64.bias), custom_call_target="tpu_custom_call" | custom-call | flops 2000000000 | tf_op jit(solution)/shard_map/pallas_call | solution.py:526
  24.6 0.6 %collective-permute-done.7.ends = f32[2,8,256]{2,1,0:T(8,128)S(1)} collective-permute-done((f32[2,8,256]{2,1,0:T(8,128)S(1)}, f32[2,8,256]{2,1,0:T(8,128)S(1)}, u32[]{:S(2)}, u32[]{:S(2)}) %collective-permute-start.7) | collective-permute-done | bytes 16416 | tf_op jit(solution)/shard_map/ppermute | solution.py:448
  25.2 1.1 %shard_map.85 = f32[2,8,135]{2,1,0:T(8,128)} custom-call(f32[2,8,256]{2,1,0:T(8,128)S(1)} %collective-permute-done.7.ends, f32[8,135]{1,0:T(8,128)S(1)} %shard_map.84.own, f32[2,8,135]{2,1,0:T(8,128)S(1)} %get-tuple-element.63.inner, f32[2,8,272,256]{3,2,1,0:T(8,128)S(1)} %get-tuple-element.47.tail, f32[2,3,136,256]{3,2,1,0:T(8,128)S(1)} %get-tuple-element.48.half, ...), custom_call_target="tpu_custom_call" | custom-call | tf_op jit(solution)/shard_map/pallas_call | solution.py:529
  (2 shorter events, 0.0 us)
Async XLA Ops:
  0.0 3.0 %copy-start = (bf16[2,8,135,135]{3,1,2,0:T(8,128)(2,1)S(1)}, bf16[2,8,135,135]{3,1,2,0:T(8,128)(2,1)}, u32[]{:S(2)}) copy-start(bf16[2,8,135,135]{3,1,2,0:T(8,128)(2,1)} %param.12) | copy-start | bytes 1749604
  0.0 3.1 %copy-start.1 = (bf16[2,8,135,135]{3,1,2,0:T(8,128)(2,1)S(1)}, bf16[2,8,135,135]{3,1,2,0:T(8,128)(2,1)}, u32[]{:S(2)}) copy-start(bf16[2,8,135,135]{3,1,2,0:T(8,128)(2,1)} %param.13) | copy-start | bytes 1749604
  0.0 6.2 %collective-permute-start = (f32[2,8,135]{2,1,0:T(8,128)}, f32[2,8,135]{2,1,0:T(8,128)S(1)}, u32[]{:S(2)}, u32[]{:S(2)}) collective-permute-start(f32[2,8,135]{2,1,0:T(8,128)} %own.3), channel_id=1, source_target_pairs={{0,1},{1,0},{2,3},{3,2},{4,5},{5,4},{6,7},{7,6},{8,9},{9,8},{10,11... | collective-permute-start | bytes 25928 | tf_op jit(solution)/shard_map/ppermute | solution.py:450
  3.5 0.8 %copy-start.2 = (f32[2,8,4,135]{3,2,1,0:T(4,128)S(1)}, f32[2,8,4,135]{3,2,1,0:T(4,128)}, u32[]{:S(2)}) copy-start(f32[2,8,4,135]{3,2,1,0:T(4,128)} %coupling.3) | copy-start | bytes 103684
  3.6 0.8 %copy-start.3 = (f32[2,8,135]{2,1,0:T(8,128)S(1)}, f32[2,8,135]{2,1,0:T(8,128)}, u32[]{:S(2)}) copy-start(f32[2,8,135]{2,1,0:T(8,128)} %right.3) | copy-start | bytes 25924
  3.6 0.8 %copy-start.4 = (f32[2,8,135]{2,1,0:T(8,128)S(1)}, f32[2,8,135]{2,1,0:T(8,128)}, u32[]{:S(2)}) copy-start(f32[2,8,135]{2,1,0:T(8,128)} %own.3) | copy-start | bytes 25924
  3.6 0.8 %copy-start.5 = (s32[2,4]{1,0:T(2,128)S(1)}, s32[2,4]{1,0:T(2,128)}, u32[]{:S(2)}) copy-start(s32[2,4]{1,0:T(2,128)} %neighbours.3) | copy-start | bytes 100
  4.4 7.7 %copy-start.6 = (bf16[2,8,135,135]{3,1,2,0:T(8,128)(2,1)S(1)}, bf16[2,8,135,135]{3,1,2,0:T(8,128)(2,1)}, u32[]{:S(2)}) copy-start(bf16[2,8,135,135]{3,1,2,0:T(8,128)(2,1)} %param.11) | copy-start | bytes 1749604
  6.2 3.7 %collective-permute-start.1 = (f32[3,136,256]{2,1,0:T(8,128)S(1)}, f32[3,136,256]{2,1,0:T(8,128)S(1)}, u32[]{:S(2)}, u32[]{:S(2)}) collective-permute-start(f32[3,136,256]{2,1,0:T(8,128)S(1)} %get-tuple-element.40), channel_id=1, source_target_pairs={{0,4},{4,0},{8,12},{12,8},{16,20},{20,16},{24,28},{28,24},{1,5},{5... | collective-permute-start | bytes 1253384 | tf_op jit(solution)/shard_map/ppermute | solution.py:448
  6.3 6.0 %collective-permute-start.3 = (f32[2,8,135]{2,1,0:T(8,128)S(1)}, f32[2,8,135]{2,1,0:T(8,128)S(1)}, u32[]{:S(2)}, u32[]{:S(2)}) collective-permute-start(f32[2,8,135]{2,1,0:T(8,128)S(1)} %copy-done.4), channel_id=1, source_target_pairs={{0,3},{1,2},{2,1},{3,0},{4,7},{5,6},{6,5},{7,4},{8,11},{9,10},{10,... | collective-permute-start | bytes 25928 | tf_op jit(solution)/shard_map/ppermute | solution.py:449
  10.5 7.7 %collective-permute-start.2 = (f32[440,128]{1,0:T(8,128)S(1)}, f32[440,128]{1,0:T(8,128)S(1)}, u32[]{:S(2)}, u32[]{:S(2)}) collective-permute-start(f32[440,128]{1,0:T(8,128)S(1)} %get-tuple-element.49.after), channel_id=1, source_target_pairs={{0,8},{4,12},{8,0},{12,4},{16,24},{20,28},{24,16},{28,20},{1,9},{5... | collective-permute-start | bytes 675848 | tf_op jit(solution)/shard_map/ppermute | solution.py:448
  13.7 1.2 %collective-permute-start.4 = (f32[8,256]{1,0:T(8,128)S(1)}, f32[8,256]{1,0:T(8,128)S(1)}, u32[]{:S(2)}, u32[]{:S(2)}) collective-permute-start(f32[8,256]{1,0:T(8,128)S(1)} %get-tuple-element.51), channel_id=1, source_target_pairs={{0,4},{4,0},{8,12},{12,8},{16,20},{20,16},{24,28},{28,24},{1,5},{5... | collective-permute-start | bytes 24584 | tf_op jit(solution)/shard_map/ppermute | solution.py:448
  15.2 3.7 %collective-permute-start.5 = (f32[8,256]{1,0:T(8,128)S(1)}, f32[8,256]{1,0:T(8,128)S(1)}, u32[]{:S(2)}, u32[]{:S(2)}) collective-permute-start(f32[8,256]{1,0:T(8,128)S(1)} %get-tuple-element.52.vectors), channel_id=1, source_target_pairs={{0,8},{4,12},{8,0},{12,4},{16,24},{20,28},{24,16},{28,20},{1,9},{5... | collective-permute-start | bytes 24584 | tf_op jit(solution)/shard_map/ppermute | solution.py:448
  19.1 4.5 %collective-permute-start.6 = (f32[160,128]{1,0:T(8,128)S(1)}, f32[160,128]{1,0:T(8,128)S(1)}, u32[]{:S(2)}, u32[]{:S(2)}) collective-permute-start(f32[160,128]{1,0:T(8,128)S(1)} %get-tuple-element.54), channel_id=1, source_target_pairs={{0,16},{4,20},{8,24},{12,28},{16,0},{20,4},{24,8},{28,12},{1,17},{... | collective-permute-start | bytes 245768 | tf_op jit(solution)/shard_map/ppermute | solution.py:448
  24.0 1.2 %collective-permute-start.7 = (f32[2,8,256]{2,1,0:T(8,128)S(1)}, f32[2,8,256]{2,1,0:T(8,128)S(1)}, u32[]{:S(2)}, u32[]{:S(2)}) collective-permute-start(f32[2,8,256]{2,1,0:T(8,128)S(1)} %get-tuple-element.61), channel_id=1, source_target_pairs={{0,4},{4,0},{8,12},{12,8},{16,20},{20,16},{24,28},{28,24},{1,5},{5... | collective-permute-start | bytes 49160 | tf_op jit(solution)/shard_map/ppermute | solution.py:448

commit v8 on v6

--- a/solution.py
+++ b/solution.py
@@ -99,7 +99,7 @@
                 ahead[l, p * per + j, :, :width] = now[l, p]
 
 
-def maps_kernel(unit, ahead, upper, tail, half, keep, send):
+def maps_kernel(unit, ahead, upper, tail, half, keep, send, spare):
     rows, cells, width, _ = upper.shape
     high = keep.shape[1]
     per = cells // 2
@@ -108,7 +108,7 @@
     blank = jnp.zeros((high, LANES - 128), F32)
     for k in range(3):
         keep[k, :, 128:] = blank
-        send[k, :, 128:] = blank
+        spare[k, :, 128:] = blank
         for l in range(rows):
             half[l, k, :, 128:] = blank
     ends = [[ahead[l, p * per + per - 1, :, :width] for p in range(2)] for l in range(rows)]
@@ -149,7 +149,8 @@
         joint.append([front[l], g[0] + both[:high], both[high:]])
     for k in range(3):
         keep[k, :, :width] = jnp.where(core == 0, joint[0][k], joint[1][k])
-        send[k, :, :width] = jnp.where(core == 0, joint[1][k], joint[0][k])
+        spare[k, :, :width] = jnp.where(core == 0, joint[1][k], joint[0][k])
+    send[...] = packed([spare[k] for k in range(3)])
 
 
 def segment_kernel(
@@ -237,9 +238,12 @@
     return times_map(f[0][:, :high], f_right) + f[1], g[0] + times_map(between[:, :high], b_left), between
 
 
-def first_maps_kernel(mine, theirs, down, full, pack):
+def first_maps_kernel(mine, theirs, down, other, full, pack):
     s = side(0)
-    f, g, b = (ordered(s, mine[k], theirs[k]) for k in range(3))
+    maps = unpacked(theirs, 3, mine.shape[1])
+    for k in range(3):
+        other[k] = maps[k]
+    f, g, b = (ordered(s, mine[k], maps[k]) for k in range(3))
     joint, inward = merged_maps(f, g, b)
     down[...] = inward
     for k, m in enumerate(joint):
@@ -462,20 +466,23 @@
     )[0]
     tail, half, keep, send = call(
         maps_kernel,
-        [f32(rows, cells, 2 * high, LANES), f32(rows, 3, high, LANES), full, full],
+        [
+            f32(rows, cells, 2 * high, LANES), f32(rows, 3, high, LANES), full,
+            f32(length(3, high), 128),
+        ],
         [VMEM] * 3,
+        [pltpu.VMEM((3, high, LANES), F32)],
         flops=12000000000,
     )(unit, ahead, upper_factor)
-    send, first = lax.optimization_barrier((send, first))
+    send, second, pivots = lax.optimization_barrier((send, second, pivots))
     theirs = swap(send, 0)
-    first_maps = keep, theirs
-    down, mine, pack = call(
+    down, theirs, mine, pack = call(
         first_maps_kernel,
-        [f32(high, LANES), full, f32(length(3, high), 128)],
+        [f32(high, LANES), full, full, f32(length(3, high), 128)],
         [VMEM] * 2,
     )(keep, theirs)
+    first_maps = keep, theirs
     theirs = swap(pack, 1)
-    pack, pivots = lax.optimization_barrier((pack, pivots))
     inner, ends, vkeep, vsend = call(
         functools.partial(segment_kernel, patches),
         [f32(rows, cells, width), f32(rows, 2, 8, LANES), row, row],

time: 26.4 us -> 26.4 us (level)
  starting transfers between devices: 10.9 us -> 9.9 us
  waiting for transfers between devices: 6.33 us -> 7.14 us
    ppermute x1, starting transfers between devices: 3.02 us -> 0.07 us  [shards(): first = lax.ppermute(previous, 'surf', pairs)]
    ppermute x1, starting transfers between devices: 3.62 us -> 5.05 us  [shards(): second = lax.ppermute(previous, 'surf', odd)]
    ppermute x6, waiting for transfers between devices: 6.32 us -> 7.04 us  [shards(): lax.ppermute(a, 'line', [(i, i ^ 1 << k) for i in range(count)])]
    ppermute x6, starting transfers between devices: 4.3 us -> 4.78 us  [shards(): lax.ppermute(a, 'line', [(i, i ^ 1 << k) for i in range(count)])]
  transfers between devices with their start and end apart: 8 -> 8, of which waited for: 5 -> 6; matrix products, arithmetic and copies ran while one was open for 3% -> 3% of each run, Pallas kernels for 24% -> 25%
where the time goes in v8:
time: 26.4 us; the launch traced here: 26.3 us
  starting transfers between devices  9.9 us (38%)
  Pallas kernels  8.32 us (32%)
  waiting for transfers between devices  7.14 us (27%)
  local copies, waits for them, and re-layouts  0.72 us (3%)
    ppermute x6, waiting for transfers between devices, shards(): lax.ppermute(a, 'line', [(i, i ^ 1 << k) for i in range(count)])  7.04 us
    ppermute x1, starting transfers between devices, shards(): second = lax.ppermute(previous, 'surf', odd)  5.05 us
    ppermute x6, starting transfers between devices, shards(): lax.ppermute(a, 'line', [(i, i ^ 1 << k) for i in range(count)])  4.78 us
    pallas_call x1, Pallas kernels, shards(): call(maps_kernel, [f32(rows, cells, 2 * high, LANES), f32(rows, 3, high,...  1.88 us
    pallas_call x1, Pallas kernels, shards(): call(functools.partial(segment_kernel, patches), [f32(rows, cells, width)...  1.43 us
    pallas_call x1, Pallas kernels, shards(): call(final_kernel, [f32(rows, cells, width)], [VMEM] * 6)  1.14 us
    pallas_call x1, Pallas kernels, shards(): call(ahead_kernel, [f32(rows, cells, high, LANES)], [VMEM] * 2, flops=120...  0.73 us
    pallas_call x1, Pallas kernels, shards(): call(first_maps_kernel, [f32(high, LANES), full, full, f32(length(3, high...  0.69 us
  transfers between devices with their start and end apart: 8, of which 6 were waited for; matrix products, arithmetic and copies ran while one was open for 3% of the time, Pallas kernels for 25%

profile of v8, /device:TPU:0, one launch (start us, length us, event | category | flops | bytes accessed | tf_op | source)
XLA Modules:
  0.0 26.3 jit_solution(9294373707781258360)
XLA Ops:
  0.0 0.0 copy-start
  0.0 0.0 copy-start.1
  0.0 5.0 %collective-permute-start = (f32[2,8,135]{2,1,0:T(8,128)}, f32[2,8,135]{2,1,0:T(8,128)S(1)}, u32[]{:S(2)}, u32[]{:S(2)}) collective-permute-start(f32[2,8,135]{2,1,0:T(8,128)} %own.1), channel_id=1, source_target_pairs={{0,3},{1,2},{2,1},{3,0},{4,7},{5,6},{6,5},{7,4},{8,11},{9,10},{10,... | collective-permute-start | bytes 25928 | tf_op jit(solution)/shard_map/ppermute | solution.py:453
  5.1 0.0 copy-done
  5.1 0.0 copy-done.1
  5.1 0.2 copy.8.lower
  5.3 0.2 copy.9.upper
  5.6 0.7 %shard_map.75.ahead = f32[2,8,136,256]{3,2,1,0:T(8,128)S(1)} custom-call(bf16[136,135]{1,0:T(8,128)(2,1)S(1)} %shard_map.74.unit, bf16[2,8,135,135]{3,2,1,0:T(8,128)(2,1)S(1)} %copy.8.lower), custom_call_target="tpu_custom_call" | custom-call | flops 12000000000 | tf_op jit(solution)/shard_map/pallas_call | solution.py:464
  6.3 0.0 copy-start.4
  6.3 0.0 copy-start.6
  6.3 1.9 %shard_map.76 = (f32[2,8,272,256]{3,2,1,0:T(8,128)S(1)}, f32[2,3,136,256]{3,2,1,0:T(8,128)S(1)}, f32[3,136,256]{2,1,0:T(8,128)S(1)}, f32[440,128]{1,0:T(8,128)S(1)}) custom-call(bf16[136,135]{1,0:T(8,128)(2,1)S(1)} %shard_map.74.unit, f32[2,8,136,256]{3,2,1,0:T(8,128)S(1)} %shard_map.75.ahead, bf16[2,8,135,135]{3,2,1,0:T(8,128)(2,1)S(1)} %copy.9.upper), custom_call_target="tpu_custom_call" | custom-call | flops 12000000000 | tf_op jit(solution)/shard_map/pallas_call | solution.py:467
  8.2 0.0 collective-permute-done.second
  8.2 0.0 copy-start.2
  8.2 0.0 copy-start.3
  8.2 0.0 copy-start.5
  8.3 0.1 collective-permute-start.1
  8.3 0.0 copy-done.4
  8.3 0.1 collective-permute-start.3
  8.4 0.0 copy-done.6
  8.4 0.2 copy.10.pivots
  8.7 1.1 %collective-permute-done.1.theirs = f32[440,128]{1,0:T(8,128)S(1)} collective-permute-done((f32[440,128]{1,0:T(8,128)S(1)}, f32[440,128]{1,0:T(8,128)S(1)}, u32[]{:S(2)}, u32[]{:S(2)}) %collective-permute-start.1) | collective-permute-done | bytes 225312 | tf_op jit(solution)/shard_map/ppermute | solution.py:452
  9.8 0.7 %shard_map.77 = (f32[136,256]{1,0:T(8,128)S(1)}, f32[3,136,256]{2,1,0:T(8,128)S(1)}, f32[3,136,256]{2,1,0:T(8,128)S(1)}, f32[440,128]{1,0:T(8,128)S(1)}) custom-call(f32[3,136,256]{2,1,0:T(8,128)S(1)} %get-tuple-element.38.mine.maps.refs_0_, f32[440,128]{1,0:T(8,128)S(1)} %collective-permute-done.1.theirs), custom_call_target="tpu_custom_call" | custom-call | tf_op jit(solution)/shard_map/pallas_call | solution.py:479
  10.5 1.5 %collective-permute-start.2 = (f32[440,128]{1,0:T(8,128)S(1)}, f32[440,128]{1,0:T(8,128)S(1)}, u32[]{:S(2)}, u32[]{:S(2)}) collective-permute-start(f32[440,128]{1,0:T(8,128)S(1)} %get-tuple-element.42.after), channel_id=1, source_target_pairs={{0,8},{4,12},{8,0},{12,4},{16,24},{20,28},{24,16},{28,20},{1,9},{5... | collective-permute-start | bytes 675848 | tf_op jit(solution)/shard_map/ppermute | solution.py:452
  12.0 0.1 collective-permute-done.3.first
  12.2 0.0 copy-done.2
  12.2 0.0 copy-done.3
  12.2 0.0 copy-done.5
  12.2 1.4 %shard_map.79 = (f32[2,8,135]{2,1,0:T(8,128)S(1)}, f32[2,2,8,256]{3,2,1,0:T(8,128)S(1)}, f32[8,256]{1,0:T(8,128)S(1)}, f32[8,256]{1,0:T(8,128)S(1)}) custom-call(s32[2,4]{1,0:T(2,128)S(1)} %copy-done.5, f32[2,8,135]{2,1,0:T(8,128)S(1)} %copy-done.3, f32[2,8,135]{2,1,0:T(8,128)S(1)} %copy-done.4, f32[2,8,135]{2,1,0:T(8,128)S(1)} %collective-permute-done.3.first, ...), custom_call_target="tpu_custom_call" | custom-call | flops 49999998976 | tf_op jit(solution)/shard_map/pallas_call | solution.py:486
  13.6 0.0 collective-permute-start.4
  13.6 1.2 %collective-permute-done.4.theirs = f32[8,256]{1,0:T(8,128)S(1)} collective-permute-done((f32[8,256]{1,0:T(8,128)S(1)}, f32[8,256]{1,0:T(8,128)S(1)}, u32[]{:S(2)}, u32[]{:S(2)}) %collective-permute-start.4) | collective-permute-done | bytes 8224 | tf_op jit(solution)/shard_map/ppermute | solution.py:452
  14.8 0.3 %shard_map.80 = (f32[8,256]{1,0:T(8,128)S(1)}, f32[2,8,256]{2,1,0:T(8,128)S(1)}) custom-call(f32[3,136,256]{2,1,0:T(8,128)S(1)} %get-tuple-element.38.mine.maps.refs_0_, f32[3,136,256]{2,1,0:T(8,128)S(1)} %get-tuple-element.45.others.refs_1_, f32[8,256]{1,0:T(8,128)S(1)} %get-tuple-element.50.mine, f32[8,256]{1,0:T(8,128)S(1)} %collective-permute-done.4.theirs), custom_call_target="tpu_custom_call" | custom-call | tf_op jit(solution)/shard_map/pallas_call | solution.py:497
  15.1 1.5 %collective-permute-start.5 = (f32[8,256]{1,0:T(8,128)S(1)}, f32[8,256]{1,0:T(8,128)S(1)}, u32[]{:S(2)}, u32[]{:S(2)}) collective-permute-start(f32[8,256]{1,0:T(8,128)S(1)} %get-tuple-element.52.vectors), channel_id=1, source_target_pairs={{0,8},{4,12},{8,0},{12,4},{16,24},{20,28},{24,16},{28,20},{1,9},{5... | collective-permute-start | bytes 24584 | tf_op jit(solution)/shard_map/ppermute | solution.py:452
  16.6 1.7 %collective-permute-done.2.theirs = f32[440,128]{1,0:T(8,128)S(1)} collective-permute-done((f32[440,128]{1,0:T(8,128)S(1)}, f32[440,128]{1,0:T(8,128)S(1)}, u32[]{:S(2)}, u32[]{:S(2)}) %collective-permute-start.2) | collective-permute-done | bytes 225312 | tf_op jit(solution)/shard_map/ppermute | solution.py:452
  18.2 0.6 %shard_map.78 = (f32[6,136,256]{2,1,0:T(8,128)S(1)}, f32[152,128]{1,0:T(8,128)S(1)}) custom-call(f32[3,136,256]{2,1,0:T(8,128)S(1)} %get-tuple-element.41.mine, f32[440,128]{1,0:T(8,128)S(1)} %collective-permute-done.2.theirs), custom_call_target="tpu_custom_call" | custom-call | flops 20000000000 | tf_op jit(solution)/shard_map/pallas_call | solution.py:506
  18.8 0.0 collective-permute-done.5.theirs
  18.8 0.2 shard_map.81
  19.0 1.6 %collective-permute-start.6 = (f32[160,128]{1,0:T(8,128)S(1)}, f32[160,128]{1,0:T(8,128)S(1)}, u32[]{:S(2)}, u32[]{:S(2)}) collective-permute-start(f32[160,128]{1,0:T(8,128)S(1)} %get-tuple-element.54), channel_id=1, source_target_pairs={{0,16},{4,20},{8,24},{12,28},{16,0},{20,4},{24,8},{28,12},{1,17},{... | collective-permute-start | bytes 245768 | tf_op jit(solution)/shard_map/ppermute | solution.py:452
  20.6 0.5 %shard_map.82 = (bf16[4,136,256]{2,1,0:T(8,128)(2,1)S(1)}, bf16[4,136,256]{2,1,0:T(8,128)(2,1)S(1)}, f32[4,8,256]{2,1,0:T(8,128)S(1)}) custom-call(f32[3,136,256]{2,1,0:T(8,128)S(1)} %get-tuple-element.38.mine.maps.refs_0_, f32[3,136,256]{2,1,0:T(8,128)S(1)} %get-tuple-element.45.others.refs_1_, f32[136,256]{1,0:T(8,128)S(1)} %get-tuple-element.55.refs_2_, ...), custom_call_target="tpu_custom_call" | custom-call | flops 3000000000 | tf_op jit(solution)/shard_map/pallas_call | solution.py:523
  21.0 2.5 %collective-permute-done.6.theirs = f32[160,128]{1,0:T(8,128)S(1)} collective-permute-done((f32[160,128]{1,0:T(8,128)S(1)}, f32[160,128]{1,0:T(8,128)S(1)}, u32[]{:S(2)}, u32[]{:S(2)}) %collective-permute-start.6) | collective-permute-done | bytes 81952 | tf_op jit(solution)/shard_map/ppermute | solution.py:452
  23.5 0.4 %shard_map.83 = (f32[2,8,256]{2,1,0:T(8,128)S(1)}, f32[2,8,256]{2,1,0:T(8,128)S(1)}) custom-call(f32[8,256]{1,0:T(8,128)S(1)} %get-tuple-element.53.vectors, f32[160,128]{1,0:T(8,128)S(1)} %collective-permute-done.6.theirs, bf16[4,136,256]{2,1,0:T(8,128)(2,1)S(1)} %get-tuple-element.58.hi, bf16[4,136,256]{2,1,0:T(8,128)(2,1)S(1)} %get-tuple-element.59.lo, ...), custom_call_target="tpu_custom_call" | custom-call | tf_op jit(solution)/shard_map/pallas_call | solution.py:529
  23.9 0.1 collective-permute-start.7
  24.0 0.5 %shard_map.84.own = f32[8,135]{1,0:T(8,128)S(1)} custom-call(f32[2,8,256]{2,1,0:T(8,128)S(1)} %get-tuple-element.62.ends, f32[2,8,135]{2,1,0:T(8,128)S(1)} %get-tuple-element.63.inner, f32[2,8,272,256]{3,2,1,0:T(8,128)S(1)} %get-tuple-element.48.tail, f32[2,3,136,256]{3,2,1,0:T(8,128)S(1)} %get-tuple-element.49.half, f32[2,2,8,256]{3,2,1,0:T(8,128)S(1)} %get-tuple-element.64.bias), custom_call_target="tpu_custom_call" | custom-call | flops 2000000000 | tf_op jit(solution)/shard_map/pallas_call | solution.py:533
  24.5 0.6 %collective-permute-done.7.ends = f32[2,8,256]{2,1,0:T(8,128)S(1)} collective-permute-done((f32[2,8,256]{2,1,0:T(8,128)S(1)}, f32[2,8,256]{2,1,0:T(8,128)S(1)}, u32[]{:S(2)}, u32[]{:S(2)}) %collective-permute-start.7) | collective-permute-done | bytes 16416 | tf_op jit(solution)/shard_map/ppermute | solution.py:452
  25.1 1.1 %shard_map.85 = f32[2,8,135]{2,1,0:T(8,128)} custom-call(f32[2,8,256]{2,1,0:T(8,128)S(1)} %collective-permute-done.7.ends, f32[8,135]{1,0:T(8,128)S(1)} %shard_map.84.own, f32[2,8,135]{2,1,0:T(8,128)S(1)} %get-tuple-element.63.inner, f32[2,8,272,256]{3,2,1,0:T(8,128)S(1)} %get-tuple-element.48.tail, f32[2,3,136,256]{3,2,1,0:T(8,128)S(1)} %get-tuple-element.49.half, ...), custom_call_target="tpu_custom_call" | custom-call | tf_op jit(solution)/shard_map/pallas_call | solution.py:536
  (2 shorter events, 0.0 us)
Async XLA Ops:
  0.0 5.1 %copy-start = (bf16[2,8,135,135]{3,1,2,0:T(8,128)(2,1)S(1)}, bf16[2,8,135,135]{3,1,2,0:T(8,128)(2,1)}, u32[]{:S(2)}) copy-start(bf16[2,8,135,135]{3,1,2,0:T(8,128)(2,1)} %param.12) | copy-start | bytes 1749604
  0.0 5.1 %copy-start.1 = (bf16[2,8,135,135]{3,1,2,0:T(8,128)(2,1)S(1)}, bf16[2,8,135,135]{3,1,2,0:T(8,128)(2,1)}, u32[]{:S(2)}) copy-start(bf16[2,8,135,135]{3,1,2,0:T(8,128)(2,1)} %param.13) | copy-start | bytes 1749604
  0.0 8.2 %collective-permute-start = (f32[2,8,135]{2,1,0:T(8,128)}, f32[2,8,135]{2,1,0:T(8,128)S(1)}, u32[]{:S(2)}, u32[]{:S(2)}) collective-permute-start(f32[2,8,135]{2,1,0:T(8,128)} %own.1), channel_id=1, source_target_pairs={{0,3},{1,2},{2,1},{3,0},{4,7},{5,6},{6,5},{7,4},{8,11},{9,10},{10,... | collective-permute-start | bytes 25928 | tf_op jit(solution)/shard_map/ppermute | solution.py:453
  6.3 2.0 %copy-start.4 = (f32[2,8,135]{2,1,0:T(8,128)S(1)}, f32[2,8,135]{2,1,0:T(8,128)}, u32[]{:S(2)}) copy-start(f32[2,8,135]{2,1,0:T(8,128)} %own.1) | copy-start | bytes 25924
  6.3 2.1 %copy-start.6 = (bf16[2,8,135,135]{3,1,2,0:T(8,128)(2,1)S(1)}, bf16[2,8,135,135]{3,1,2,0:T(8,128)(2,1)}, u32[]{:S(2)}) copy-start(bf16[2,8,135,135]{3,1,2,0:T(8,128)(2,1)} %param.11) | copy-start | bytes 1749604
  8.2 3.9 %copy-start.2 = (f32[2,8,4,135]{3,2,1,0:T(4,128)S(1)}, f32[2,8,4,135]{3,2,1,0:T(4,128)}, u32[]{:S(2)}) copy-start(f32[2,8,4,135]{3,2,1,0:T(4,128)} %coupling.1) | copy-start | bytes 103684
  8.2 3.9 %copy-start.3 = (f32[2,8,135]{2,1,0:T(8,128)S(1)}, f32[2,8,135]{2,1,0:T(8,128)}, u32[]{:S(2)}) copy-start(f32[2,8,135]{2,1,0:T(8,128)} %right.1) | copy-start | bytes 25924
  8.2 3.9 %copy-start.5 = (s32[2,4]{1,0:T(2,128)S(1)}, s32[2,4]{1,0:T(2,128)}, u32[]{:S(2)}) copy-start(s32[2,4]{1,0:T(2,128)} %neighbours.1) | copy-start | bytes 100
  8.3 1.5 %collective-permute-start.1 = (f32[440,128]{1,0:T(8,128)S(1)}, f32[440,128]{1,0:T(8,128)S(1)}, u32[]{:S(2)}, u32[]{:S(2)}) collective-permute-start(f32[440,128]{1,0:T(8,128)S(1)} %get-tuple-element.40), channel_id=1, source_target_pairs={{0,4},{4,0},{8,12},{12,8},{16,20},{20,16},{24,28},{28,24},{1,5},{5... | collective-permute-start | bytes 675848 | tf_op jit(solution)/shard_map/ppermute | solution.py:452
  8.3 3.8 %collective-permute-start.3 = (f32[2,8,135]{2,1,0:T(8,128)S(1)}, f32[2,8,135]{2,1,0:T(8,128)S(1)}, u32[]{:S(2)}, u32[]{:S(2)}) collective-permute-start(f32[2,8,135]{2,1,0:T(8,128)S(1)} %copy-done.4), channel_id=1, source_target_pairs={{0,1},{1,0},{2,3},{3,2},{4,5},{5,4},{6,7},{7,6},{8,9},{9,8},{10,11... | collective-permute-start | bytes 25928 | tf_op jit(solution)/shard_map/ppermute | solution.py:454
  10.5 7.7 %collective-permute-start.2 = (f32[440,128]{1,0:T(8,128)S(1)}, f32[440,128]{1,0:T(8,128)S(1)}, u32[]{:S(2)}, u32[]{:S(2)}) collective-permute-start(f32[440,128]{1,0:T(8,128)S(1)} %get-tuple-element.42.after), channel_id=1, source_target_pairs={{0,8},{4,12},{8,0},{12,4},{16,24},{20,28},{24,16},{28,20},{1,9},{5... | collective-permute-start | bytes 675848 | tf_op jit(solution)/shard_map/ppermute | solution.py:452
  13.6 1.2 %collective-permute-start.4 = (f32[8,256]{1,0:T(8,128)S(1)}, f32[8,256]{1,0:T(8,128)S(1)}, u32[]{:S(2)}, u32[]{:S(2)}) collective-permute-start(f32[8,256]{1,0:T(8,128)S(1)} %get-tuple-element.51), channel_id=1, source_target_pairs={{0,4},{4,0},{8,12},{12,8},{16,20},{20,16},{24,28},{28,24},{1,5},{5... | collective-permute-start | bytes 24584 | tf_op jit(solution)/shard_map/ppermute | solution.py:452
  15.1 3.7 %collective-permute-start.5 = (f32[8,256]{1,0:T(8,128)S(1)}, f32[8,256]{1,0:T(8,128)S(1)}, u32[]{:S(2)}, u32[]{:S(2)}) collective-permute-start(f32[8,256]{1,0:T(8,128)S(1)} %get-tuple-element.52.vectors), channel_id=1, source_target_pairs={{0,8},{4,12},{8,0},{12,4},{16,24},{20,28},{24,16},{28,20},{1,9},{5... | collective-permute-start | bytes 24584 | tf_op jit(solution)/shard_map/ppermute | solution.py:452
  19.0 4.5 %collective-permute-start.6 = (f32[160,128]{1,0:T(8,128)S(1)}, f32[160,128]{1,0:T(8,128)S(1)}, u32[]{:S(2)}, u32[]{:S(2)}) collective-permute-start(f32[160,128]{1,0:T(8,128)S(1)} %get-tuple-element.54), channel_id=1, source_target_pairs={{0,16},{4,20},{8,24},{12,28},{16,0},{20,4},{24,8},{28,12},{1,17},{... | collective-permute-start | bytes 245768 | tf_op jit(solution)/shard_map/ppermute | solution.py:452
  23.9 1.2 %collective-permute-start.7 = (f32[2,8,256]{2,1,0:T(8,128)S(1)}, f32[2,8,256]{2,1,0:T(8,128)S(1)}, u32[]{:S(2)}, u32[]{:S(2)}) collective-permute-start(f32[2,8,256]{2,1,0:T(8,128)S(1)} %get-tuple-element.61), channel_id=1, source_target_pairs={{0,4},{4,0},{8,12},{12,8},{16,20},{20,16},{24,28},{28,24},{1,5},{5... | collective-permute-start | bytes 49160 | tf_op jit(solution)/shard_map/ppermute | solution.py:452
